TPU v7x, 128 devices: a whole 4x4x4 slice. The times are simulated.
128 devices in a mesh: row: 8 (over x, core), col: 16 (over y, z).
Axes of the slice: x: 4, y: 4, z: 4, core: 2. Of those that a mesh axis runs over, the one named last changes fastest.
Arguments:
- series: bfloat16 [512, 32768], P(None, ('row', 'col')), may hold values from -6 to 6
- lag_weight: float32 [4], replicated, may hold values from 0.25 to 1
- start_basis: bfloat16 [64, 32768], P(None, ('row', 'col')), may hold values from -5.25 to 5.25
- block_pairs: int32 [8, 16, 32, 2], P('row', 'col'), may hold values from 0 to 127, as said below
- pair_count: int32 [8, 16], P('row', 'col'), may hold values from 1 to 32, as said below
Outputs:
- basis: float32 [64, 32768], P(None, ('row', 'col'))
- rayleigh: float32 [64, 64], replicated
Inputs may be any that keep to these rules, and one draw needn't show every extreme that they name: For every slot s of device (r, c), block_pairs[r, c, s, 0] is a block of row group r, from r * 16 to (r + 1) * 16 - 1, and block_pairs[r, c, s, 1] is a block held by a device of mesh column c: (block_pairs[r, c, s, 1]) mod (16) equals c. Slots that are not live hold blocks of the same ranges and are no part of the network. `pair_count`: the number of live slots of device (r, c); some device has exactly 32.
All inputs are finite; a program needn't handle non-finite values.
Results may differ from a plain program's by a relative error of at most 0.0045.
Values may be sent and summed in bfloat16 or wider, within the bound.
No kernel may reach another device: no remote copies, remote signals or barrier semaphores. Data moves between devices by JAX's collectives and lax.ppermute only.
A program may use at most 64 MiB of HBM per device.

v0:
```python
import jax
import jax.numpy as jnp
from jax import lax
from jax.experimental import pallas as pl
from jax.experimental.pallas import tpu as pltpu
from jax.sharding import PartitionSpec as P


BLOCK = 256
DAYS = 512
LAGS = 4
RANK = 64
SLOTS = 32
N_ROW = 8
N_COL = 16
CELLS = 32768
BETA_CORR = 8.0
GRAM_EPS = 1e-05
TILE_SCALE = 0.25 / 16.0
HIGHEST = lax.Precision.HIGHEST
F32 = jnp.float32
BF16 = jnp.bfloat16
VMEM = pl.BlockSpec(memory_space=pltpu.VMEM)
HBM = pl.BlockSpec(memory_space=pltpu.HBM)
ANY = pl.BlockSpec(memory_space=pl.ANY)
SMEM = pl.BlockSpec(memory_space=pltpu.SMEM)


def call(body, out_shape, in_specs, flops, nbytes, limit, scratch=(), out_specs=None):
    many = isinstance(out_shape, (list, tuple))
    return pl.pallas_call(
        body,
        out_shape=out_shape,
        in_specs=in_specs,
        out_specs=out_specs or ([VMEM] * len(out_shape) if many else VMEM),
        scratch_shapes=list(scratch),
        compiler_params=pltpu.CompilerParams(vmem_limit_bytes=limit << 20),
        cost_estimate=pl.CostEstimate(flops=flops, bytes_accessed=nbytes, transcendentals=0),
    )


def shape(*dims, dtype=F32):
    return jax.ShapeDtypeStruct(dims, dtype)


def shift_body(own_ref, other_ref, out_ref, xc_ref):
    day = lax.broadcasted_iota(jnp.int32, (DAYS, BLOCK), 0)
    for core, ref in enumerate((own_ref, other_ref)):

        def one(step, carry, core=core, ref=ref):
            block = 4 * core + step
            x = ref[step, :DAYS].astype(F32) * (BETA_CORR / DAYS)
            out_ref[block, 0] = (x + x).astype(BF16)
            for lag in range(1, LAGS):
                later = jnp.where(day < DAYS - lag, pltpu.roll(x, DAYS - lag, 0), 0.0)
                earlier = jnp.where(day >= lag, pltpu.roll(x, lag, 0), 0.0)
                out_ref[block, lag] = (later + earlier).astype(BF16)
            xc_ref[block] = ref[step, DAYS:]
            return carry

        lax.fori_loop(0, 4, one, 0)


def day_sums(own, other):
    return call(
        shift_body,
        [shape(N_ROW, LAGS, DAYS, BLOCK, dtype=BF16), shape(N_ROW, RANK, BLOCK, dtype=BF16)],
        [VMEM, VMEM],
        10_000_000,
        24 << 20,
        16,
    )(own, other)


HALF = BLOCK // 2
GROUP = 4
TILE_ROOM = 288


def row_offset(place, j):
    return ((j ^ place[1]) & 1) * 4 + ((place[0] - j // 2) & 3)


def groups_of(count):
    return (count[0] + GROUP - 1) // GROUP


def build_body(pairs, count, place, weight, sums_ref, xc_ref, *rest):
    first, second = rest[:8], rest[8:16]
    tiles_ref, rows_ref, cols_ref, at_ref, xr_ref, buffer, sems, out_sems = rest[16:]
    copies = []

    def fetch(src, dst):
        copies.append(pltpu.make_async_copy(src, dst, sems.at[len(copies)]))
        copies[-1].start()

    for k in range(4):
        for h in range(2):
            two = slice(2 * h, 2 * h + 2)
            a, b = first[2 * k + h], second[2 * k + h]
            fetch(a.at[:, :HALF], at_ref.at[k, two, :HALF])
            fetch(b.at[:, :HALF], at_ref.at[two, k, HALF:])
            for q in range(2):
                lanes = slice(BLOCK * q, BLOCK * q + BLOCK)
                fetch(a.at[:, HALF:, lanes], xr_ref.at[k, two, 32 * q : 32 * q + 16])
                fetch(b.at[:, HALF:, lanes], xr_ref.at[two, k, 32 * q + 16 : 32 * q + 32])
    rows_ref[...] = jnp.zeros_like(rows_ref)
    cols_ref[...] = jnp.zeros_like(cols_ref)
    buffer[1] = jnp.zeros((2, BLOCK, BLOCK), BF16)
    for copy in copies:
        copy.wait()
    twos = (count[0] + 1) // 2

    def indices(slot):
        i = pairs[2 * slot] % N_COL
        from_y = (place[2] - i // 4) & 3
        from_z = (place[3] - i) & 3
        return i, from_y, from_z, row_offset(place, pairs[2 * slot + 1] // N_COL)

    def products(two, side):
        done = []
        for k in range(2):
            i, from_y, from_z, from_row = indices(2 * two + k)
            tile = buffer[side, k]
            into_cols = jnp.dot(xr_ref[from_y, from_z], tile, preferred_element_type=F32)
            into_rows = lax.dot_general(
                xc_ref[from_row], tile, (((1,), (1,)), ((), ())), preferred_element_type=F32
            )
            done.append((i, from_row, into_rows, into_cols))
        for i, from_row, into_rows, into_cols in done:
            cols_ref[from_row] += into_cols
            rows_ref[i] += into_rows

    def tile_of(slot):
        _, from_y, from_z, from_row = indices(slot)
        live = jnp.where(slot < count[0], TILE_SCALE, 0.0)
        lead = at_ref[from_y, from_z]
        total = None
        for lag in range(LAGS):
            lagged = jnp.dot(lead, sums_ref[from_row, lag], preferred_element_type=F32)
            term = weight[lag] * jnp.tanh(lagged)
            total = term if total is None else total + term
        return (total * live).astype(BF16)

    def store(two, side):
        return pltpu.make_async_copy(
            buffer.at[side], tiles_ref.at[pl.ds(2 * two, 2)], out_sems.at[side]
        )

    def one(two, carry):
        side = two & 1
        products(jnp.maximum(two - 1, 0), 1 - side)
        here, there = tile_of(2 * two), tile_of(2 * two + 1)

        @pl.when(two >= 2)
        def _():
            store(two - 2, side).wait()

        buffer[side, 0] = here
        buffer[side, 1] = there
        store(two, side).start()
        return carry

    lax.fori_loop(0, twos, one, 0)
    products(twos - 1, (twos - 1) & 1)

    @pl.when(twos >= 2)
    def _():
        store(twos - 2, twos & 1).wait()

    store(twos - 1, (twos - 1) & 1).wait()


def build(pairs, count, place, weight, sums, xc, first, second):
    return call(
        build_body,
        [
            shape(TILE_ROOM, BLOCK, BLOCK, dtype=BF16),
            shape(N_COL, RANK, BLOCK),
            shape(N_ROW, RANK, BLOCK),
        ],
        [SMEM] * 4 + [VMEM] * 2 + [ANY] * 16,
        9_000_000_000,
        20 << 20,
        30,
        scratch=[
            pltpu.VMEM((4, 4, BLOCK, DAYS), BF16),
            pltpu.VMEM((4, 4, RANK, BLOCK), BF16),
            pltpu.VMEM((2, 2, BLOCK, BLOCK), BF16),
            pltpu.SemaphoreType.DMA((48,)),
            pltpu.SemaphoreType.DMA((2,)),
        ],
        out_specs=[HBM, VMEM, VMEM],
    )(pairs, count, place, weight, sums, xc, *first, *second)


def total_of(rr_ref, own_ref, parts):
    total = rr_ref[0] + own_ref[0, :RANK]
    for k in range(1, N_COL):
        total = total + rr_ref[k]
    for part in parts:
        total = total + part[0, :RANK]
    return total


def mid1_body(rr_ref, own_ref, a_ref, b_ref, c_ref, out_ref, wide_ref):
    total = total_of(rr_ref, own_ref, (a_ref, b_ref, c_ref))
    high = total.astype(BF16)
    both = jnp.concatenate([high, (total - high.astype(F32)).astype(BF16)], axis=0)
    out_ref[...] = both
    for k in range(N_COL):
        wide_ref[k] = both


def mid1(rr, own, parts):
    return call(
        mid1_body,
        [shape(2 * RANK, BLOCK, dtype=BF16), shape(N_COL, 2 * RANK, BLOCK, dtype=BF16)],
        [VMEM] * 5,
        1_000_000,
        4 << 20,
        8,
    )(rr, own, *parts)


def load(tiles_ref, tiles, sems, group):
    slots = pl.ds(group * GROUP, GROUP)
    return pltpu.make_async_copy(tiles_ref.at[slots], tiles.at[slots], sems.at[group])


def load_all(count, tiles_ref, tiles, sems):
    def begin(group, carry):
        load(tiles_ref, tiles, sems, group).start()
        return carry

    lax.fori_loop(0, groups_of(count), begin, 0)


def arrive(count, tiles_ref, tiles, sems, group):
    load(tiles_ref, tiles, sems, group).wait()

    def clear(slot, carry):
        tiles[slot] = jnp.zeros((BLOCK, BLOCK), BF16)
        return carry

    lax.fori_loop(jnp.maximum(count[0], group * GROUP), group * GROUP + GROUP, clear, 0)


TILES = [pltpu.VMEM((SLOTS, BLOCK, BLOCK), BF16), pltpu.SemaphoreType.DMA((SLOTS // GROUP,))]


def join(near_ref, far_ref, joined_ref):
    joined_ref[:4] = near_ref[...]
    joined_ref[4:] = far_ref[...]


def product_body(pairs, count, place, tiles_ref, qr_ref, near_ref, far_ref, rows_ref, cols_ref, qc_ref, tiles, sems):
    load_all(count, tiles_ref, tiles, sems)
    rows_ref[...] = jnp.zeros_like(rows_ref)
    cols_ref[...] = jnp.zeros_like(cols_ref)
    join(near_ref, far_ref, qc_ref)

    def some(group, carry):
        arrive(count, tiles_ref, tiles, sems, group)
        done = []
        for k in range(GROUP):
            slot = group * GROUP + k
            i = pairs[2 * slot] % N_COL
            j = row_offset(place, pairs[2 * slot + 1] // N_COL)
            tile = tiles[slot]
            into_cols = jnp.dot(qr_ref[i], tile, preferred_element_type=F32)
            into_rows = lax.dot_general(
                qc_ref[j], tile, (((1,), (1,)), ((), ())), preferred_element_type=F32
            )
            done.append((i, j, into_rows[:RANK] + into_rows[RANK:], into_cols[:RANK] + into_cols[RANK:]))
        for i, j, into_rows, into_cols in done:
            cols_ref[j, :RANK] += into_cols
            rows_ref[i] += into_rows
        return carry

    lax.fori_loop(0, groups_of(count), some, 0)
    gram = jnp.zeros((RANK, RANK), F32)
    for k in range(N_COL):
        both = lax.dot_general(
            qr_ref[k, :RANK], qr_ref[k], (((1,), (1,)), ((), ())), preferred_element_type=F32
        )
        low_high = lax.dot_general(
            qr_ref[k, RANK:], qr_ref[k, :RANK], (((1,), (1,)), ((), ())), preferred_element_type=F32
        )
        gram = gram + both[:, :RANK] + (both[:, RANK:] + low_high)
    for k in range(N_ROW):
        for q in range(4):
            cols_ref[k, RANK:, 64 * q : 64 * q + 64] = gram[16 * q : 16 * q + 16]


def product(pairs, count, place, tiles, qr, near, far):
    return call(
        product_body,
        [shape(N_COL, RANK, BLOCK), shape(N_ROW, RANK + 16, BLOCK)],
        [SMEM] * 3 + [HBM] + [VMEM] * 3,
        1_000_000_000,
        8 << 20,
        30,
        scratch=[pltpu.VMEM((N_ROW, 2 * RANK, BLOCK), BF16)] + TILES,
    )(pairs, count, place, tiles, qr, near, far)


PANEL = 8
PACKED = RANK // 2 + 8


def inverse_factor(gram):
    eye = (
        lax.broadcasted_iota(jnp.int32, (RANK, RANK), 0)
        == lax.broadcasted_iota(jnp.int32, (RANK, RANK), 1)
    ).astype(F32)
    work = jnp.concatenate([gram, eye], axis=1)
    out = []
    for base in range(0, RANK, PANEL):
        rows = [work[p : p + 1, :] for p in range(PANEL)]
        entry = {
            (p, q): jnp.broadcast_to(rows[p][:, base + q : base + q + 1], (1, 2 * RANK))
            for p in range(PANEL)
            for q in range(p, PANEL)
        }
        work = work[PANEL:]
        more = base + PANEL < RANK
        factor = [
            jnp.broadcast_to(work[:, base + p : base + p + 1], work.shape)
            for p in range(PANEL if more else 0)
        ]
        for p in range(PANEL):
            inverse = 1.0 / entry[p, p]
            for q in range(p + 1, PANEL):
                ratio = entry[p, q] * inverse
                rows[q] = rows[q] - ratio * rows[p]
                for r in range(q, PANEL):
                    entry[q, r] = entry[q, r] - ratio * entry[p, r]
            if more:
                factor[p] = factor[p] * inverse
                for q in range(p + 1, PANEL):
                    factor[q] = factor[q] - factor[p] * entry[p, q]
            out.append(lax.rsqrt(entry[p, p]) * rows[p])
        if more:
            for p in range(PANEL):
                work = work - factor[p] * rows[p]
    return jnp.concatenate(out, axis=0)[:, RANK:]


def row_less_col(strict):
    row = lax.broadcasted_iota(jnp.int32, (RANK, RANK), 0)
    col = lax.broadcasted_iota(jnp.int32, (RANK, RANK), 1)
    return row < col if strict else row <= col


def eps_eye():
    same = lax.broadcasted_iota(jnp.int32, (RANK, RANK), 0) == lax.broadcasted_iota(
        jnp.int32, (RANK, RANK), 1
    )
    return jnp.where(same, GRAM_EPS, 0.0).astype(F32)


def dot_t(a, b):
    return lax.dot_general(
        a, b, (((1,), (1,)), ((), ())), precision=HIGHEST, preferred_element_type=F32
    )


def mid2_body(rr_ref, own_ref, a_ref, b_ref, c_ref, p_ref, q_ref, wide_ref, gram_ref):
    parts = (a_ref, b_ref, c_ref)
    total = total_of(rr_ref, own_ref, parts)
    packed = own_ref[0, RANK:]
    for part in parts:
        packed = packed + part[0, RANK:]
    gram = jnp.concatenate([packed[:, 64 * q : 64 * q + 64] for q in range(4)], axis=0)
    inverse = inverse_factor(gram / CELLS + eps_eye())
    normal = jnp.dot(inverse, total, precision=HIGHEST, preferred_element_type=F32)
    p_ref[...] = normal
    rounded = normal.astype(BF16)
    q_ref[...] = rounded
    for k in range(N_COL):
        wide_ref[k] = rounded
    gram_ref[...] = dot_t(normal, normal)


def mid2(rr, own, parts):
    return call(
        mid2_body,
        [
            shape(RANK, BLOCK),
            shape(RANK, BLOCK, dtype=BF16),
            shape(N_COL, RANK, BLOCK, dtype=BF16),
            shape(RANK, RANK),
        ],
        [VMEM] * 5,
        10_000_000,
        2 << 20,
        8,
    )(rr, own, *parts)


def project_body(
    pairs, count, place, tiles_ref, qr_ref, near_ref, far_ref, gram_ref, out_ref, cols_ref, qc_ref, tiles, sems
):
    load_all(count, tiles_ref, tiles, sems)
    cols_ref[...] = jnp.zeros_like(cols_ref)
    join(near_ref, far_ref, qc_ref)

    def some(group, carry):
        arrive(count, tiles_ref, tiles, sems, group)
        done = []
        for k in range(GROUP):
            slot = group * GROUP + k
            i = pairs[2 * slot] % N_COL
            j = row_offset(place, pairs[2 * slot + 1] // N_COL)
            done.append((j, jnp.dot(qr_ref[i], tiles[slot], preferred_element_type=F32)))
        for j, into_cols in done:
            cols_ref[j] += into_cols
        return carry

    lax.fori_loop(0, groups_of(count), some, 0)
    form = jnp.zeros((RANK, RANK), F32)
    for k in range(N_ROW):
        form = form + dot_t(cols_ref[k], qc_ref[k].astype(F32))
    gram = gram_ref[...]
    packed = jnp.where(row_less_col(False), form + form.T, gram)
    diagonal = jnp.sum(jnp.where(eps_eye() > 0.0, gram, 0.0), axis=0, keepdims=True)
    both = jnp.concatenate([packed[: RANK // 2], packed[RANK // 2 :]], axis=1)
    tail = jnp.concatenate([diagonal, jnp.zeros((1, RANK), F32)], axis=1)
    for k in range(N_ROW):
        out_ref[k, : RANK // 2] = both
        out_ref[k, RANK // 2 :] = jnp.broadcast_to(tail, (8, 2 * RANK))


def project(pairs, count, place, tiles, qr, near, far, gram):
    return call(
        project_body,
        shape(N_ROW, PACKED, 2 * RANK),
        [SMEM] * 3 + [HBM] + [VMEM] * 4,
        500_000_000,
        6 << 20,
        30,
        scratch=[pltpu.VMEM((N_ROW, RANK, BLOCK), F32), pltpu.VMEM((N_ROW, RANK, BLOCK), BF16)]
        + TILES,
    )(pairs, count, place, tiles, qr, near, far, gram)


def respread_body(parts_ref, out_ref):
    total = parts_ref[0]
    for k in range(1, N_ROW):
        total = total + parts_ref[k]
    for k in range(N_COL):
        out_ref[k] = total


def respread(parts):
    return call(respread_body, shape(N_COL, PACKED, 2 * RANK), [VMEM], 100_000, 1 << 19, 4)(parts)


def finish_body(parts_ref, p_ref, basis_ref, form_ref):
    total = parts_ref[0]
    for k in range(1, N_COL):
        total = total + parts_ref[k]
    top = total[: RANK // 2]
    packed = jnp.concatenate([top[:, :RANK], top[:, RANK:]], axis=0)
    lower = jnp.where(row_less_col(False), 0.0, packed)
    diagonal = jnp.where(eps_eye() > 0.0, total[RANK // 2 : RANK // 2 + 1, :RANK], 0.0)
    inverse = inverse_factor((lower + lower.T + diagonal) / CELLS + eps_eye())
    basis_ref[...] = jnp.dot(inverse, p_ref[...], precision=HIGHEST, preferred_element_type=F32)
    upper = jnp.where(row_less_col(False), packed, 0.0)
    form = (upper + jnp.where(row_less_col(True), packed, 0.0).T) / CELLS
    form_ref[...] = jnp.dot(
        inverse, dot_t(form, inverse), precision=HIGHEST, preferred_element_type=F32
    )


def finish(parts, p):
    return call(
        finish_body, [shape(RANK, BLOCK), shape(RANK, RANK)], [VMEM, VMEM], 10_000_000, 1 << 20, 6
    )(parts, p)


def swap(x, axis):
    return lax.all_to_all(x, axis, 0, 0, tiled=True)


def shift(x, axis, k):
    if axis == "x":
        pairs = [(d, (d // 2 + k) % 4 * 2 + d % 2) for d in range(N_ROW)]
    elif axis == "core":
        pairs = [(d, d ^ k) for d in range(N_ROW)]
    elif axis == "y":
        pairs = [(d, (d // 4 + k) % 4 * 4 + d % 4) for d in range(N_COL)]
    else:
        pairs = [(d, d // 4 * 4 + (d + k) % 4) for d in range(N_COL)]
    return lax.ppermute(x, "row" if axis in ("x", "core") else "col", pairs)


def around(x, axis):
    return [x] + [shift(x, axis, k) for k in range(1, 4)]


def both_ways(pieces, axis):
    low, high = jnp.stack(pieces[:2]), jnp.stack(pieces[2:])
    low_up, high_down = shift(low, axis, 1), shift(high, axis, 3)
    high_up, low_down = shift(high, axis, 1), shift(low, axis, 3)
    low_far, high_far = shift(low_up, axis, 1), shift(high_down, axis, 3)
    return [low, high, low_up, high_up, low_far, high_far, low_down, high_down]


def scatter(rows, cols):
    own = cols[:4] + shift(cols[4:], "core", 1)
    parts = [shift(own[k : k + 1], "x", 4 - k) for k in range(1, 4)]
    return swap(rows, "col"), own, parts


def gather(q, wide):
    near = around(q, "x")
    qr = swap(wide, "col")
    near = jnp.stack(near)
    return qr, near, shift(near, "core", 1)


def local(series, lag_weight, start_basis, block_pairs, pair_count):
    pairs = block_pairs.reshape(2 * SLOTS)
    count = pair_count.reshape(1)
    row, col = lax.axis_index("row"), lax.axis_index("col")
    place = jnp.stack([row // 2, row % 2, col // 4, col % 4]).astype(jnp.int32)
    lead = series.T
    packed = jnp.concatenate([start_basis[:32], start_basis[32:]], axis=1)
    first = jnp.concatenate([lead[:HALF], packed[:16]], axis=0)
    second = jnp.concatenate([lead[HALF:], packed[16:]], axis=0)
    trail = jnp.concatenate([series, start_basis], axis=0)
    first, second, trail = lax.optimization_barrier((first, second, trail))
    first, second = around(first, "z"), around(second, "y")
    trail = around(trail, "x")
    first, second = lax.optimization_barrier((first, second))
    first, second = both_ways(first, "y"), both_ways(second, "z")
    own = jnp.stack(trail)
    other = shift(own, "core", 1)
    sums, xc = day_sums(own, other)
    tiles, rows, cols = build(pairs, count, place, lag_weight, sums, xc, first, second)
    q1, wide = mid1(*scatter(rows, cols))
    rows, cols = product(pairs, count, place, tiles, *gather(q1, wide))
    p2, q2, wide, gram = mid2(*scatter(rows, cols))
    part = project(pairs, count, place, tiles, *gather(q2, wide), gram)
    return finish(swap(respread(swap(part, "row")), "col"), p2)


def solution(mesh):
    return jax.shard_map(
        local,
        mesh=mesh,
        in_specs=(
            P(None, ("row", "col")),
            P(),
            P(None, ("row", "col")),
            P("row", "col", None, None),
            P("row", "col"),
        ),
        out_specs=(P(None, ("row", "col")), P()),
        check_vma=False,
    )
```

profile of v0, /device:TPU:1, one launch (start us, length us, event | category | flops | bytes accessed | tf_op | source)
XLA Modules:
  0.0 210.0 jit_solution(4720496767619944880)
XLA Ops:
  3.5 3.4 %collective-permute-start.2 = (bf16[576,256]{1,0:T(8,128)(2,1)S(1)}, bf16[576,256]{1,0:T(8,128)(2,1)S(1)}, u32[]{:S(2)}, u32[]{:S(2)}) collective-permute-start(bf16[576,256]{1,0:T(8,128)(2,1)S(1)} %pad_maximum_fusion.1), channel_id=1, source_target_pairs={{0,96},{16,112},{32,0},{48,16},{64,32},{80,48},{96,64},{112,80},{1... | collective-permute-start | bytes 884744 | tf_op jit(solution)/shard_map/ppermute | solution.py:496
  8.0 5.7 %collective-permute-done.2 = bf16[576,256]{1,0:T(8,128)(2,1)S(1)} collective-permute-done((bf16[576,256]{1,0:T(8,128)(2,1)S(1)}, bf16[576,256]{1,0:T(8,128)(2,1)S(1)}, u32[]{:S(2)}, u32[]{:S(2)}) %collective-permute-start.2) | collective-permute-done | bytes 294944 | tf_op jit(solution)/shard_map/ppermute | solution.py:496
  16.1 7.6 %collective-permute-done = bf16[576,256]{1,0:T(8,128)(2,1)S(1)} collective-permute-done((bf16[576,256]{1,0:T(8,128)(2,1)S(1)}, bf16[576,256]{1,0:T(8,128)(2,1)S(1)}, u32[]{:S(2)}, u32[]{:S(2)}) %collective-permute-start) | collective-permute-done | bytes 294944 | tf_op jit(solution)/shard_map/ppermute | solution.py:496
  24.4 3.8 %collective-permute-start.6 = (bf16[144,512]{1,0:T(8,128)(2,1)S(1)}, bf16[144,512]{1,0:T(8,128)(2,1)S(1)}, u32[]{:S(2)}, u32[]{:S(2)}) collective-permute-start(bf16[144,512]{1,0:T(8,128)(2,1)S(1)} %get-tuple-element.31), channel_id=1, source_target_pairs={{0,3},{1,0},{2,1},{3,2},{4,7},{5,4},{6,5},{7,6},{8,11},{9,8},{10,9... | collective-permute-start | bytes 442376 | tf_op jit(solution)/shard_map/ppermute | solution.py:496
  40.5 4.0 %collective-permute-done.7 = bf16[144,512]{1,0:T(8,128)(2,1)S(1)} collective-permute-done((bf16[144,512]{1,0:T(8,128)(2,1)S(1)}, bf16[144,512]{1,0:T(8,128)(2,1)S(1)}, u32[]{:S(2)}, u32[]{:S(2)}) %collective-permute-start.7) | collective-permute-done | bytes 147488 | tf_op jit(solution)/shard_map/ppermute | solution.py:496
  44.6 3.5 %collective-permute-start.19 = (bf16[2,144,512]{2,1,0:T(8,128)(2,1)S(1)}, bf16[2,144,512]{2,1,0:T(8,128)(2,1)}, u32[]{:S(2)}, u32[]{:S(2)}) collective-permute-start(bf16[2,144,512]{2,1,0:T(8,128)(2,1)S(1)} %pad_maximum_fusion.5.rest_9_), channel_id=1, source_target_pairs={{0,3},{1,0},{2,1},{3,2},{4,7},{5,4},{6,5},{7,6},{8,11},{9,8},{10,9... | collective-permute-start | bytes 884744 | tf_op jit(solution)/shard_map/ppermute | solution.py:496
  53.2 3.1 %collective-permute-done.17.rest_11_ = bf16[2,144,512]{2,1,0:T(8,128)(2,1)S(1)} collective-permute-done((bf16[2,144,512]{2,1,0:T(8,128)(2,1)S(1)}, bf16[2,144,512]{2,1,0:T(8,128)(2,1)S(1)}, u32[]{:S(2)}, u32[]{:S(2)}) %collective-permute-start.17) | collective-permute-done | bytes 294944 | tf_op jit(solution)/shard_map/ppermute | solution.py:496
  63.0 3.4 %collective-permute-start.20 = (bf16[2,144,512]{2,1,0:T(8,128)(2,1)}, bf16[2,144,512]{2,1,0:T(8,128)(2,1)}, u32[]{:S(2)}, u32[]{:S(2)}) collective-permute-start(bf16[2,144,512]{2,1,0:T(8,128)(2,1)} %collective-permute-done.19.rest_15_), channel_id=1, source_target_pairs={{0,3},{1,0},{2,1},{3,2},{4,7},{5,4},{6,5},{7,6},{8,11},{9,8},{10,9... | collective-permute-start | bytes 884744 | tf_op jit(solution)/shard_map/ppermute | solution.py:496
  77.0 12.8 %shard_map.69 = (bf16[288,256,256]{2,1,0:T(8,128)(2,1)}, f32[16,64,256]{2,1,0:T(8,128)}, f32[8,64,256]{2,1,0:T(8,128)S(1)}) custom-call(s32[64]{0:T(128)S(1)} %reshape.10.pairs, s32[1]{0:T(128)} %bitcast.28.count, s32[4]{0:T(128)S(1)} %pad_add_fusion.place, f32[4]{0:T(128)S(1)} %copy-done.6, bf16[8,4,512,256]{3,2,1,0:T(8,128)(2,1)S(1)} %get-tuple-element.27.sums_ref, ...), custom_call_target="tpu_custom_call" | custom-call | flops 8999999488 | bytes 20971520 | tf_op jit(solution)/shard_map/pallas_call | solution.py:175
  89.8 7.4 %all-to-all-start = ((f32[16,64,256]{2,1,0:T(8,128)}), f32[16,64,256]{2,1,0:T(8,128)S(1)}, u32[]{:S(2)}, u32[]{:S(2)}) async-start(f32[16,64,256]{2,1,0:T(8,128)} %get-tuple-element.40), calls=%async_computation | async-start | bytes 2097152 | tf_op jit(solution)/shard_map/all_to_all | solution.py:484
  97.3 8.8 %collective-permute-start.22 = (f32[4,64,256]{2,1,0:T(8,128)S(1)}, f32[4,64,256]{2,1,0:T(8,128)S(1)}, u32[]{:S(2)}, u32[]{:S(2)}) collective-permute-start(f32[4,64,256]{2,1,0:T(8,128)S(1)} %slice.55), channel_id=1, source_target_pairs={{0,16},{16,0},{32,48},{48,32},{64,80},{80,64},{96,112},{112,96},{1... | collective-permute-start | bytes 786440 | tf_op jit(solution)/shard_map/ppermute | solution.py:496
  110.2 3.6 %collective-permute-done.25.c_ref = f32[1,64,256]{2,1,0:T(8,128)S(1)} collective-permute-done((f32[1,64,256]{2,1,0:T(8,128)S(1)}, f32[1,64,256]{2,1,0:T(8,128)S(1)}, u32[]{:S(2)}, u32[]{:S(2)}) %collective-permute-start.25) | collective-permute-done | bytes 65568 | tf_op jit(solution)/shard_map/ppermute | solution.py:496
  114.9 6.9 %all-to-all-start.1 = ((bf16[16,128,256]{2,1,0:T(8,128)(2,1)}), bf16[16,128,256]{2,1,0:T(8,128)(2,1)S(1)}, u32[]{:S(2)}, u32[]{:S(2)}) async-start(bf16[16,128,256]{2,1,0:T(8,128)(2,1)} %get-tuple-element.42), calls=%async_computation.1 | async-start | bytes 2097152 | tf_op jit(solution)/shard_map/all_to_all | solution.py:484
  133.7 3.3 %all-to-all-done.1.qr_ref = bf16[16,128,256]{2,1,0:T(8,128)(2,1)S(1)} async-done(((bf16[16,128,256]{2,1,0:T(8,128)(2,1)}), bf16[16,128,256]{2,1,0:T(8,128)(2,1)S(1)}, u32[]{:S(2)}, u32[]{:S(2)}) %all-to-all-start.1) | async-done | bytes 1048608 | tf_op jit(solution)/shard_map/all_to_all | solution.py:484
  137.1 5.2 %shard_map.71 = (f32[16,64,256]{2,1,0:T(8,128)}, f32[8,80,256]{2,1,0:T(8,128)S(1)}) custom-call(s32[64]{0:T(128)S(1)} %reshape.10.pairs, s32[1]{0:T(128)} %bitcast.29.count, s32[4]{0:T(128)S(1)} %pad_add_fusion.place, bf16[288,256,256]{2,1,0:T(8,128)(2,1)} %get-tuple-element.39.tiles_ref, bf16[16,128,256]{2,1,0:T(8,128)(2,1)S(1)} %all-to-all-done.1.qr_ref, ...), custom_call_target="tpu_custom_call" | custom-call | flops 1000000000 | bytes 8388608 | tf_op jit(solution)/shard_map/pallas_call | solution.py:297
  142.2 3.7 %all-to-all-start.2 = ((f32[16,64,256]{2,1,0:T(8,128)}), f32[16,64,256]{2,1,0:T(8,128)S(1)}, u32[]{:S(2)}, u32[]{:S(2)}) async-start(f32[16,64,256]{2,1,0:T(8,128)} %get-tuple-element.44), calls=%async_computation.2 | async-start | bytes 2097152 | tf_op jit(solution)/shard_map/all_to_all | solution.py:484
  146.0 4.3 %collective-permute-start.30 = (f32[4,80,256]{2,1,0:T(8,128)S(1)}, f32[4,80,256]{2,1,0:T(8,128)S(1)}, u32[]{:S(2)}, u32[]{:S(2)}) collective-permute-start(f32[4,80,256]{2,1,0:T(8,128)S(1)} %slice.60), channel_id=1, source_target_pairs={{0,16},{16,0},{32,48},{48,32},{64,80},{80,64},{96,112},{112,96},{1... | collective-permute-start | bytes 983048 | tf_op jit(solution)/shard_map/ppermute | solution.py:496
  154.4 4.3 %collective-permute-done.33.c_ref = f32[1,80,256]{2,1,0:T(8,128)S(1)} collective-permute-done((f32[1,80,256]{2,1,0:T(8,128)S(1)}, f32[1,80,256]{2,1,0:T(8,128)S(1)}, u32[]{:S(2)}, u32[]{:S(2)}) %collective-permute-start.33) | collective-permute-done | bytes 81952 | tf_op jit(solution)/shard_map/ppermute | solution.py:496
  161.5 6.9 %all-to-all-start.3 = ((bf16[16,64,256]{2,1,0:T(8,128)(2,1)}), bf16[16,64,256]{2,1,0:T(8,128)(2,1)S(1)}, u32[]{:S(2)}, u32[]{:S(2)}) async-start(bf16[16,64,256]{2,1,0:T(8,128)(2,1)} %get-tuple-element.46), calls=%async_computation.3 | async-start | bytes 1048576 | tf_op jit(solution)/shard_map/all_to_all | solution.py:484
  172.2 3.3 %collective-permute-done.35 = bf16[64,256]{1,0:T(8,128)(2,1)S(1)} collective-permute-done((bf16[64,256]{1,0:T(8,128)(2,1)S(1)}, bf16[64,256]{1,0:T(8,128)(2,1)S(1)}, u32[]{:S(2)}, u32[]{:S(2)}) %collective-permute-start.35) | collective-permute-done | bytes 32800 | tf_op jit(solution)/shard_map/ppermute | solution.py:496
  175.6 3.9 %collective-permute-start.37 = (bf16[4,64,256]{2,1,0:T(8,128)(2,1)S(1)}, bf16[4,64,256]{2,1,0:T(8,128)(2,1)S(1)}, u32[]{:S(2)}, u32[]{:S(2)}) collective-permute-start(bf16[4,64,256]{2,1,0:T(8,128)(2,1)S(1)} %pad_maximum_fusion.8.near_ref), channel_id=1, source_target_pairs={{0,16},{16,0},{32,48},{48,32},{64,80},{80,64},{96,112},{112,96},{1... | collective-permute-start | bytes 393224 | tf_op jit(solution)/shard_map/ppermute | solution.py:496
  180.5 3.7 %shard_map.73 = f32[8,40,128]{2,1,0:T(8,128)S(1)} custom-call(s32[64]{0:T(128)S(1)} %reshape.10.pairs, s32[1]{0:T(128)} %bitcast.30.count, s32[4]{0:T(128)S(1)} %pad_add_fusion.place, bf16[288,256,256]{2,1,0:T(8,128)(2,1)} %get-tuple-element.39.tiles_ref, bf16[16,64,256]{2,1,0:T(8,128)(2,1)S(1)} %all-to-all-done.3.qr_ref, ...), custom_call_target="tpu_custom_call" | custom-call | flops 500000000 | bytes 6291456 | tf_op jit(solution)/shard_map/pallas_call | solution.py:436
  184.1 9.0 %all_to_all.30.parts_ref = f32[8,40,128]{2,1,0:T(8,128)S(1)} all-to-all(f32[8,40,128]{2,1,0:T(8,128)S(1)} %shard_map.73), channel_id=1, replica_groups=mesh['row'=8,'col'=16] {'row'}, dimensions={0} | all-to-all | bytes 327680 | tf_op jit(solution)/shard_map/all_to_all | solution.py:484
  193.2 13.9 %all_to_all.31.parts_ref = f32[16,40,128]{2,1,0:T(8,128)S(1)} all-to-all(f32[16,40,128]{2,1,0:T(8,128)S(1)} %shard_map.74), channel_id=1, replica_groups=mesh['row'=8,'col'=16] {'col'}, dimensions={0} | all-to-all | bytes 655360 | tf_op jit(solution)/shard_map/all_to_all | solution.py:484
  (108 shorter events, 73.0 us)
Async XLA Ops:
  3.5 10.2 %collective-permute-start.2 = (bf16[576,256]{1,0:T(8,128)(2,1)S(1)}, bf16[576,256]{1,0:T(8,128)(2,1)S(1)}, u32[]{:S(2)}, u32[]{:S(2)}) collective-permute-start(bf16[576,256]{1,0:T(8,128)(2,1)S(1)} %pad_maximum_fusion.1), channel_id=1, source_target_pairs={{0,96},{16,112},{32,0},{48,16},{64,32},{80,48},{96,64},{112,80},{1... | collective-permute-start | bytes 884744 | tf_op jit(solution)/shard_map/ppermute | solution.py:496
  6.9 9.2 %collective-permute-start.1 = (bf16[576,256]{1,0:T(8,128)(2,1)S(1)}, bf16[576,256]{1,0:T(8,128)(2,1)S(1)}, u32[]{:S(2)}, u32[]{:S(2)}) collective-permute-start(bf16[576,256]{1,0:T(8,128)(2,1)S(1)} %pad_maximum_fusion.1), channel_id=1, source_target_pairs={{0,64},{16,80},{32,96},{48,112},{64,0},{80,16},{96,32},{112,48},{1... | collective-permute-start | bytes 884744 | tf_op jit(solution)/shard_map/ppermute | solution.py:496
  7.4 16.2 %collective-permute-start = (bf16[576,256]{1,0:T(8,128)(2,1)S(1)}, bf16[576,256]{1,0:T(8,128)(2,1)S(1)}, u32[]{:S(2)}, u32[]{:S(2)}) collective-permute-start(bf16[576,256]{1,0:T(8,128)(2,1)S(1)} %pad_maximum_fusion.1), channel_id=1, source_target_pairs={{0,32},{16,48},{32,64},{48,80},{64,96},{80,112},{96,0},{112,16},{1... | collective-permute-start | bytes 884744 | tf_op jit(solution)/shard_map/ppermute | solution.py:496
  23.8 45.2 %collective-permute-start.3 = (bf16[4,576,256]{2,1,0:T(8,128)(2,1)S(1)}, bf16[4,576,256]{2,1,0:T(8,128)(2,1)S(1)}, u32[]{:S(2)}, u32[]{:S(2)}) collective-permute-start(bf16[4,576,256]{2,1,0:T(8,128)(2,1)S(1)} %pad_maximum_fusion.own_ref), channel_id=1, source_target_pairs={{0,16},{16,0},{32,48},{48,32},{64,80},{80,64},{96,112},{112,96},{1... | collective-permute-start | bytes 3538952 | tf_op jit(solution)/shard_map/ppermute | solution.py:496
  24.4 10.1 %collective-permute-start.6 = (bf16[144,512]{1,0:T(8,128)(2,1)S(1)}, bf16[144,512]{1,0:T(8,128)(2,1)S(1)}, u32[]{:S(2)}, u32[]{:S(2)}) collective-permute-start(bf16[144,512]{1,0:T(8,128)(2,1)S(1)} %get-tuple-element.31), channel_id=1, source_target_pairs={{0,3},{1,0},{2,1},{3,2},{4,7},{5,4},{6,5},{7,6},{8,11},{9,8},{10,9... | collective-permute-start | bytes 442376 | tf_op jit(solution)/shard_map/ppermute | solution.py:496
  28.1 9.3 %collective-permute-start.5 = (bf16[144,512]{1,0:T(8,128)(2,1)S(1)}, bf16[144,512]{1,0:T(8,128)(2,1)S(1)}, u32[]{:S(2)}, u32[]{:S(2)}) collective-permute-start(bf16[144,512]{1,0:T(8,128)(2,1)S(1)} %get-tuple-element.31), channel_id=1, source_target_pairs={{0,2},{1,3},{2,0},{3,1},{4,6},{5,7},{6,4},{7,5},{8,10},{9,11},{10,... | collective-permute-start | bytes 442376 | tf_op jit(solution)/shard_map/ppermute | solution.py:496
  28.1 9.8 %collective-permute-start.4 = (bf16[144,512]{1,0:T(8,128)(2,1)S(1)}, bf16[144,512]{1,0:T(8,128)(2,1)S(1)}, u32[]{:S(2)}, u32[]{:S(2)}) collective-permute-start(bf16[144,512]{1,0:T(8,128)(2,1)S(1)} %get-tuple-element.31), channel_id=1, source_target_pairs={{0,1},{1,2},{2,3},{3,0},{4,5},{5,6},{6,7},{7,4},{8,9},{9,10},{10,1... | collective-permute-start | bytes 442376 | tf_op jit(solution)/shard_map/ppermute | solution.py:496
  28.8 9.2 %collective-permute-start.9 = (bf16[144,512]{1,0:T(8,128)(2,1)S(1)}, bf16[144,512]{1,0:T(8,128)(2,1)S(1)}, u32[]{:S(2)}, u32[]{:S(2)}) collective-permute-start(bf16[144,512]{1,0:T(8,128)(2,1)S(1)} %get-tuple-element.35), channel_id=1, source_target_pairs={{0,12},{1,13},{2,14},{3,15},{4,0},{5,1},{6,2},{7,3},{8,4},{9,5},{1... | collective-permute-start | bytes 442376 | tf_op jit(solution)/shard_map/ppermute | solution.py:496
  44.6 8.6 %collective-permute-start.19 = (bf16[2,144,512]{2,1,0:T(8,128)(2,1)S(1)}, bf16[2,144,512]{2,1,0:T(8,128)(2,1)}, u32[]{:S(2)}, u32[]{:S(2)}) collective-permute-start(bf16[2,144,512]{2,1,0:T(8,128)(2,1)S(1)} %pad_maximum_fusion.5.rest_9_), channel_id=1, source_target_pairs={{0,3},{1,0},{2,1},{3,2},{4,7},{5,4},{6,5},{7,6},{8,11},{9,8},{10,9... | collective-permute-start | bytes 884744 | tf_op jit(solution)/shard_map/ppermute | solution.py:496
  48.1 8.3 %collective-permute-start.17 = (bf16[2,144,512]{2,1,0:T(8,128)(2,1)S(1)}, bf16[2,144,512]{2,1,0:T(8,128)(2,1)S(1)}, u32[]{:S(2)}, u32[]{:S(2)}) collective-permute-start(bf16[2,144,512]{2,1,0:T(8,128)(2,1)S(1)} %pad_maximum_fusion.5.rest_9_), channel_id=1, source_target_pairs={{0,1},{1,2},{2,3},{3,0},{4,5},{5,6},{6,7},{7,4},{8,9},{9,10},{10,1... | collective-permute-start | bytes 884744 | tf_op jit(solution)/shard_map/ppermute | solution.py:496
  48.1 11.4 %collective-permute-start.21 = (bf16[2,144,512]{2,1,0:T(8,128)(2,1)S(1)}, bf16[2,144,512]{2,1,0:T(8,128)(2,1)S(1)}, u32[]{:S(2)}, u32[]{:S(2)}) collective-permute-start(bf16[2,144,512]{2,1,0:T(8,128)(2,1)S(1)} %pad_maximum_fusion.4.rest_8_), channel_id=1, source_target_pairs={{0,3},{1,0},{2,1},{3,2},{4,7},{5,4},{6,5},{7,6},{8,11},{9,8},{10,9... | collective-permute-start | bytes 884744 | tf_op jit(solution)/shard_map/ppermute | solution.py:496
  50.9 11.9 %collective-permute-start.16 = (bf16[2,144,512]{2,1,0:T(8,128)(2,1)S(1)}, bf16[2,144,512]{2,1,0:T(8,128)(2,1)}, u32[]{:S(2)}, u32[]{:S(2)}) collective-permute-start(bf16[2,144,512]{2,1,0:T(8,128)(2,1)S(1)} %pad_maximum_fusion.4.rest_8_), channel_id=1, source_target_pairs={{0,1},{1,2},{2,3},{3,0},{4,5},{5,6},{6,7},{7,4},{8,9},{9,10},{10,1... | collective-permute-start | bytes 884744 | tf_op jit(solution)/shard_map/ppermute | solution.py:496
  53.2 9.7 %collective-permute-start.13 = (bf16[2,144,512]{2,1,0:T(8,128)(2,1)S(1)}, bf16[2,144,512]{2,1,0:T(8,128)(2,1)}, u32[]{:S(2)}, u32[]{:S(2)}) collective-permute-start(bf16[2,144,512]{2,1,0:T(8,128)(2,1)S(1)} %pad_maximum_fusion.3.rest_1_), channel_id=1, source_target_pairs={{0,12},{1,13},{2,14},{3,15},{4,0},{5,1},{6,2},{7,3},{8,4},{9,5},{1... | collective-permute-start | bytes 884744 | tf_op jit(solution)/shard_map/ppermute | solution.py:496
  57.1 9.3 %collective-permute-start.11 = (bf16[2,144,512]{2,1,0:T(8,128)(2,1)S(1)}, bf16[2,144,512]{2,1,0:T(8,128)(2,1)S(1)}, u32[]{:S(2)}, u32[]{:S(2)}) collective-permute-start(bf16[2,144,512]{2,1,0:T(8,128)(2,1)S(1)} %pad_maximum_fusion.3.rest_1_), channel_id=1, source_target_pairs={{0,4},{1,5},{2,6},{3,7},{4,8},{5,9},{6,10},{7,11},{8,12},{9,13},{1... | collective-permute-start | bytes 884744 | tf_op jit(solution)/shard_map/ppermute | solution.py:496
  60.3 8.7 %collective-permute-start.10 = (bf16[2,144,512]{2,1,0:T(8,128)(2,1)S(1)}, bf16[2,144,512]{2,1,0:T(8,128)(2,1)}, u32[]{:S(2)}, u32[]{:S(2)}) collective-permute-start(bf16[2,144,512]{2,1,0:T(8,128)(2,1)S(1)} %pad_maximum_fusion.2.rest_0_), channel_id=1, source_target_pairs={{0,4},{1,5},{2,6},{3,7},{4,8},{5,9},{6,10},{7,11},{8,12},{9,13},{1... | collective-permute-start | bytes 884744 | tf_op jit(solution)/shard_map/ppermute | solution.py:496
  62.8 12.7 %collective-permute-start.15 = (bf16[2,144,512]{2,1,0:T(8,128)(2,1)S(1)}, bf16[2,144,512]{2,1,0:T(8,128)(2,1)}, u32[]{:S(2)}, u32[]{:S(2)}) collective-permute-start(bf16[2,144,512]{2,1,0:T(8,128)(2,1)S(1)} %pad_maximum_fusion.2.rest_0_), channel_id=1, source_target_pairs={{0,12},{1,13},{2,14},{3,15},{4,0},{5,1},{6,2},{7,3},{8,4},{9,5},{1... | collective-permute-start | bytes 884744 | tf_op jit(solution)/shard_map/ppermute | solution.py:496
  63.0 12.5 %collective-permute-start.20 = (bf16[2,144,512]{2,1,0:T(8,128)(2,1)}, bf16[2,144,512]{2,1,0:T(8,128)(2,1)}, u32[]{:S(2)}, u32[]{:S(2)}) collective-permute-start(bf16[2,144,512]{2,1,0:T(8,128)(2,1)} %collective-permute-done.19.rest_15_), channel_id=1, source_target_pairs={{0,3},{1,0},{2,1},{3,2},{4,7},{5,4},{6,5},{7,6},{8,11},{9,8},{10,9... | collective-permute-start | bytes 884744 | tf_op jit(solution)/shard_map/ppermute | solution.py:496
  67.1 8.4 %collective-permute-start.18 = (bf16[2,144,512]{2,1,0:T(8,128)(2,1)}, bf16[2,144,512]{2,1,0:T(8,128)(2,1)}, u32[]{:S(2)}, u32[]{:S(2)}) collective-permute-start(bf16[2,144,512]{2,1,0:T(8,128)(2,1)} %collective-permute-done.16.rest_10_), channel_id=1, source_target_pairs={{0,1},{1,2},{2,3},{3,0},{4,5},{5,6},{6,7},{7,4},{8,9},{9,10},{10,1... | collective-permute-start | bytes 884744 | tf_op jit(solution)/shard_map/ppermute | solution.py:496
  69.0 8.0 %collective-permute-start.12 = (bf16[2,144,512]{2,1,0:T(8,128)(2,1)}, bf16[2,144,512]{2,1,0:T(8,128)(2,1)}, u32[]{:S(2)}, u32[]{:S(2)}) collective-permute-start(bf16[2,144,512]{2,1,0:T(8,128)(2,1)} %collective-permute-done.10.rest_2_), channel_id=1, source_target_pairs={{0,4},{1,5},{2,6},{3,7},{4,8},{5,9},{6,10},{7,11},{8,12},{9,13},{1... | collective-permute-start | bytes 884744 | tf_op jit(solution)/shard_map/ppermute | solution.py:496
  89.8 24.0 %all-to-all-start = ((f32[16,64,256]{2,1,0:T(8,128)}), f32[16,64,256]{2,1,0:T(8,128)S(1)}, u32[]{:S(2)}, u32[]{:S(2)}) async-start(f32[16,64,256]{2,1,0:T(8,128)} %get-tuple-element.40), calls=%async_computation | async-start | bytes 2097152 | tf_op jit(solution)/shard_map/all_to_all | solution.py:484
  97.3 10.0 %collective-permute-start.22 = (f32[4,64,256]{2,1,0:T(8,128)S(1)}, f32[4,64,256]{2,1,0:T(8,128)S(1)}, u32[]{:S(2)}, u32[]{:S(2)}) collective-permute-start(f32[4,64,256]{2,1,0:T(8,128)S(1)} %slice.55), channel_id=1, source_target_pairs={{0,16},{16,0},{32,48},{48,32},{64,80},{80,64},{96,112},{112,96},{1... | collective-permute-start | bytes 786440 | tf_op jit(solution)/shard_map/ppermute | solution.py:496
  114.9 22.2 %all-to-all-start.1 = ((bf16[16,128,256]{2,1,0:T(8,128)(2,1)}), bf16[16,128,256]{2,1,0:T(8,128)(2,1)S(1)}, u32[]{:S(2)}, u32[]{:S(2)}) async-start(bf16[16,128,256]{2,1,0:T(8,128)(2,1)} %get-tuple-element.42), calls=%async_computation.1 | async-start | bytes 2097152 | tf_op jit(solution)/shard_map/all_to_all | solution.py:484
  142.2 16.4 %all-to-all-start.2 = ((f32[16,64,256]{2,1,0:T(8,128)}), f32[16,64,256]{2,1,0:T(8,128)S(1)}, u32[]{:S(2)}, u32[]{:S(2)}) async-start(f32[16,64,256]{2,1,0:T(8,128)} %get-tuple-element.44), calls=%async_computation.2 | async-start | bytes 2097152 | tf_op jit(solution)/shard_map/all_to_all | solution.py:484
  161.5 19.0 %all-to-all-start.3 = ((bf16[16,64,256]{2,1,0:T(8,128)(2,1)}), bf16[16,64,256]{2,1,0:T(8,128)(2,1)S(1)}, u32[]{:S(2)}, u32[]{:S(2)}) async-start(bf16[16,64,256]{2,1,0:T(8,128)(2,1)} %get-tuple-element.46), calls=%async_computation.3 | async-start | bytes 1048576 | tf_op jit(solution)/shard_map/all_to_all | solution.py:484
  (26 other events, 145.8 us)
where the time goes:
time: 212 us; the launch traced here: 210 us
  starting transfers between devices  84.2 us (40%)
  waiting for transfers between devices  62.8 us (30%)
  Pallas kernels  31.3 us (15%)
  blocking collectives  22.9 us (11%)
  local copies, waits for them, and re-layouts  5.63 us (3%)
    ppermute x38, waiting for transfers between devices, shift(): return lax.ppermute(x, 'row' if axis in ('x', 'core') else 'col', pairs)  59.4 us
    ppermute x38, starting transfers between devices, shift(): return lax.ppermute(x, 'row' if axis in ('x', 'core') else 'col', pairs)  59.4 us
    all_to_all x4, starting transfers between devices, swap(): return lax.all_to_all(x, axis, 0, 0, tiled=True)  24.8 us
    all_to_all x2, blocking collectives, swap(): return lax.all_to_all(x, axis, 0, 0, tiled=True)  22.9 us
    pallas_call x1, Pallas kernels, build(): call(build_body, [shape(TILE_ROOM, BLOCK, BLOCK, dtype=BF16), shape(N_COL...  12.8 us
    pallas_call x1, Pallas kernels, product(): call(product_body, [shape(N_COL, RANK, BLOCK), shape(N_ROW, RANK + 16, BL...  5.17 us
  transfers between devices with their start and end apart: 42, of which 25 were waited for; matrix products, arithmetic and copies ran while one was open for 1% of the time, Pallas kernels for 1%

commit v1 on v0

--- a/solution.py
+++ b/solution.py
@@ -74,18 +74,23 @@
 
 HALF = BLOCK // 2
 GROUP = 4
+PLACE = 2 * SLOTS + 1
 TILE_ROOM = 288
 
 
-def row_offset(place, j):
-    return ((j ^ place[1]) & 1) * 4 + ((place[0] - j // 2) & 3)
-
-
-def groups_of(count):
-    return (count[0] + GROUP - 1) // GROUP
-
-
-def build_body(pairs, count, place, weight, sums_ref, xc_ref, *rest):
+def count_of(table):
+    return table[2 * SLOTS]
+
+
+def row_offset(table, j):
+    return ((j ^ table[PLACE + 1]) & 1) * 4 + ((table[PLACE] - j // 2) & 3)
+
+
+def groups_of(table):
+    return (count_of(table) + GROUP - 1) // GROUP
+
+
+def build_body(table, weight, sums_ref, xc_ref, *rest):
     first, second = rest[:8], rest[8:16]
     tiles_ref, rows_ref, cols_ref, at_ref, xr_ref, buffer, sems, out_sems = rest[16:]
     copies = []
@@ -106,21 +111,21 @@
                 fetch(b.at[:, HALF:, lanes], xr_ref.at[two, k, 32 * q + 16 : 32 * q + 32])
     rows_ref[...] = jnp.zeros_like(rows_ref)
     cols_ref[...] = jnp.zeros_like(cols_ref)
-    buffer[1] = jnp.zeros((2, BLOCK, BLOCK), BF16)
+    buffer[1] = jnp.zeros((GROUP, BLOCK, BLOCK), BF16)
     for copy in copies:
         copy.wait()
-    twos = (count[0] + 1) // 2
+    groups = groups_of(table)
 
     def indices(slot):
-        i = pairs[2 * slot] % N_COL
-        from_y = (place[2] - i // 4) & 3
-        from_z = (place[3] - i) & 3
-        return i, from_y, from_z, row_offset(place, pairs[2 * slot + 1] // N_COL)
-
-    def products(two, side):
+        i = table[2 * slot] % N_COL
+        from_y = (table[PLACE + 2] - i // 4) & 3
+        from_z = (table[PLACE + 3] - i) & 3
+        return i, from_y, from_z, row_offset(table, table[2 * slot + 1] // N_COL)
+
+    def products(group, side):
         done = []
-        for k in range(2):
-            i, from_y, from_z, from_row = indices(2 * two + k)
+        for k in range(GROUP):
+            i, from_y, from_z, from_row = indices(GROUP * group + k)
             tile = buffer[side, k]
             into_cols = jnp.dot(xr_ref[from_y, from_z], tile, preferred_element_type=F32)
             into_rows = lax.dot_general(
@@ -133,7 +138,7 @@
 
     def tile_of(slot):
         _, from_y, from_z, from_row = indices(slot)
-        live = jnp.where(slot < count[0], TILE_SCALE, 0.0)
+        live = jnp.where(slot < count_of(table), TILE_SCALE, 0.0)
         lead = at_ref[from_y, from_z]
         total = None
         for lag in range(LAGS):
@@ -142,36 +147,36 @@
             total = term if total is None else total + term
         return (total * live).astype(BF16)
 
-    def store(two, side):
+    def store(group, side):
         return pltpu.make_async_copy(
-            buffer.at[side], tiles_ref.at[pl.ds(2 * two, 2)], out_sems.at[side]
+            buffer.at[side], tiles_ref.at[pl.ds(GROUP * group, GROUP)], out_sems.at[side]
         )
 
-    def one(two, carry):
-        side = two & 1
-        products(jnp.maximum(two - 1, 0), 1 - side)
-        here, there = tile_of(2 * two), tile_of(2 * two + 1)
-
-        @pl.when(two >= 2)
+    def one(group, carry):
+        side = group & 1
+        products(jnp.maximum(group - 1, 0), 1 - side)
+        made = [tile_of(GROUP * group + k) for k in range(GROUP)]
+
+        @pl.when(group >= 2)
         def _():
-            store(two - 2, side).wait()
-
-        buffer[side, 0] = here
-        buffer[side, 1] = there
-        store(two, side).start()
+            store(group - 2, side).wait()
+
+        for k in range(GROUP):
+            buffer[side, k] = made[k]
+        store(group, side).start()
         return carry
 
-    lax.fori_loop(0, twos, one, 0)
-    products(twos - 1, (twos - 1) & 1)
-
-    @pl.when(twos >= 2)
+    lax.fori_loop(0, groups, one, 0)
+    products(groups - 1, (groups - 1) & 1)
+
+    @pl.when(groups >= 2)
     def _():
-        store(twos - 2, twos & 1).wait()
-
-    store(twos - 1, (twos - 1) & 1).wait()
-
-
-def build(pairs, count, place, weight, sums, xc, first, second):
+        store(groups - 2, groups & 1).wait()
+
+    store(groups - 1, (groups - 1) & 1).wait()
+
+
+def build(table, weight, sums, xc, first, second):
     return call(
         build_body,
         [
@@ -179,19 +184,19 @@
             shape(N_COL, RANK, BLOCK),
             shape(N_ROW, RANK, BLOCK),
         ],
-        [SMEM] * 4 + [VMEM] * 2 + [ANY] * 16,
+        [SMEM] * 2 + [VMEM] * 2 + [ANY] * 16,
         9_000_000_000,
         20 << 20,
         30,
         scratch=[
             pltpu.VMEM((4, 4, BLOCK, DAYS), BF16),
             pltpu.VMEM((4, 4, RANK, BLOCK), BF16),
-            pltpu.VMEM((2, 2, BLOCK, BLOCK), BF16),
+            pltpu.VMEM((2, GROUP, BLOCK, BLOCK), BF16),
             pltpu.SemaphoreType.DMA((48,)),
             pltpu.SemaphoreType.DMA((2,)),
         ],
         out_specs=[HBM, VMEM, VMEM],
-    )(pairs, count, place, weight, sums, xc, *first, *second)
+    )(table, weight, sums, xc, *first, *second)
 
 
 def total_of(rr_ref, own_ref, parts):
@@ -228,22 +233,12 @@
     return pltpu.make_async_copy(tiles_ref.at[slots], tiles.at[slots], sems.at[group])
 
 
-def load_all(count, tiles_ref, tiles, sems):
+def load_all(table, tiles_ref, tiles, sems):
     def begin(group, carry):
         load(tiles_ref, tiles, sems, group).start()
         return carry
 
-    lax.fori_loop(0, groups_of(count), begin, 0)
-
-
-def arrive(count, tiles_ref, tiles, sems, group):
-    load(tiles_ref, tiles, sems, group).wait()
-
-    def clear(slot, carry):
-        tiles[slot] = jnp.zeros((BLOCK, BLOCK), BF16)
-        return carry
-
-    lax.fori_loop(jnp.maximum(count[0], group * GROUP), group * GROUP + GROUP, clear, 0)
+    lax.fori_loop(0, groups_of(table), begin, 0)
 
 
 TILES = [pltpu.VMEM((SLOTS, BLOCK, BLOCK), BF16), pltpu.SemaphoreType.DMA((SLOTS // GROUP,))]
@@ -254,19 +249,19 @@
     joined_ref[4:] = far_ref[...]
 
 
-def product_body(pairs, count, place, tiles_ref, qr_ref, near_ref, far_ref, rows_ref, cols_ref, qc_ref, tiles, sems):
-    load_all(count, tiles_ref, tiles, sems)
+def product_body(table, tiles_ref, qr_ref, near_ref, far_ref, rows_ref, cols_ref, qc_ref, tiles, sems):
+    load_all(table, tiles_ref, tiles, sems)
     rows_ref[...] = jnp.zeros_like(rows_ref)
     cols_ref[...] = jnp.zeros_like(cols_ref)
     join(near_ref, far_ref, qc_ref)
 
     def some(group, carry):
-        arrive(count, tiles_ref, tiles, sems, group)
+        load(tiles_ref, tiles, sems, group).wait()
         done = []
         for k in range(GROUP):
             slot = group * GROUP + k
-            i = pairs[2 * slot] % N_COL
-            j = row_offset(place, pairs[2 * slot + 1] // N_COL)
+            i = table[2 * slot] % N_COL
+            j = row_offset(table, table[2 * slot + 1] // N_COL)
             tile = tiles[slot]
             into_cols = jnp.dot(qr_ref[i], tile, preferred_element_type=F32)
             into_rows = lax.dot_general(
@@ -278,7 +273,7 @@
             rows_ref[i] += into_rows
         return carry
 
-    lax.fori_loop(0, groups_of(count), some, 0)
+    lax.fori_loop(0, groups_of(table), some, 0)
     gram = jnp.zeros((RANK, RANK), F32)
     for k in range(N_COL):
         both = lax.dot_general(
@@ -293,16 +288,16 @@
             cols_ref[k, RANK:, 64 * q : 64 * q + 64] = gram[16 * q : 16 * q + 16]
 
 
-def product(pairs, count, place, tiles, qr, near, far):
+def product(table, tiles, qr, near, far):
     return call(
         product_body,
         [shape(N_COL, RANK, BLOCK), shape(N_ROW, RANK + 16, BLOCK)],
-        [SMEM] * 3 + [HBM] + [VMEM] * 3,
+        [SMEM] + [HBM] + [VMEM] * 3,
         1_000_000_000,
         8 << 20,
         30,
         scratch=[pltpu.VMEM((N_ROW, 2 * RANK, BLOCK), BF16)] + TILES,
-    )(pairs, count, place, tiles, qr, near, far)
+    )(table, tiles, qr, near, far)
 
 
 PANEL = 8
@@ -400,67 +395,60 @@
 
 
 def project_body(
-    pairs, count, place, tiles_ref, qr_ref, near_ref, far_ref, gram_ref, out_ref, cols_ref, qc_ref, tiles, sems
+    table, tiles_ref, qr_ref, near_ref, far_ref, gram_ref, out_ref, cols_ref, qc_ref, tiles, sems
 ):
-    load_all(count, tiles_ref, tiles, sems)
+    load_all(table, tiles_ref, tiles, sems)
     cols_ref[...] = jnp.zeros_like(cols_ref)
     join(near_ref, far_ref, qc_ref)
 
     def some(group, carry):
-        arrive(count, tiles_ref, tiles, sems, group)
+        load(tiles_ref, tiles, sems, group).wait()
         done = []
         for k in range(GROUP):
             slot = group * GROUP + k
-            i = pairs[2 * slot] % N_COL
-            j = row_offset(place, pairs[2 * slot + 1] // N_COL)
+            i = table[2 * slot] % N_COL
+            j = row_offset(table, table[2 * slot + 1] // N_COL)
             done.append((j, jnp.dot(qr_ref[i], tiles[slot], preferred_element_type=F32)))
         for j, into_cols in done:
             cols_ref[j] += into_cols
         return carry
 
-    lax.fori_loop(0, groups_of(count), some, 0)
+    lax.fori_loop(0, groups_of(table), some, 0)
     form = jnp.zeros((RANK, RANK), F32)
     for k in range(N_ROW):
-        form = form + dot_t(cols_ref[k], qc_ref[k].astype(F32))
+        high = cols_ref[k].astype(BF16)
+        low = (cols_ref[k] - high.astype(F32)).astype(BF16)
+        both = lax.dot_general(
+            jnp.concatenate([high, low], axis=0),
+            qc_ref[k],
+            (((1,), (1,)), ((), ())),
+            preferred_element_type=F32,
+        )
+        form = form + (both[:RANK] + both[RANK:])
     gram = gram_ref[...]
     packed = jnp.where(row_less_col(False), form + form.T, gram)
     diagonal = jnp.sum(jnp.where(eps_eye() > 0.0, gram, 0.0), axis=0, keepdims=True)
     both = jnp.concatenate([packed[: RANK // 2], packed[RANK // 2 :]], axis=1)
     tail = jnp.concatenate([diagonal, jnp.zeros((1, RANK), F32)], axis=1)
-    for k in range(N_ROW):
-        out_ref[k, : RANK // 2] = both
-        out_ref[k, RANK // 2 :] = jnp.broadcast_to(tail, (8, 2 * RANK))
-
-
-def project(pairs, count, place, tiles, qr, near, far, gram):
+    out_ref[: RANK // 2] = both
+    out_ref[RANK // 2 :] = jnp.broadcast_to(tail, (8, 2 * RANK))
+
+
+def project(table, tiles, qr, near, far, gram):
     return call(
         project_body,
-        shape(N_ROW, PACKED, 2 * RANK),
-        [SMEM] * 3 + [HBM] + [VMEM] * 4,
+        shape(PACKED, 2 * RANK),
+        [SMEM] + [HBM] + [VMEM] * 4,
         500_000_000,
         6 << 20,
         30,
         scratch=[pltpu.VMEM((N_ROW, RANK, BLOCK), F32), pltpu.VMEM((N_ROW, RANK, BLOCK), BF16)]
         + TILES,
-    )(pairs, count, place, tiles, qr, near, far, gram)
-
-
-def respread_body(parts_ref, out_ref):
-    total = parts_ref[0]
-    for k in range(1, N_ROW):
-        total = total + parts_ref[k]
-    for k in range(N_COL):
-        out_ref[k] = total
-
-
-def respread(parts):
-    return call(respread_body, shape(N_COL, PACKED, 2 * RANK), [VMEM], 100_000, 1 << 19, 4)(parts)
-
-
-def finish_body(parts_ref, p_ref, basis_ref, form_ref):
-    total = parts_ref[0]
-    for k in range(1, N_COL):
-        total = total + parts_ref[k]
+    )(table, tiles, qr, near, far, gram)
+
+
+def finish_body(own_ref, a_ref, b_ref, c_ref, p_ref, basis_ref, form_ref):
+    total = sum_of_four(own_ref[...], a_ref[...], b_ref[...], c_ref[...])
     top = total[: RANK // 2]
     packed = jnp.concatenate([top[:, :RANK], top[:, RANK:]], axis=0)
     lower = jnp.where(row_less_col(False), 0.0, packed)
@@ -474,10 +462,14 @@
     )
 
 
+def sum_of_four(own, one, two, three):
+    return (own + two) + (one + three)
+
+
 def finish(parts, p):
     return call(
-        finish_body, [shape(RANK, BLOCK), shape(RANK, RANK)], [VMEM, VMEM], 10_000_000, 1 << 20, 6
-    )(parts, p)
+        finish_body, [shape(RANK, BLOCK), shape(RANK, RANK)], [VMEM] * 5, 10_000_000, 1 << 20, 6
+    )(*parts, p)
 
 
 def swap(x, axis):
@@ -522,10 +514,9 @@
 
 
 def local(series, lag_weight, start_basis, block_pairs, pair_count):
-    pairs = block_pairs.reshape(2 * SLOTS)
-    count = pair_count.reshape(1)
     row, col = lax.axis_index("row"), lax.axis_index("col")
     place = jnp.stack([row // 2, row % 2, col // 4, col % 4]).astype(jnp.int32)
+    table = jnp.concatenate([block_pairs.reshape(2 * SLOTS), pair_count.reshape(1), place])
     lead = series.T
     packed = jnp.concatenate([start_basis[:32], start_basis[32:]], axis=1)
     first = jnp.concatenate([lead[:HALF], packed[:16]], axis=0)
@@ -539,12 +530,15 @@
     own = jnp.stack(trail)
     other = shift(own, "core", 1)
     sums, xc = day_sums(own, other)
-    tiles, rows, cols = build(pairs, count, place, lag_weight, sums, xc, first, second)
+    tiles, rows, cols = build(table, lag_weight, sums, xc, first, second)
     q1, wide = mid1(*scatter(rows, cols))
-    rows, cols = product(pairs, count, place, tiles, *gather(q1, wide))
+    rows, cols = product(table, tiles, *gather(q1, wide))
     p2, q2, wide, gram = mid2(*scatter(rows, cols))
-    part = project(pairs, count, place, tiles, *gather(q2, wide), gram)
-    return finish(swap(respread(swap(part, "row")), "col"), p2)
+    part = project(table, tiles, *gather(q2, wide), gram)
+    part = part + shift(part, "core", 1)
+    part = sum_of_four(*around(part, "x"))
+    part = sum_of_four(*around(part, "z"))
+    return finish(around(part, "y"), p2)
 
 
 def solution(mesh):

time: 212 us -> 210 us (level)
  the two profiles are of different devices: /device:TPU:1 before, /device:TPU:0 now
where the time goes in v1:
time: 210 us; the launch traced here: 209 us
  waiting for transfers between devices  88.2 us (42%)
  starting transfers between devices  73.9 us (35%)
  Pallas kernels  37.5 us (18%)
  local copies, waits for them, and re-layouts  6.23 us (3%)
    ppermute x48, waiting for transfers between devices, shift(): return lax.ppermute(x, 'row' if axis in ('x', 'core') else 'col', pairs)  74.7 us
    ppermute x48, starting transfers between devices, shift(): return lax.ppermute(x, 'row' if axis in ('x', 'core') else 'col', pairs)  59.1 us
    pallas_call x1, Pallas kernels, build(): call(build_body, [shape(TILE_ROOM, BLOCK, BLOCK, dtype=BF16), shape(N_COL...  17.5 us
    all_to_all x4, starting transfers between devices, swap(): return lax.all_to_all(x, axis, 0, 0, tiled=True)  14.7 us
    all_to_all x4, waiting for transfers between devices, swap(): return lax.all_to_all(x, axis, 0, 0, tiled=True)  13.5 us
    pallas_call x1, Pallas kernels, product(): call(product_body, [shape(N_COL, RANK, BLOCK), shape(N_ROW, RANK + 16, BL...  6.36 us
  transfers between devices with their start and end apart: 52, of which 35 were waited for; matrix products, arithmetic and copies ran while one was open for 1% of the time, Pallas kernels for 1%

profile of v1, /device:TPU:0, one launch (start us, length us, event | category | flops | bytes accessed | tf_op | source)
XLA Modules:
  0.0 208.9 jit_solution(8509485431921120795)
XLA Ops:
  8.2 10.9 %collective-permute-done.2 = bf16[576,256]{1,0:T(8,128)(2,1)S(1)} collective-permute-done((bf16[576,256]{1,0:T(8,128)(2,1)S(1)}, bf16[576,256]{1,0:T(8,128)(2,1)S(1)}, u32[]{:S(2)}, u32[]{:S(2)}) %collective-permute-start.2) | collective-permute-done | bytes 294944 | tf_op jit(solution)/shard_map/ppermute | solution.py:488
  19.1 3.7 %collective-permute-done = bf16[576,256]{1,0:T(8,128)(2,1)S(1)} collective-permute-done((bf16[576,256]{1,0:T(8,128)(2,1)S(1)}, bf16[576,256]{1,0:T(8,128)(2,1)S(1)}, u32[]{:S(2)}, u32[]{:S(2)}) %collective-permute-start) | collective-permute-done | bytes 294944 | tf_op jit(solution)/shard_map/ppermute | solution.py:488
  23.0 4.1 %collective-permute-start.6 = (bf16[144,512]{1,0:T(8,128)(2,1)S(1)}, bf16[144,512]{1,0:T(8,128)(2,1)S(1)}, u32[]{:S(2)}, u32[]{:S(2)}) collective-permute-start(bf16[144,512]{1,0:T(8,128)(2,1)S(1)} %get-tuple-element.31), channel_id=1, source_target_pairs={{0,3},{1,0},{2,1},{3,2},{4,7},{5,4},{6,5},{7,6},{8,11},{9,8},{10,9... | collective-permute-start | bytes 442376 | tf_op jit(solution)/shard_map/ppermute | solution.py:488
  37.9 4.3 %collective-permute-done.8 = bf16[144,512]{1,0:T(8,128)(2,1)S(1)} collective-permute-done((bf16[144,512]{1,0:T(8,128)(2,1)S(1)}, bf16[144,512]{1,0:T(8,128)(2,1)S(1)}, u32[]{:S(2)}, u32[]{:S(2)}) %collective-permute-start.8) | collective-permute-done | bytes 147488 | tf_op jit(solution)/shard_map/ppermute | solution.py:488
  44.4 3.8 %collective-permute-start.19 = (bf16[2,144,512]{2,1,0:T(8,128)(2,1)S(1)}, bf16[2,144,512]{2,1,0:T(8,128)(2,1)}, u32[]{:S(2)}, u32[]{:S(2)}) collective-permute-start(bf16[2,144,512]{2,1,0:T(8,128)(2,1)S(1)} %pad_maximum_fusion.5.rest_9_), channel_id=1, source_target_pairs={{0,3},{1,0},{2,1},{3,2},{4,7},{5,4},{6,5},{7,6},{8,11},{9,8},{10,9... | collective-permute-start | bytes 884744 | tf_op jit(solution)/shard_map/ppermute | solution.py:488
  48.2 3.3 %collective-permute-start.21 = (bf16[2,144,512]{2,1,0:T(8,128)(2,1)S(1)}, bf16[2,144,512]{2,1,0:T(8,128)(2,1)S(1)}, u32[]{:S(2)}, u32[]{:S(2)}) collective-permute-start(bf16[2,144,512]{2,1,0:T(8,128)(2,1)S(1)} %pad_maximum_fusion.4.rest_8_), channel_id=1, source_target_pairs={{0,3},{1,0},{2,1},{3,2},{4,7},{5,4},{6,5},{7,6},{8,11},{9,8},{10,9... | collective-permute-start | bytes 884744 | tf_op jit(solution)/shard_map/ppermute | solution.py:488
  51.6 4.0 %collective-permute-done.19.rest_15_ = bf16[2,144,512]{2,1,0:T(8,128)(2,1)} collective-permute-done((bf16[2,144,512]{2,1,0:T(8,128)(2,1)S(1)}, bf16[2,144,512]{2,1,0:T(8,128)(2,1)}, u32[]{:S(2)}, u32[]{:S(2)}) %collective-permute-start.19) | collective-permute-done | bytes 294944 | tf_op jit(solution)/shard_map/ppermute | solution.py:488
  55.8 3.5 %collective-permute-done.17.rest_11_ = bf16[2,144,512]{2,1,0:T(8,128)(2,1)S(1)} collective-permute-done((bf16[2,144,512]{2,1,0:T(8,128)(2,1)S(1)}, bf16[2,144,512]{2,1,0:T(8,128)(2,1)S(1)}, u32[]{:S(2)}, u32[]{:S(2)}) %collective-permute-start.17) | collective-permute-done | bytes 294944 | tf_op jit(solution)/shard_map/ppermute | solution.py:488
  81.6 17.5 %shard_map.69 = (bf16[288,256,256]{2,1,0:T(8,128)(2,1)}, f32[16,64,256]{2,1,0:T(8,128)}, f32[8,64,256]{2,1,0:T(8,128)S(1)}) custom-call(s32[69]{0:T(128)S(1)} %concatenate.15.table, f32[4]{0:T(128)S(1)} %copy-done.6, bf16[8,4,512,256]{3,2,1,0:T(8,128)(2,1)S(1)} %get-tuple-element.27.sums_ref, bf16[8,64,256]{2,1,0:T(8,128)(2,1)S(1)} %get-tuple-element.28.xc_ref, ...), custom_call_target="tpu_custom_call" | custom-call | flops 8999999488 | bytes 20971520 | tf_op jit(solution)/shard_map/pallas_call | solution.py:180
  99.2 3.8 %all-to-all-start = ((f32[16,64,256]{2,1,0:T(8,128)}), f32[16,64,256]{2,1,0:T(8,128)S(1)}, u32[]{:S(2)}, u32[]{:S(2)}) async-start(f32[16,64,256]{2,1,0:T(8,128)} %get-tuple-element.40), calls=%async_computation | async-start | bytes 2097152 | tf_op jit(solution)/shard_map/all_to_all | solution.py:476
  108.0 3.5 %collective-permute-done.25.c_ref = f32[1,64,256]{2,1,0:T(8,128)S(1)} collective-permute-done((f32[1,64,256]{2,1,0:T(8,128)S(1)}, f32[1,64,256]{2,1,0:T(8,128)S(1)}, u32[]{:S(2)}, u32[]{:S(2)}) %collective-permute-start.25) | collective-permute-done | bytes 65568 | tf_op jit(solution)/shard_map/ppermute | solution.py:488
  112.1 3.8 %all-to-all-done.rr_ref = f32[16,64,256]{2,1,0:T(8,128)S(1)} async-done(((f32[16,64,256]{2,1,0:T(8,128)}), f32[16,64,256]{2,1,0:T(8,128)S(1)}, u32[]{:S(2)}, u32[]{:S(2)}) %all-to-all-start) | async-done | bytes 1048608 | tf_op jit(solution)/shard_map/all_to_all | solution.py:476
  117.0 3.7 %all-to-all-start.1 = ((bf16[16,128,256]{2,1,0:T(8,128)(2,1)}), bf16[16,128,256]{2,1,0:T(8,128)(2,1)S(1)}, u32[]{:S(2)}, u32[]{:S(2)}) async-start(bf16[16,128,256]{2,1,0:T(8,128)(2,1)} %get-tuple-element.42), calls=%async_computation.1 | async-start | bytes 2097152 | tf_op jit(solution)/shard_map/all_to_all | solution.py:476
  125.3 3.3 %collective-permute-done.27 = bf16[128,256]{1,0:T(8,128)(2,1)S(1)} collective-permute-done((bf16[128,256]{1,0:T(8,128)(2,1)S(1)}, bf16[128,256]{1,0:T(8,128)(2,1)S(1)}, u32[]{:S(2)}, u32[]{:S(2)}) %collective-permute-start.27) | collective-permute-done | bytes 65568 | tf_op jit(solution)/shard_map/ppermute | solution.py:488
  131.0 5.8 %all-to-all-done.1.qr_ref = bf16[16,128,256]{2,1,0:T(8,128)(2,1)S(1)} async-done(((bf16[16,128,256]{2,1,0:T(8,128)(2,1)}), bf16[16,128,256]{2,1,0:T(8,128)(2,1)S(1)}, u32[]{:S(2)}, u32[]{:S(2)}) %all-to-all-start.1) | async-done | bytes 1048608 | tf_op jit(solution)/shard_map/all_to_all | solution.py:476
  136.8 6.4 %shard_map.71 = (f32[16,64,256]{2,1,0:T(8,128)}, f32[8,80,256]{2,1,0:T(8,128)S(1)}) custom-call(s32[69]{0:T(128)S(1)} %concatenate.15.table, bf16[288,256,256]{2,1,0:T(8,128)(2,1)} %get-tuple-element.39.tiles_ref, bf16[16,128,256]{2,1,0:T(8,128)(2,1)S(1)} %all-to-all-done.1.qr_ref, bf16[4,128,256]{2,1,0:T(8,128)(2,1)S(1)} %pad_maximum_fusion.6.near_ref, ...), custom_call_target="tpu_custom_call" | custom-call | flops 1000000000 | bytes 8388608 | tf_op jit(solution)/shard_map/pallas_call | solution.py:292
  143.1 3.7 %all-to-all-start.2 = ((f32[16,64,256]{2,1,0:T(8,128)}), f32[16,64,256]{2,1,0:T(8,128)S(1)}, u32[]{:S(2)}, u32[]{:S(2)}) async-start(f32[16,64,256]{2,1,0:T(8,128)} %get-tuple-element.44), calls=%async_computation.2 | async-start | bytes 2097152 | tf_op jit(solution)/shard_map/all_to_all | solution.py:476
  151.9 4.2 %collective-permute-done.33.c_ref = f32[1,80,256]{2,1,0:T(8,128)S(1)} collective-permute-done((f32[1,80,256]{2,1,0:T(8,128)S(1)}, f32[1,80,256]{2,1,0:T(8,128)S(1)}, u32[]{:S(2)}, u32[]{:S(2)}) %collective-permute-start.33) | collective-permute-done | bytes 81952 | tf_op jit(solution)/shard_map/ppermute | solution.py:488
  156.7 3.9 %all-to-all-done.2.rr_ref = f32[16,64,256]{2,1,0:T(8,128)S(1)} async-done(((f32[16,64,256]{2,1,0:T(8,128)}), f32[16,64,256]{2,1,0:T(8,128)S(1)}, u32[]{:S(2)}, u32[]{:S(2)}) %all-to-all-start.2) | async-done | bytes 1048608 | tf_op jit(solution)/shard_map/all_to_all | solution.py:476
  163.5 3.6 %all-to-all-start.3 = ((bf16[16,64,256]{2,1,0:T(8,128)(2,1)}), bf16[16,64,256]{2,1,0:T(8,128)(2,1)S(1)}, u32[]{:S(2)}, u32[]{:S(2)}) async-start(bf16[16,64,256]{2,1,0:T(8,128)(2,1)} %get-tuple-element.46), calls=%async_computation.3 | async-start | bytes 1048576 | tf_op jit(solution)/shard_map/all_to_all | solution.py:476
  167.1 3.6 %collective-permute-start.36 = (bf16[64,256]{1,0:T(8,128)(2,1)S(1)}, bf16[64,256]{1,0:T(8,128)(2,1)S(1)}, u32[]{:S(2)}, u32[]{:S(2)}) collective-permute-start(bf16[64,256]{1,0:T(8,128)(2,1)S(1)} %get-tuple-element.47), channel_id=1, source_target_pairs={{0,96},{16,112},{32,0},{48,16},{64,32},{80,48},{96,64},{112,80},{1... | collective-permute-start | bytes 98312 | tf_op jit(solution)/shard_map/ppermute | solution.py:488
  172.3 3.9 %collective-permute-done.35 = bf16[64,256]{1,0:T(8,128)(2,1)S(1)} collective-permute-done((bf16[64,256]{1,0:T(8,128)(2,1)S(1)}, bf16[64,256]{1,0:T(8,128)(2,1)S(1)}, u32[]{:S(2)}, u32[]{:S(2)}) %collective-permute-start.35) | collective-permute-done | bytes 32800 | tf_op jit(solution)/shard_map/ppermute | solution.py:488
  177.6 4.0 %shard_map.73 = f32[40,128]{1,0:T(8,128)S(1)} custom-call(s32[69]{0:T(128)S(1)} %concatenate.15.table, bf16[288,256,256]{2,1,0:T(8,128)(2,1)} %get-tuple-element.39.tiles_ref, bf16[16,64,256]{2,1,0:T(8,128)(2,1)S(1)} %all-to-all-done.3.qr_ref, bf16[4,64,256]{2,1,0:T(8,128)(2,1)S(1)} %pad_maximum_fusion.8.near_ref, ...), custom_call_target="tpu_custom_call" | custom-call | flops 500000000 | bytes 6291456 | tf_op jit(solution)/shard_map/pallas_call | solution.py:438
  202.2 3.3 %collective-permute-done.46.b_ref = f32[40,128]{1,0:T(8,128)S(1)} collective-permute-done((f32[40,128]{1,0:T(8,128)S(1)}, f32[40,128]{1,0:T(8,128)S(1)}, u32[]{:S(2)}, u32[]{:S(2)}) %collective-permute-start.46) | collective-permute-done | bytes 20512 | tf_op jit(solution)/shard_map/ppermute | solution.py:488
  (126 shorter events, 91.9 us)
Async XLA Ops:
  3.5 15.5 %collective-permute-start.2 = (bf16[576,256]{1,0:T(8,128)(2,1)S(1)}, bf16[576,256]{1,0:T(8,128)(2,1)S(1)}, u32[]{:S(2)}, u32[]{:S(2)}) collective-permute-start(bf16[576,256]{1,0:T(8,128)(2,1)S(1)} %pad_maximum_fusion.1), channel_id=1, source_target_pairs={{0,96},{16,112},{32,0},{48,16},{64,32},{80,48},{96,64},{112,80},{1... | collective-permute-start | bytes 884744 | tf_op jit(solution)/shard_map/ppermute | solution.py:488
  6.5 12.6 %collective-permute-start.1 = (bf16[576,256]{1,0:T(8,128)(2,1)S(1)}, bf16[576,256]{1,0:T(8,128)(2,1)S(1)}, u32[]{:S(2)}, u32[]{:S(2)}) collective-permute-start(bf16[576,256]{1,0:T(8,128)(2,1)S(1)} %pad_maximum_fusion.1), channel_id=1, source_target_pairs={{0,64},{16,80},{32,96},{48,112},{64,0},{80,16},{96,32},{112,48},{1... | collective-permute-start | bytes 884744 | tf_op jit(solution)/shard_map/ppermute | solution.py:488
  7.3 15.5 %collective-permute-start = (bf16[576,256]{1,0:T(8,128)(2,1)S(1)}, bf16[576,256]{1,0:T(8,128)(2,1)S(1)}, u32[]{:S(2)}, u32[]{:S(2)}) collective-permute-start(bf16[576,256]{1,0:T(8,128)(2,1)S(1)} %pad_maximum_fusion.1), channel_id=1, source_target_pairs={{0,32},{16,48},{32,64},{48,80},{64,96},{80,112},{96,0},{112,16},{1... | collective-permute-start | bytes 884744 | tf_op jit(solution)/shard_map/ppermute | solution.py:488
  22.9 50.5 %collective-permute-start.3 = (bf16[4,576,256]{2,1,0:T(8,128)(2,1)S(1)}, bf16[4,576,256]{2,1,0:T(8,128)(2,1)S(1)}, u32[]{:S(2)}, u32[]{:S(2)}) collective-permute-start(bf16[4,576,256]{2,1,0:T(8,128)(2,1)S(1)} %pad_maximum_fusion.own_ref), channel_id=1, source_target_pairs={{0,16},{16,0},{32,48},{48,32},{64,80},{80,64},{96,112},{112,96},{1... | collective-permute-start | bytes 3538952 | tf_op jit(solution)/shard_map/ppermute | solution.py:488
  23.0 11.0 %collective-permute-start.6 = (bf16[144,512]{1,0:T(8,128)(2,1)S(1)}, bf16[144,512]{1,0:T(8,128)(2,1)S(1)}, u32[]{:S(2)}, u32[]{:S(2)}) collective-permute-start(bf16[144,512]{1,0:T(8,128)(2,1)S(1)} %get-tuple-element.31), channel_id=1, source_target_pairs={{0,3},{1,0},{2,1},{3,2},{4,7},{5,4},{6,5},{7,6},{8,11},{9,8},{10,9... | collective-permute-start | bytes 442376 | tf_op jit(solution)/shard_map/ppermute | solution.py:488
  27.1 10.1 %collective-permute-start.5 = (bf16[144,512]{1,0:T(8,128)(2,1)S(1)}, bf16[144,512]{1,0:T(8,128)(2,1)S(1)}, u32[]{:S(2)}, u32[]{:S(2)}) collective-permute-start(bf16[144,512]{1,0:T(8,128)(2,1)S(1)} %get-tuple-element.31), channel_id=1, source_target_pairs={{0,2},{1,3},{2,0},{3,1},{4,6},{5,7},{6,4},{7,5},{8,10},{9,11},{10,... | collective-permute-start | bytes 442376 | tf_op jit(solution)/shard_map/ppermute | solution.py:488
  27.1 10.7 %collective-permute-start.4 = (bf16[144,512]{1,0:T(8,128)(2,1)S(1)}, bf16[144,512]{1,0:T(8,128)(2,1)S(1)}, u32[]{:S(2)}, u32[]{:S(2)}) collective-permute-start(bf16[144,512]{1,0:T(8,128)(2,1)S(1)} %get-tuple-element.31), channel_id=1, source_target_pairs={{0,1},{1,2},{2,3},{3,0},{4,5},{5,6},{6,7},{7,4},{8,9},{9,10},{10,1... | collective-permute-start | bytes 442376 | tf_op jit(solution)/shard_map/ppermute | solution.py:488
  28.4 9.5 %collective-permute-start.9 = (bf16[144,512]{1,0:T(8,128)(2,1)S(1)}, bf16[144,512]{1,0:T(8,128)(2,1)S(1)}, u32[]{:S(2)}, u32[]{:S(2)}) collective-permute-start(bf16[144,512]{1,0:T(8,128)(2,1)S(1)} %get-tuple-element.35), channel_id=1, source_target_pairs={{0,12},{1,13},{2,14},{3,15},{4,0},{5,1},{6,2},{7,3},{8,4},{9,5},{1... | collective-permute-start | bytes 442376 | tf_op jit(solution)/shard_map/ppermute | solution.py:488
  34.0 8.1 %collective-permute-start.8 = (bf16[144,512]{1,0:T(8,128)(2,1)S(1)}, bf16[144,512]{1,0:T(8,128)(2,1)S(1)}, u32[]{:S(2)}, u32[]{:S(2)}) collective-permute-start(bf16[144,512]{1,0:T(8,128)(2,1)S(1)} %get-tuple-element.35), channel_id=1, source_target_pairs={{0,8},{1,9},{2,10},{3,11},{4,12},{5,13},{6,14},{7,15},{8,0},{9,1},... | collective-permute-start | bytes 442376 | tf_op jit(solution)/shard_map/ppermute | solution.py:488
  44.4 11.2 %collective-permute-start.19 = (bf16[2,144,512]{2,1,0:T(8,128)(2,1)S(1)}, bf16[2,144,512]{2,1,0:T(8,128)(2,1)}, u32[]{:S(2)}, u32[]{:S(2)}) collective-permute-start(bf16[2,144,512]{2,1,0:T(8,128)(2,1)S(1)} %pad_maximum_fusion.5.rest_9_), channel_id=1, source_target_pairs={{0,3},{1,0},{2,1},{3,2},{4,7},{5,4},{6,5},{7,6},{8,11},{9,8},{10,9... | collective-permute-start | bytes 884744 | tf_op jit(solution)/shard_map/ppermute | solution.py:488
  48.2 11.1 %collective-permute-start.17 = (bf16[2,144,512]{2,1,0:T(8,128)(2,1)S(1)}, bf16[2,144,512]{2,1,0:T(8,128)(2,1)S(1)}, u32[]{:S(2)}, u32[]{:S(2)}) collective-permute-start(bf16[2,144,512]{2,1,0:T(8,128)(2,1)S(1)} %pad_maximum_fusion.5.rest_9_), channel_id=1, source_target_pairs={{0,1},{1,2},{2,3},{3,0},{4,5},{5,6},{6,7},{7,4},{8,9},{9,10},{10,1... | collective-permute-start | bytes 884744 | tf_op jit(solution)/shard_map/ppermute | solution.py:488
  48.2 13.1 %collective-permute-start.21 = (bf16[2,144,512]{2,1,0:T(8,128)(2,1)S(1)}, bf16[2,144,512]{2,1,0:T(8,128)(2,1)S(1)}, u32[]{:S(2)}, u32[]{:S(2)}) collective-permute-start(bf16[2,144,512]{2,1,0:T(8,128)(2,1)S(1)} %pad_maximum_fusion.4.rest_8_), channel_id=1, source_target_pairs={{0,3},{1,0},{2,1},{3,2},{4,7},{5,4},{6,5},{7,6},{8,11},{9,8},{10,9... | collective-permute-start | bytes 884744 | tf_op jit(solution)/shard_map/ppermute | solution.py:488
  51.5 12.2 %collective-permute-start.16 = (bf16[2,144,512]{2,1,0:T(8,128)(2,1)S(1)}, bf16[2,144,512]{2,1,0:T(8,128)(2,1)}, u32[]{:S(2)}, u32[]{:S(2)}) collective-permute-start(bf16[2,144,512]{2,1,0:T(8,128)(2,1)S(1)} %pad_maximum_fusion.4.rest_8_), channel_id=1, source_target_pairs={{0,1},{1,2},{2,3},{3,0},{4,5},{5,6},{6,7},{7,4},{8,9},{9,10},{10,1... | collective-permute-start | bytes 884744 | tf_op jit(solution)/shard_map/ppermute | solution.py:488
  55.6 9.8 %collective-permute-start.13 = (bf16[2,144,512]{2,1,0:T(8,128)(2,1)S(1)}, bf16[2,144,512]{2,1,0:T(8,128)(2,1)}, u32[]{:S(2)}, u32[]{:S(2)}) collective-permute-start(bf16[2,144,512]{2,1,0:T(8,128)(2,1)S(1)} %pad_maximum_fusion.3.rest_1_), channel_id=1, source_target_pairs={{0,12},{1,13},{2,14},{3,15},{4,0},{5,1},{6,2},{7,3},{8,4},{9,5},{1... | collective-permute-start | bytes 884744 | tf_op jit(solution)/shard_map/ppermute | solution.py:488
  60.0 9.5 %collective-permute-start.11 = (bf16[2,144,512]{2,1,0:T(8,128)(2,1)S(1)}, bf16[2,144,512]{2,1,0:T(8,128)(2,1)S(1)}, u32[]{:S(2)}, u32[]{:S(2)}) collective-permute-start(bf16[2,144,512]{2,1,0:T(8,128)(2,1)S(1)} %pad_maximum_fusion.3.rest_1_), channel_id=1, source_target_pairs={{0,4},{1,5},{2,6},{3,7},{4,8},{5,9},{6,10},{7,11},{8,12},{9,13},{1... | collective-permute-start | bytes 884744 | tf_op jit(solution)/shard_map/ppermute | solution.py:488
  62.1 11.3 %collective-permute-start.10 = (bf16[2,144,512]{2,1,0:T(8,128)(2,1)S(1)}, bf16[2,144,512]{2,1,0:T(8,128)(2,1)}, u32[]{:S(2)}, u32[]{:S(2)}) collective-permute-start(bf16[2,144,512]{2,1,0:T(8,128)(2,1)S(1)} %pad_maximum_fusion.2.rest_0_), channel_id=1, source_target_pairs={{0,4},{1,5},{2,6},{3,7},{4,8},{5,9},{6,10},{7,11},{8,12},{9,13},{1... | collective-permute-start | bytes 884744 | tf_op jit(solution)/shard_map/ppermute | solution.py:488
  63.8 17.2 %collective-permute-start.15 = (bf16[2,144,512]{2,1,0:T(8,128)(2,1)S(1)}, bf16[2,144,512]{2,1,0:T(8,128)(2,1)}, u32[]{:S(2)}, u32[]{:S(2)}) collective-permute-start(bf16[2,144,512]{2,1,0:T(8,128)(2,1)S(1)} %pad_maximum_fusion.2.rest_0_), channel_id=1, source_target_pairs={{0,12},{1,13},{2,14},{3,15},{4,0},{5,1},{6,2},{7,3},{8,4},{9,5},{1... | collective-permute-start | bytes 884744 | tf_op jit(solution)/shard_map/ppermute | solution.py:488
  65.3 15.6 %collective-permute-start.20 = (bf16[2,144,512]{2,1,0:T(8,128)(2,1)}, bf16[2,144,512]{2,1,0:T(8,128)(2,1)}, u32[]{:S(2)}, u32[]{:S(2)}) collective-permute-start(bf16[2,144,512]{2,1,0:T(8,128)(2,1)} %collective-permute-done.19.rest_15_), channel_id=1, source_target_pairs={{0,3},{1,0},{2,1},{3,2},{4,7},{5,4},{6,5},{7,6},{8,11},{9,8},{10,9... | collective-permute-start | bytes 884744 | tf_op jit(solution)/shard_map/ppermute | solution.py:488
  70.3 10.7 %collective-permute-start.18 = (bf16[2,144,512]{2,1,0:T(8,128)(2,1)}, bf16[2,144,512]{2,1,0:T(8,128)(2,1)}, u32[]{:S(2)}, u32[]{:S(2)}) collective-permute-start(bf16[2,144,512]{2,1,0:T(8,128)(2,1)} %collective-permute-done.16.rest_10_), channel_id=1, source_target_pairs={{0,1},{1,2},{2,3},{3,0},{4,5},{5,6},{6,7},{7,4},{8,9},{9,10},{10,1... | collective-permute-start | bytes 884744 | tf_op jit(solution)/shard_map/ppermute | solution.py:488
  73.4 8.3 %collective-permute-start.12 = (bf16[2,144,512]{2,1,0:T(8,128)(2,1)}, bf16[2,144,512]{2,1,0:T(8,128)(2,1)}, u32[]{:S(2)}, u32[]{:S(2)}) collective-permute-start(bf16[2,144,512]{2,1,0:T(8,128)(2,1)} %collective-permute-done.10.rest_2_), channel_id=1, source_target_pairs={{0,4},{1,5},{2,6},{3,7},{4,8},{5,9},{6,10},{7,11},{8,12},{9,13},{1... | collective-permute-start | bytes 884744 | tf_op jit(solution)/shard_map/ppermute | solution.py:488
  99.2 16.7 %all-to-all-start = ((f32[16,64,256]{2,1,0:T(8,128)}), f32[16,64,256]{2,1,0:T(8,128)S(1)}, u32[]{:S(2)}, u32[]{:S(2)}) async-start(f32[16,64,256]{2,1,0:T(8,128)} %get-tuple-element.40), calls=%async_computation | async-start | bytes 2097152 | tf_op jit(solution)/shard_map/all_to_all | solution.py:476
  117.0 19.8 %all-to-all-start.1 = ((bf16[16,128,256]{2,1,0:T(8,128)(2,1)}), bf16[16,128,256]{2,1,0:T(8,128)(2,1)S(1)}, u32[]{:S(2)}, u32[]{:S(2)}) async-start(bf16[16,128,256]{2,1,0:T(8,128)(2,1)} %get-tuple-element.42), calls=%async_computation.1 | async-start | bytes 2097152 | tf_op jit(solution)/shard_map/all_to_all | solution.py:476
  143.1 17.5 %all-to-all-start.2 = ((f32[16,64,256]{2,1,0:T(8,128)}), f32[16,64,256]{2,1,0:T(8,128)S(1)}, u32[]{:S(2)}, u32[]{:S(2)}) async-start(f32[16,64,256]{2,1,0:T(8,128)} %get-tuple-element.44), calls=%async_computation.2 | async-start | bytes 2097152 | tf_op jit(solution)/shard_map/all_to_all | solution.py:476
  163.5 14.1 %all-to-all-start.3 = ((bf16[16,64,256]{2,1,0:T(8,128)(2,1)}), bf16[16,64,256]{2,1,0:T(8,128)(2,1)S(1)}, u32[]{:S(2)}, u32[]{:S(2)}) async-start(bf16[16,64,256]{2,1,0:T(8,128)(2,1)} %get-tuple-element.46), calls=%async_computation.3 | async-start | bytes 1048576 | tf_op jit(solution)/shard_map/all_to_all | solution.py:476
  (35 other events, 156.1 us)

commit v2 on v1

--- a/solution.py
+++ b/solution.py
@@ -92,7 +92,7 @@
 
 def build_body(table, weight, sums_ref, xc_ref, *rest):
     first, second = rest[:8], rest[8:16]
-    tiles_ref, rows_ref, cols_ref, at_ref, xr_ref, buffer, sems, out_sems = rest[16:]
+    tiles_ref, rows_ref, cols_ref, at_ref, buffer, sems, out_sems = rest[16:]
     copies = []
 
     def fetch(src, dst):
@@ -103,12 +103,8 @@
         for h in range(2):
             two = slice(2 * h, 2 * h + 2)
             a, b = first[2 * k + h], second[2 * k + h]
-            fetch(a.at[:, :HALF], at_ref.at[k, two, :HALF])
-            fetch(b.at[:, :HALF], at_ref.at[two, k, HALF:])
-            for q in range(2):
-                lanes = slice(BLOCK * q, BLOCK * q + BLOCK)
-                fetch(a.at[:, HALF:, lanes], xr_ref.at[k, two, 32 * q : 32 * q + 16])
-                fetch(b.at[:, HALF:, lanes], xr_ref.at[two, k, 32 * q + 16 : 32 * q + 32])
+            fetch(a, at_ref.at[k, two, : HALF + 16])
+            fetch(b, at_ref.at[two, k, HALF + 16 :])
     rows_ref[...] = jnp.zeros_like(rows_ref)
     cols_ref[...] = jnp.zeros_like(cols_ref)
     buffer[1] = jnp.zeros((GROUP, BLOCK, BLOCK), BF16)
@@ -122,12 +118,16 @@
         from_z = (table[PLACE + 3] - i) & 3
         return i, from_y, from_z, row_offset(table, table[2 * slot + 1] // N_COL)
 
+    def basis_of(from_y, from_z):
+        ends = [at_ref[from_y, from_z, :16], at_ref[from_y, from_z, 16 + BLOCK :]]
+        return jnp.concatenate([e[:, BLOCK * q : BLOCK * q + BLOCK] for q in range(2) for e in ends], axis=0)
+
     def products(group, side):
         done = []
         for k in range(GROUP):
             i, from_y, from_z, from_row = indices(GROUP * group + k)
             tile = buffer[side, k]
-            into_cols = jnp.dot(xr_ref[from_y, from_z], tile, preferred_element_type=F32)
+            into_cols = jnp.dot(basis_of(from_y, from_z), tile, preferred_element_type=F32)
             into_rows = lax.dot_general(
                 xc_ref[from_row], tile, (((1,), (1,)), ((), ())), preferred_element_type=F32
             )
@@ -139,7 +139,7 @@
     def tile_of(slot):
         _, from_y, from_z, from_row = indices(slot)
         live = jnp.where(slot < count_of(table), TILE_SCALE, 0.0)
-        lead = at_ref[from_y, from_z]
+        lead = at_ref[from_y, from_z, 16 : 16 + BLOCK]
         total = None
         for lag in range(LAGS):
             lagged = jnp.dot(lead, sums_ref[from_row, lag], preferred_element_type=F32)
@@ -189,10 +189,9 @@
         20 << 20,
         30,
         scratch=[
-            pltpu.VMEM((4, 4, BLOCK, DAYS), BF16),
-            pltpu.VMEM((4, 4, RANK, BLOCK), BF16),
+            pltpu.VMEM((4, 4, BLOCK + 32, DAYS), BF16),
             pltpu.VMEM((2, GROUP, BLOCK, BLOCK), BF16),
-            pltpu.SemaphoreType.DMA((48,)),
+            pltpu.SemaphoreType.DMA((16,)),
             pltpu.SemaphoreType.DMA((2,)),
         ],
         out_specs=[HBM, VMEM, VMEM],
@@ -254,6 +253,15 @@
     rows_ref[...] = jnp.zeros_like(rows_ref)
     cols_ref[...] = jnp.zeros_like(cols_ref)
     join(near_ref, far_ref, qc_ref)
+    gram = jnp.zeros((2 * RANK, 2 * RANK), F32)
+    for k in range(N_COL):
+        gram = gram + lax.dot_general(
+            qr_ref[k], qr_ref[k], (((1,), (1,)), ((), ())), preferred_element_type=F32
+        )
+    gram = gram[:RANK, :RANK] + ((gram[:RANK, RANK:] + gram[RANK:, :RANK]) + gram[RANK:, RANK:])
+    for k in range(N_ROW):
+        for q in range(4):
+            cols_ref[k, RANK:, 64 * q : 64 * q + 64] = gram[16 * q : 16 * q + 16]
 
     def some(group, carry):
         load(tiles_ref, tiles, sems, group).wait()
@@ -274,18 +282,6 @@
         return carry
 
     lax.fori_loop(0, groups_of(table), some, 0)
-    gram = jnp.zeros((RANK, RANK), F32)
-    for k in range(N_COL):
-        both = lax.dot_general(
-            qr_ref[k, :RANK], qr_ref[k], (((1,), (1,)), ((), ())), preferred_element_type=F32
-        )
-        low_high = lax.dot_general(
-            qr_ref[k, RANK:], qr_ref[k, :RANK], (((1,), (1,)), ((), ())), preferred_element_type=F32
-        )
-        gram = gram + both[:, :RANK] + (both[:, RANK:] + low_high)
-    for k in range(N_ROW):
-        for q in range(4):
-            cols_ref[k, RANK:, 64 * q : 64 * q + 64] = gram[16 * q : 16 * q + 16]
 
 
 def product(table, tiles, qr, near, far):
@@ -519,13 +515,12 @@
     table = jnp.concatenate([block_pairs.reshape(2 * SLOTS), pair_count.reshape(1), place])
     lead = series.T
     packed = jnp.concatenate([start_basis[:32], start_basis[32:]], axis=1)
-    first = jnp.concatenate([lead[:HALF], packed[:16]], axis=0)
+    first = jnp.concatenate([packed[:16], lead[:HALF]], axis=0)
     second = jnp.concatenate([lead[HALF:], packed[16:]], axis=0)
     trail = jnp.concatenate([series, start_basis], axis=0)
     first, second, trail = lax.optimization_barrier((first, second, trail))
     first, second = around(first, "z"), around(second, "y")
     trail = around(trail, "x")
-    first, second = lax.optimization_barrier((first, second))
     first, second = both_ways(first, "y"), both_ways(second, "z")
     own = jnp.stack(trail)
     other = shift(own, "core", 1)

time: 210 us -> 201 us (0.957)
  waiting for transfers between devices: 88.2 us -> 76.8 us
  starting transfers between devices: 73.9 us -> 77.4 us
    ppermute x48, waiting for transfers between devices: 74.7 us -> 63.3 us  [shift(): return lax.ppermute(x, 'row' if axis in ('x', 'core') else 'col', pairs)]
    ppermute x48, starting transfers between devices: 59.1 us -> 62.5 us  [shift(): return lax.ppermute(x, 'row' if axis in ('x', 'core') else 'col', pairs)]
  transfers between devices with their start and end apart: 52 -> 52, of which waited for: 35 -> 31; matrix products, arithmetic and copies ran while one was open for 1% -> 1% of each run, Pallas kernels for 1% -> 1%
where the time goes in v2:
time: 201 us; the launch traced here: 200 us
  starting transfers between devices  77.4 us (39%)
  waiting for transfers between devices  76.8 us (38%)
  Pallas kernels  36.7 us (18%)
  local copies, waits for them, and re-layouts  6.22 us (3%)
    ppermute x48, waiting for transfers between devices, shift(): return lax.ppermute(x, 'row' if axis in ('x', 'core') else 'col', pairs)  63.3 us
    ppermute x48, starting transfers between devices, shift(): return lax.ppermute(x, 'row' if axis in ('x', 'core') else 'col', pairs)  62.5 us
    pallas_call x1, Pallas kernels, build(): call(build_body, [shape(TILE_ROOM, BLOCK, BLOCK, dtype=BF16), shape(N_COL...  17.2 us
    all_to_all x4, starting transfers between devices, swap(): return lax.all_to_all(x, axis, 0, 0, tiled=True)  15 us
    all_to_all x4, waiting for transfers between devices, swap(): return lax.all_to_all(x, axis, 0, 0, tiled=True)  13.5 us
    pallas_call x1, Pallas kernels, product(): call(product_body, [shape(N_COL, RANK, BLOCK), shape(N_ROW, RANK + 16, BL...  5.93 us
    unnamed x16, local copies, waits for them, and re-layouts  4.03 us
  transfers between devices with their start and end apart: 52, of which 31 were waited for; matrix products, arithmetic and copies ran while one was open for 1% of the time, Pallas kernels for 1%

profile of v2, /device:TPU:0, one launch (start us, length us, event | category | flops | bytes accessed | tf_op | source)
XLA Modules:
  0.0 200.3 jit_solution(2008506976967268528)
XLA Ops:
  8.2 10.9 %collective-permute-done.2 = bf16[576,256]{1,0:T(8,128)(2,1)S(1)} collective-permute-done((bf16[576,256]{1,0:T(8,128)(2,1)S(1)}, bf16[576,256]{1,0:T(8,128)(2,1)S(1)}, u32[]{:S(2)}, u32[]{:S(2)}) %collective-permute-start.2) | collective-permute-done | bytes 294944 | tf_op jit(solution)/shard_map/ppermute | solution.py:484
  19.1 3.7 %collective-permute-done = bf16[576,256]{1,0:T(8,128)(2,1)S(1)} collective-permute-done((bf16[576,256]{1,0:T(8,128)(2,1)S(1)}, bf16[576,256]{1,0:T(8,128)(2,1)S(1)}, u32[]{:S(2)}, u32[]{:S(2)}) %collective-permute-start) | collective-permute-done | bytes 294944 | tf_op jit(solution)/shard_map/ppermute | solution.py:484
  28.3 4.0 %collective-permute-start.6 = (bf16[144,512]{1,0:T(8,128)(2,1)S(1)}, bf16[144,512]{1,0:T(8,128)(2,1)S(1)}, u32[]{:S(2)}, u32[]{:S(2)}) collective-permute-start(bf16[144,512]{1,0:T(8,128)(2,1)S(1)} %get-tuple-element.21), channel_id=1, source_target_pairs={{0,3},{1,0},{2,1},{3,2},{4,7},{5,4},{6,5},{7,6},{8,11},{9,8},{10,9... | collective-permute-start | bytes 442376 | tf_op jit(solution)/shard_map/ppermute | solution.py:484
  38.1 4.2 %collective-permute-start.19 = (bf16[2,144,512]{2,1,0:T(8,128)(2,1)S(1)}, bf16[2,144,512]{2,1,0:T(8,128)(2,1)}, u32[]{:S(2)}, u32[]{:S(2)}) collective-permute-start(bf16[2,144,512]{2,1,0:T(8,128)(2,1)S(1)} %pad_maximum_fusion.5.rest_9_), channel_id=1, source_target_pairs={{0,3},{1,0},{2,1},{3,2},{4,7},{5,4},{6,5},{7,6},{8,11},{9,8},{10,9... | collective-permute-start | bytes 884744 | tf_op jit(solution)/shard_map/ppermute | solution.py:484
  42.4 6.5 %collective-permute-done.4 = bf16[144,512]{1,0:T(8,128)(2,1)S(1)} collective-permute-done((bf16[144,512]{1,0:T(8,128)(2,1)S(1)}, bf16[144,512]{1,0:T(8,128)(2,1)S(1)}, u32[]{:S(2)}, u32[]{:S(2)}) %collective-permute-start.4) | collective-permute-done | bytes 147488 | tf_op jit(solution)/shard_map/ppermute | solution.py:484
  52.1 3.2 %collective-permute-start.10 = (bf16[2,144,512]{2,1,0:T(8,128)(2,1)S(1)}, bf16[2,144,512]{2,1,0:T(8,128)(2,1)}, u32[]{:S(2)}, u32[]{:S(2)}) collective-permute-start(bf16[2,144,512]{2,1,0:T(8,128)(2,1)S(1)} %pad_maximum_fusion.3.rest_1_), channel_id=1, source_target_pairs={{0,12},{1,13},{2,14},{3,15},{4,0},{5,1},{6,2},{7,3},{8,4},{9,5},{1... | collective-permute-start | bytes 884744 | tf_op jit(solution)/shard_map/ppermute | solution.py:484
  64.6 3.1 %collective-permute-start.11 = (bf16[2,144,512]{2,1,0:T(8,128)(2,1)}, bf16[2,144,512]{2,1,0:T(8,128)(2,1)}, u32[]{:S(2)}, u32[]{:S(2)}) collective-permute-start(bf16[2,144,512]{2,1,0:T(8,128)(2,1)} %collective-permute-done.10.rest_7_), channel_id=1, source_target_pairs={{0,12},{1,13},{2,14},{3,15},{4,0},{5,1},{6,2},{7,3},{8,4},{9,5},{1... | collective-permute-start | bytes 884744 | tf_op jit(solution)/shard_map/ppermute | solution.py:484
  73.4 17.2 %shard_map.69 = (bf16[288,256,256]{2,1,0:T(8,128)(2,1)}, f32[16,64,256]{2,1,0:T(8,128)}, f32[8,64,256]{2,1,0:T(8,128)S(1)}) custom-call(s32[69]{0:T(128)S(1)} %concatenate.15.table, f32[4]{0:T(128)S(1)} %copy-done.6, bf16[8,4,512,256]{3,2,1,0:T(8,128)(2,1)S(1)} %get-tuple-element.19.sums_ref, bf16[8,64,256]{2,1,0:T(8,128)(2,1)S(1)} %get-tuple-element.20.xc_ref, ...), custom_call_target="tpu_custom_call" | custom-call | flops 8999999488 | bytes 20971520 | tf_op jit(solution)/shard_map/pallas_call | solution.py:180
  90.6 4.0 %all-to-all-start = ((f32[16,64,256]{2,1,0:T(8,128)}), f32[16,64,256]{2,1,0:T(8,128)S(1)}, u32[]{:S(2)}, u32[]{:S(2)}) async-start(f32[16,64,256]{2,1,0:T(8,128)} %get-tuple-element.24), calls=%async_computation | async-start | bytes 2097152 | tf_op jit(solution)/shard_map/all_to_all | solution.py:472
  96.7 3.1 %collective-permute-start.23 = (f32[1,64,256]{2,1,0:T(8,128)S(1)}, f32[1,64,256]{2,1,0:T(8,128)S(1)}, u32[]{:S(2)}, u32[]{:S(2)}) collective-permute-start(f32[1,64,256]{2,1,0:T(8,128)S(1)} %get-tuple-element.39), channel_id=1, source_target_pairs={{0,96},{16,112},{32,0},{48,16},{64,32},{80,48},{96,64},{112,80},{1... | collective-permute-start | bytes 196616 | tf_op jit(solution)/shard_map/ppermute | solution.py:484
  99.8 3.5 %collective-permute-done.25.c_ref = f32[1,64,256]{2,1,0:T(8,128)S(1)} collective-permute-done((f32[1,64,256]{2,1,0:T(8,128)S(1)}, f32[1,64,256]{2,1,0:T(8,128)S(1)}, u32[]{:S(2)}, u32[]{:S(2)}) %collective-permute-start.25) | collective-permute-done | bytes 65568 | tf_op jit(solution)/shard_map/ppermute | solution.py:484
  103.9 3.6 %all-to-all-done.rr_ref = f32[16,64,256]{2,1,0:T(8,128)S(1)} async-done(((f32[16,64,256]{2,1,0:T(8,128)}), f32[16,64,256]{2,1,0:T(8,128)S(1)}, u32[]{:S(2)}, u32[]{:S(2)}) %all-to-all-start) | async-done | bytes 1048608 | tf_op jit(solution)/shard_map/all_to_all | solution.py:472
  108.6 3.7 %all-to-all-start.1 = ((bf16[16,128,256]{2,1,0:T(8,128)(2,1)}), bf16[16,128,256]{2,1,0:T(8,128)(2,1)S(1)}, u32[]{:S(2)}, u32[]{:S(2)}) async-start(bf16[16,128,256]{2,1,0:T(8,128)(2,1)} %get-tuple-element.26), calls=%async_computation.1 | async-start | bytes 2097152 | tf_op jit(solution)/shard_map/all_to_all | solution.py:472
  117.2 3.3 %collective-permute-done.27 = bf16[128,256]{1,0:T(8,128)(2,1)S(1)} collective-permute-done((bf16[128,256]{1,0:T(8,128)(2,1)S(1)}, bf16[128,256]{1,0:T(8,128)(2,1)S(1)}, u32[]{:S(2)}, u32[]{:S(2)}) %collective-permute-start.27) | collective-permute-done | bytes 65568 | tf_op jit(solution)/shard_map/ppermute | solution.py:484
  122.8 6.0 %all-to-all-done.1.qr_ref = bf16[16,128,256]{2,1,0:T(8,128)(2,1)S(1)} async-done(((bf16[16,128,256]{2,1,0:T(8,128)(2,1)}), bf16[16,128,256]{2,1,0:T(8,128)(2,1)S(1)}, u32[]{:S(2)}, u32[]{:S(2)}) %all-to-all-start.1) | async-done | bytes 1048608 | tf_op jit(solution)/shard_map/all_to_all | solution.py:472
  128.8 5.9 %shard_map.71 = (f32[16,64,256]{2,1,0:T(8,128)}, f32[8,80,256]{2,1,0:T(8,128)S(1)}) custom-call(s32[69]{0:T(128)S(1)} %concatenate.15.table, bf16[288,256,256]{2,1,0:T(8,128)(2,1)} %get-tuple-element.23.tiles_ref, bf16[16,128,256]{2,1,0:T(8,128)(2,1)S(1)} %all-to-all-done.1.qr_ref, bf16[4,128,256]{2,1,0:T(8,128)(2,1)S(1)} %pad_maximum_fusion.6.near_ref, ...), custom_call_target="tpu_custom_call" | custom-call | flops 1000000000 | bytes 8388608 | tf_op jit(solution)/shard_map/pallas_call | solution.py:288
  134.7 3.7 %all-to-all-start.2 = ((f32[16,64,256]{2,1,0:T(8,128)}), f32[16,64,256]{2,1,0:T(8,128)S(1)}, u32[]{:S(2)}, u32[]{:S(2)}) async-start(f32[16,64,256]{2,1,0:T(8,128)} %get-tuple-element.28), calls=%async_computation.2 | async-start | bytes 2097152 | tf_op jit(solution)/shard_map/all_to_all | solution.py:472
  143.5 4.2 %collective-permute-done.33.c_ref = f32[1,80,256]{2,1,0:T(8,128)S(1)} collective-permute-done((f32[1,80,256]{2,1,0:T(8,128)S(1)}, f32[1,80,256]{2,1,0:T(8,128)S(1)}, u32[]{:S(2)}, u32[]{:S(2)}) %collective-permute-start.33) | collective-permute-done | bytes 81952 | tf_op jit(solution)/shard_map/ppermute | solution.py:484
  148.3 3.9 %all-to-all-done.2.rr_ref = f32[16,64,256]{2,1,0:T(8,128)S(1)} async-done(((f32[16,64,256]{2,1,0:T(8,128)}), f32[16,64,256]{2,1,0:T(8,128)S(1)}, u32[]{:S(2)}, u32[]{:S(2)}) %all-to-all-start.2) | async-done | bytes 1048608 | tf_op jit(solution)/shard_map/all_to_all | solution.py:472
  155.1 3.6 %all-to-all-start.3 = ((bf16[16,64,256]{2,1,0:T(8,128)(2,1)}), bf16[16,64,256]{2,1,0:T(8,128)(2,1)S(1)}, u32[]{:S(2)}, u32[]{:S(2)}) async-start(bf16[16,64,256]{2,1,0:T(8,128)(2,1)} %get-tuple-element.30), calls=%async_computation.3 | async-start | bytes 1048576 | tf_op jit(solution)/shard_map/all_to_all | solution.py:472
  158.6 3.5 %collective-permute-start.36 = (bf16[64,256]{1,0:T(8,128)(2,1)S(1)}, bf16[64,256]{1,0:T(8,128)(2,1)S(1)}, u32[]{:S(2)}, u32[]{:S(2)}) collective-permute-start(bf16[64,256]{1,0:T(8,128)(2,1)S(1)} %get-tuple-element.31), channel_id=1, source_target_pairs={{0,96},{16,112},{32,0},{48,16},{64,32},{80,48},{96,64},{112,80},{1... | collective-permute-start | bytes 98312 | tf_op jit(solution)/shard_map/ppermute | solution.py:484
  163.7 3.9 %collective-permute-done.35 = bf16[64,256]{1,0:T(8,128)(2,1)S(1)} collective-permute-done((bf16[64,256]{1,0:T(8,128)(2,1)S(1)}, bf16[64,256]{1,0:T(8,128)(2,1)S(1)}, u32[]{:S(2)}, u32[]{:S(2)}) %collective-permute-start.35) | collective-permute-done | bytes 32800 | tf_op jit(solution)/shard_map/ppermute | solution.py:484
  169.1 4.0 %shard_map.73 = f32[40,128]{1,0:T(8,128)S(1)} custom-call(s32[69]{0:T(128)S(1)} %concatenate.15.table, bf16[288,256,256]{2,1,0:T(8,128)(2,1)} %get-tuple-element.23.tiles_ref, bf16[16,64,256]{2,1,0:T(8,128)(2,1)S(1)} %all-to-all-done.3.qr_ref, bf16[4,64,256]{2,1,0:T(8,128)(2,1)S(1)} %pad_maximum_fusion.8.near_ref, ...), custom_call_target="tpu_custom_call" | custom-call | flops 500000000 | bytes 6291456 | tf_op jit(solution)/shard_map/pallas_call | solution.py:434
  193.6 3.3 %collective-permute-done.46.b_ref = f32[40,128]{1,0:T(8,128)S(1)} collective-permute-done((f32[40,128]{1,0:T(8,128)S(1)}, f32[40,128]{1,0:T(8,128)S(1)}, u32[]{:S(2)}, u32[]{:S(2)}) %collective-permute-start.46) | collective-permute-done | bytes 20512 | tf_op jit(solution)/shard_map/ppermute | solution.py:484
  (126 shorter events, 82.7 us)
Async XLA Ops:
  3.5 15.5 %collective-permute-start.2 = (bf16[576,256]{1,0:T(8,128)(2,1)S(1)}, bf16[576,256]{1,0:T(8,128)(2,1)S(1)}, u32[]{:S(2)}, u32[]{:S(2)}) collective-permute-start(bf16[576,256]{1,0:T(8,128)(2,1)S(1)} %pad_maximum_fusion.1), channel_id=1, source_target_pairs={{0,96},{16,112},{32,0},{48,16},{64,32},{80,48},{96,64},{112,80},{1... | collective-permute-start | bytes 884744 | tf_op jit(solution)/shard_map/ppermute | solution.py:484
  6.5 12.6 %collective-permute-start.1 = (bf16[576,256]{1,0:T(8,128)(2,1)S(1)}, bf16[576,256]{1,0:T(8,128)(2,1)S(1)}, u32[]{:S(2)}, u32[]{:S(2)}) collective-permute-start(bf16[576,256]{1,0:T(8,128)(2,1)S(1)} %pad_maximum_fusion.1), channel_id=1, source_target_pairs={{0,64},{16,80},{32,96},{48,112},{64,0},{80,16},{96,32},{112,48},{1... | collective-permute-start | bytes 884744 | tf_op jit(solution)/shard_map/ppermute | solution.py:484
  7.3 15.5 %collective-permute-start = (bf16[576,256]{1,0:T(8,128)(2,1)S(1)}, bf16[576,256]{1,0:T(8,128)(2,1)S(1)}, u32[]{:S(2)}, u32[]{:S(2)}) collective-permute-start(bf16[576,256]{1,0:T(8,128)(2,1)S(1)} %pad_maximum_fusion.1), channel_id=1, source_target_pairs={{0,32},{16,48},{32,64},{48,80},{64,96},{80,112},{96,0},{112,16},{1... | collective-permute-start | bytes 884744 | tf_op jit(solution)/shard_map/ppermute | solution.py:484
  22.9 41.7 %collective-permute-start.3 = (bf16[4,576,256]{2,1,0:T(8,128)(2,1)S(1)}, bf16[4,576,256]{2,1,0:T(8,128)(2,1)S(1)}, u32[]{:S(2)}, u32[]{:S(2)}) collective-permute-start(bf16[4,576,256]{2,1,0:T(8,128)(2,1)S(1)} %pad_maximum_fusion.own_ref), channel_id=1, source_target_pairs={{0,16},{16,0},{32,48},{48,32},{64,80},{80,64},{96,112},{112,96},{1... | collective-permute-start | bytes 3538952 | tf_op jit(solution)/shard_map/ppermute | solution.py:484
  23.0 9.3 %collective-permute-start.13 = (bf16[144,512]{1,0:T(8,128)(2,1)S(1)}, bf16[144,512]{1,0:T(8,128)(2,1)S(1)}, u32[]{:S(2)}, u32[]{:S(2)}) collective-permute-start(bf16[144,512]{1,0:T(8,128)(2,1)S(1)} %get-tuple-element.22), channel_id=1, source_target_pairs={{0,4},{1,5},{2,6},{3,7},{4,8},{5,9},{6,10},{7,11},{8,12},{9,13},{1... | collective-permute-start | bytes 442376 | tf_op jit(solution)/shard_map/ppermute | solution.py:484
  24.7 9.8 %collective-permute-start.15 = (bf16[144,512]{1,0:T(8,128)(2,1)S(1)}, bf16[144,512]{1,0:T(8,128)(2,1)S(1)}, u32[]{:S(2)}, u32[]{:S(2)}) collective-permute-start(bf16[144,512]{1,0:T(8,128)(2,1)S(1)} %get-tuple-element.22), channel_id=1, source_target_pairs={{0,12},{1,13},{2,14},{3,15},{4,0},{5,1},{6,2},{7,3},{8,4},{9,5},{1... | collective-permute-start | bytes 442376 | tf_op jit(solution)/shard_map/ppermute | solution.py:484
  26.3 9.1 %collective-permute-start.14 = (bf16[144,512]{1,0:T(8,128)(2,1)S(1)}, bf16[144,512]{1,0:T(8,128)(2,1)S(1)}, u32[]{:S(2)}, u32[]{:S(2)}) collective-permute-start(bf16[144,512]{1,0:T(8,128)(2,1)S(1)} %get-tuple-element.22), channel_id=1, source_target_pairs={{0,8},{1,9},{2,10},{3,11},{4,12},{5,13},{6,14},{7,15},{8,0},{9,1},... | collective-permute-start | bytes 442376 | tf_op jit(solution)/shard_map/ppermute | solution.py:484
  28.3 9.8 %collective-permute-start.6 = (bf16[144,512]{1,0:T(8,128)(2,1)S(1)}, bf16[144,512]{1,0:T(8,128)(2,1)S(1)}, u32[]{:S(2)}, u32[]{:S(2)}) collective-permute-start(bf16[144,512]{1,0:T(8,128)(2,1)S(1)} %get-tuple-element.21), channel_id=1, source_target_pairs={{0,3},{1,0},{2,1},{3,2},{4,7},{5,4},{6,5},{7,6},{8,11},{9,8},{10,9... | collective-permute-start | bytes 442376 | tf_op jit(solution)/shard_map/ppermute | solution.py:484
  32.3 10.0 %collective-permute-start.5 = (bf16[144,512]{1,0:T(8,128)(2,1)S(1)}, bf16[144,512]{1,0:T(8,128)(2,1)S(1)}, u32[]{:S(2)}, u32[]{:S(2)}) collective-permute-start(bf16[144,512]{1,0:T(8,128)(2,1)S(1)} %get-tuple-element.21), channel_id=1, source_target_pairs={{0,2},{1,3},{2,0},{3,1},{4,6},{5,7},{6,4},{7,5},{8,10},{9,11},{10,... | collective-permute-start | bytes 442376 | tf_op jit(solution)/shard_map/ppermute | solution.py:484
  34.5 14.9 %collective-permute-start.21 = (bf16[2,144,512]{2,1,0:T(8,128)(2,1)S(1)}, bf16[2,144,512]{2,1,0:T(8,128)(2,1)S(1)}, u32[]{:S(2)}, u32[]{:S(2)}) collective-permute-start(bf16[2,144,512]{2,1,0:T(8,128)(2,1)S(1)} %pad_maximum_fusion.4.rest_8_), channel_id=1, source_target_pairs={{0,3},{1,0},{2,1},{3,2},{4,7},{5,4},{6,5},{7,6},{8,11},{9,8},{10,9... | collective-permute-start | bytes 884744 | tf_op jit(solution)/shard_map/ppermute | solution.py:484
  35.4 16.6 %collective-permute-start.16 = (bf16[2,144,512]{2,1,0:T(8,128)(2,1)S(1)}, bf16[2,144,512]{2,1,0:T(8,128)(2,1)}, u32[]{:S(2)}, u32[]{:S(2)}) collective-permute-start(bf16[2,144,512]{2,1,0:T(8,128)(2,1)S(1)} %pad_maximum_fusion.4.rest_8_), channel_id=1, source_target_pairs={{0,1},{1,2},{2,3},{3,0},{4,5},{5,6},{6,7},{7,4},{8,9},{9,10},{10,1... | collective-permute-start | bytes 884744 | tf_op jit(solution)/shard_map/ppermute | solution.py:484
  38.1 13.9 %collective-permute-start.19 = (bf16[2,144,512]{2,1,0:T(8,128)(2,1)S(1)}, bf16[2,144,512]{2,1,0:T(8,128)(2,1)}, u32[]{:S(2)}, u32[]{:S(2)}) collective-permute-start(bf16[2,144,512]{2,1,0:T(8,128)(2,1)S(1)} %pad_maximum_fusion.5.rest_9_), channel_id=1, source_target_pairs={{0,3},{1,0},{2,1},{3,2},{4,7},{5,4},{6,5},{7,6},{8,11},{9,8},{10,9... | collective-permute-start | bytes 884744 | tf_op jit(solution)/shard_map/ppermute | solution.py:484
  48.8 8.8 %collective-permute-start.17 = (bf16[2,144,512]{2,1,0:T(8,128)(2,1)S(1)}, bf16[2,144,512]{2,1,0:T(8,128)(2,1)S(1)}, u32[]{:S(2)}, u32[]{:S(2)}) collective-permute-start(bf16[2,144,512]{2,1,0:T(8,128)(2,1)S(1)} %pad_maximum_fusion.5.rest_9_), channel_id=1, source_target_pairs={{0,1},{1,2},{2,3},{3,0},{4,5},{5,6},{6,7},{7,4},{8,9},{9,10},{10,1... | collective-permute-start | bytes 884744 | tf_op jit(solution)/shard_map/ppermute | solution.py:484
  50.0 9.9 %collective-permute-start.12 = (bf16[2,144,512]{2,1,0:T(8,128)(2,1)S(1)}, bf16[2,144,512]{2,1,0:T(8,128)(2,1)S(1)}, u32[]{:S(2)}, u32[]{:S(2)}) collective-permute-start(bf16[2,144,512]{2,1,0:T(8,128)(2,1)S(1)} %pad_maximum_fusion.2.rest_0_), channel_id=1, source_target_pairs={{0,12},{1,13},{2,14},{3,15},{4,0},{5,1},{6,2},{7,3},{8,4},{9,5},{1... | collective-permute-start | bytes 884744 | tf_op jit(solution)/shard_map/ppermute | solution.py:484
  52.1 10.3 %collective-permute-start.7 = (bf16[2,144,512]{2,1,0:T(8,128)(2,1)S(1)}, bf16[2,144,512]{2,1,0:T(8,128)(2,1)}, u32[]{:S(2)}, u32[]{:S(2)}) collective-permute-start(bf16[2,144,512]{2,1,0:T(8,128)(2,1)S(1)} %pad_maximum_fusion.2.rest_0_), channel_id=1, source_target_pairs={{0,4},{1,5},{2,6},{3,7},{4,8},{5,9},{6,10},{7,11},{8,12},{9,13},{1... | collective-permute-start | bytes 884744 | tf_op jit(solution)/shard_map/ppermute | solution.py:484
  52.1 12.4 %collective-permute-start.10 = (bf16[2,144,512]{2,1,0:T(8,128)(2,1)S(1)}, bf16[2,144,512]{2,1,0:T(8,128)(2,1)}, u32[]{:S(2)}, u32[]{:S(2)}) collective-permute-start(bf16[2,144,512]{2,1,0:T(8,128)(2,1)S(1)} %pad_maximum_fusion.3.rest_1_), channel_id=1, source_target_pairs={{0,12},{1,13},{2,14},{3,15},{4,0},{5,1},{6,2},{7,3},{8,4},{9,5},{1... | collective-permute-start | bytes 884744 | tf_op jit(solution)/shard_map/ppermute | solution.py:484
  58.3 14.9 %collective-permute-start.8 = (bf16[2,144,512]{2,1,0:T(8,128)(2,1)S(1)}, bf16[2,144,512]{2,1,0:T(8,128)(2,1)}, u32[]{:S(2)}, u32[]{:S(2)}) collective-permute-start(bf16[2,144,512]{2,1,0:T(8,128)(2,1)S(1)} %pad_maximum_fusion.3.rest_1_), channel_id=1, source_target_pairs={{0,4},{1,5},{2,6},{3,7},{4,8},{5,9},{6,10},{7,11},{8,12},{9,13},{1... | collective-permute-start | bytes 884744 | tf_op jit(solution)/shard_map/ppermute | solution.py:484
  60.7 12.6 %collective-permute-start.18 = (bf16[2,144,512]{2,1,0:T(8,128)(2,1)}, bf16[2,144,512]{2,1,0:T(8,128)(2,1)}, u32[]{:S(2)}, u32[]{:S(2)}) collective-permute-start(bf16[2,144,512]{2,1,0:T(8,128)(2,1)} %collective-permute-done.16.rest_10_), channel_id=1, source_target_pairs={{0,1},{1,2},{2,3},{3,0},{4,5},{5,6},{6,7},{7,4},{8,9},{9,10},{10,1... | collective-permute-start | bytes 884744 | tf_op jit(solution)/shard_map/ppermute | solution.py:484
  62.3 10.9 %collective-permute-start.20 = (bf16[2,144,512]{2,1,0:T(8,128)(2,1)}, bf16[2,144,512]{2,1,0:T(8,128)(2,1)}, u32[]{:S(2)}, u32[]{:S(2)}) collective-permute-start(bf16[2,144,512]{2,1,0:T(8,128)(2,1)} %collective-permute-done.19.rest_15_), channel_id=1, source_target_pairs={{0,3},{1,0},{2,1},{3,2},{4,7},{5,4},{6,5},{7,6},{8,11},{9,8},{10,9... | collective-permute-start | bytes 884744 | tf_op jit(solution)/shard_map/ppermute | solution.py:484
  64.5 8.8 %collective-permute-start.9 = (bf16[2,144,512]{2,1,0:T(8,128)(2,1)}, bf16[2,144,512]{2,1,0:T(8,128)(2,1)}, u32[]{:S(2)}, u32[]{:S(2)}) collective-permute-start(bf16[2,144,512]{2,1,0:T(8,128)(2,1)} %collective-permute-done.7.rest_2_), channel_id=1, source_target_pairs={{0,4},{1,5},{2,6},{3,7},{4,8},{5,9},{6,10},{7,11},{8,12},{9,13},{1... | collective-permute-start | bytes 884744 | tf_op jit(solution)/shard_map/ppermute | solution.py:484
  90.6 17.0 %all-to-all-start = ((f32[16,64,256]{2,1,0:T(8,128)}), f32[16,64,256]{2,1,0:T(8,128)S(1)}, u32[]{:S(2)}, u32[]{:S(2)}) async-start(f32[16,64,256]{2,1,0:T(8,128)} %get-tuple-element.24), calls=%async_computation | async-start | bytes 2097152 | tf_op jit(solution)/shard_map/all_to_all | solution.py:472
  108.6 20.2 %all-to-all-start.1 = ((bf16[16,128,256]{2,1,0:T(8,128)(2,1)}), bf16[16,128,256]{2,1,0:T(8,128)(2,1)S(1)}, u32[]{:S(2)}, u32[]{:S(2)}) async-start(bf16[16,128,256]{2,1,0:T(8,128)(2,1)} %get-tuple-element.26), calls=%async_computation.1 | async-start | bytes 2097152 | tf_op jit(solution)/shard_map/all_to_all | solution.py:472
  134.7 17.5 %all-to-all-start.2 = ((f32[16,64,256]{2,1,0:T(8,128)}), f32[16,64,256]{2,1,0:T(8,128)S(1)}, u32[]{:S(2)}, u32[]{:S(2)}) async-start(f32[16,64,256]{2,1,0:T(8,128)} %get-tuple-element.28), calls=%async_computation.2 | async-start | bytes 2097152 | tf_op jit(solution)/shard_map/all_to_all | solution.py:472
  155.1 14.0 %all-to-all-start.3 = ((bf16[16,64,256]{2,1,0:T(8,128)(2,1)}), bf16[16,64,256]{2,1,0:T(8,128)(2,1)S(1)}, u32[]{:S(2)}, u32[]{:S(2)}) async-start(bf16[16,64,256]{2,1,0:T(8,128)(2,1)} %get-tuple-element.30), calls=%async_computation.3 | async-start | bytes 1048576 | tf_op jit(solution)/shard_map/all_to_all | solution.py:472
  (35 other events, 154.5 us)

commit v3 on v2

--- a/solution.py
+++ b/solution.py
@@ -43,6 +43,29 @@
     return jax.ShapeDtypeStruct(dims, dtype)
 
 
+def pack_body(series_ref, start_ref, first_ref, second_ref, trail_ref):
+    trail_ref[:DAYS] = series_ref[...]
+    trail_ref[DAYS:] = start_ref[...]
+    first_ref[:16, :BLOCK] = start_ref[:16]
+    first_ref[:16, BLOCK:] = start_ref[32:48]
+    second_ref[BLOCK // 2 :, :BLOCK] = start_ref[16:32]
+    second_ref[BLOCK // 2 :, BLOCK:] = start_ref[48:]
+    first_ref[16:] = series_ref[:, : BLOCK // 2].T
+    second_ref[: BLOCK // 2] = series_ref[:, BLOCK // 2 :].T
+
+
+def pack(series, start):
+    half = shape(BLOCK // 2 + 16, DAYS, dtype=BF16)
+    return call(
+        pack_body,
+        [half, half, shape(DAYS + RANK, BLOCK, dtype=BF16)],
+        [VMEM, VMEM],
+        100_000,
+        1 << 20,
+        4,
+    )(series, start)
+
+
 def shift_body(own_ref, other_ref, out_ref, xc_ref):
     day = lax.broadcasted_iota(jnp.int32, (DAYS, BLOCK), 0)
     for core, ref in enumerate((own_ref, other_ref)):
@@ -74,23 +97,24 @@
 
 HALF = BLOCK // 2
 GROUP = 4
-PLACE = 2 * SLOTS + 1
 TILE_ROOM = 288
 
 
 def count_of(table):
-    return table[2 * SLOTS]
+    return table[1][0, 0]
 
 
 def row_offset(table, j):
-    return ((j ^ table[PLACE + 1]) & 1) * 4 + ((table[PLACE] - j // 2) & 3)
+    place = table[2]
+    return ((j ^ place[1]) & 1) * 4 + ((place[0] - j // 2) & 3)
 
 
 def groups_of(table):
     return (count_of(table) + GROUP - 1) // GROUP
 
 
-def build_body(table, weight, sums_ref, xc_ref, *rest):
+def build_body(pairs, count, place, weight, sums_ref, xc_ref, *rest):
+    table = (pairs, count, place)
     first, second = rest[:8], rest[8:16]
     tiles_ref, rows_ref, cols_ref, at_ref, buffer, sems, out_sems = rest[16:]
     copies = []
@@ -113,10 +137,10 @@
     groups = groups_of(table)
 
     def indices(slot):
-        i = table[2 * slot] % N_COL
-        from_y = (table[PLACE + 2] - i // 4) & 3
-        from_z = (table[PLACE + 3] - i) & 3
-        return i, from_y, from_z, row_offset(table, table[2 * slot + 1] // N_COL)
+        i = table[0][0, slot] % N_COL
+        from_y = (table[2][2] - i // 4) & 3
+        from_z = (table[2][3] - i) & 3
+        return i, from_y, from_z, row_offset(table, table[0][1, slot] // N_COL)
 
     def basis_of(from_y, from_z):
         ends = [at_ref[from_y, from_z, :16], at_ref[from_y, from_z, 16 + BLOCK :]]
@@ -184,7 +208,7 @@
             shape(N_COL, RANK, BLOCK),
             shape(N_ROW, RANK, BLOCK),
         ],
-        [SMEM] * 2 + [VMEM] * 2 + [ANY] * 16,
+        [SMEM] * 4 + [VMEM] * 2 + [ANY] * 16,
         9_000_000_000,
         20 << 20,
         30,
@@ -195,7 +219,7 @@
             pltpu.SemaphoreType.DMA((2,)),
         ],
         out_specs=[HBM, VMEM, VMEM],
-    )(table, weight, sums, xc, *first, *second)
+    )(*table, weight, sums, xc, *first, *second)
 
 
 def total_of(rr_ref, own_ref, parts):
@@ -248,7 +272,10 @@
     joined_ref[4:] = far_ref[...]
 
 
-def product_body(table, tiles_ref, qr_ref, near_ref, far_ref, rows_ref, cols_ref, qc_ref, tiles, sems):
+def product_body(
+    pairs, count, place, tiles_ref, qr_ref, near_ref, far_ref, rows_ref, cols_ref, qc_ref, tiles, sems
+):
+    table = (pairs, count, place)
     load_all(table, tiles_ref, tiles, sems)
     rows_ref[...] = jnp.zeros_like(rows_ref)
     cols_ref[...] = jnp.zeros_like(cols_ref)
@@ -268,8 +295,8 @@
         done = []
         for k in range(GROUP):
             slot = group * GROUP + k
-            i = table[2 * slot] % N_COL
-            j = row_offset(table, table[2 * slot + 1] // N_COL)
+            i = table[0][0, slot] % N_COL
+            j = row_offset(table, table[0][1, slot] // N_COL)
             tile = tiles[slot]
             into_cols = jnp.dot(qr_ref[i], tile, preferred_element_type=F32)
             into_rows = lax.dot_general(
@@ -288,12 +315,12 @@
     return call(
         product_body,
         [shape(N_COL, RANK, BLOCK), shape(N_ROW, RANK + 16, BLOCK)],
-        [SMEM] + [HBM] + [VMEM] * 3,
+        [SMEM] * 3 + [HBM] + [VMEM] * 3,
         1_000_000_000,
         8 << 20,
         30,
         scratch=[pltpu.VMEM((N_ROW, 2 * RANK, BLOCK), BF16)] + TILES,
-    )(table, tiles, qr, near, far)
+    )(*table, tiles, qr, near, far)
 
 
 PANEL = 8
@@ -391,8 +418,21 @@
 
 
 def project_body(
-    table, tiles_ref, qr_ref, near_ref, far_ref, gram_ref, out_ref, cols_ref, qc_ref, tiles, sems
+    pairs,
+    count,
+    place,
+    tiles_ref,
+    qr_ref,
+    near_ref,
+    far_ref,
+    gram_ref,
+    out_ref,
+    cols_ref,
+    qc_ref,
+    tiles,
+    sems,
 ):
+    table = (pairs, count, place)
     load_all(table, tiles_ref, tiles, sems)
     cols_ref[...] = jnp.zeros_like(cols_ref)
     join(near_ref, far_ref, qc_ref)
@@ -402,8 +442,8 @@
         done = []
         for k in range(GROUP):
             slot = group * GROUP + k
-            i = table[2 * slot] % N_COL
-            j = row_offset(table, table[2 * slot + 1] // N_COL)
+            i = table[0][0, slot] % N_COL
+            j = row_offset(table, table[0][1, slot] // N_COL)
             done.append((j, jnp.dot(qr_ref[i], tiles[slot], preferred_element_type=F32)))
         for j, into_cols in done:
             cols_ref[j] += into_cols
@@ -434,13 +474,13 @@
     return call(
         project_body,
         shape(PACKED, 2 * RANK),
-        [SMEM] + [HBM] + [VMEM] * 4,
+        [SMEM] * 3 + [HBM] + [VMEM] * 4,
         500_000_000,
         6 << 20,
         30,
         scratch=[pltpu.VMEM((N_ROW, RANK, BLOCK), F32), pltpu.VMEM((N_ROW, RANK, BLOCK), BF16)]
         + TILES,
-    )(table, tiles, qr, near, far, gram)
+    )(*table, tiles, qr, near, far, gram)
 
 
 def finish_body(own_ref, a_ref, b_ref, c_ref, p_ref, basis_ref, form_ref):
@@ -512,13 +552,8 @@
 def local(series, lag_weight, start_basis, block_pairs, pair_count):
     row, col = lax.axis_index("row"), lax.axis_index("col")
     place = jnp.stack([row // 2, row % 2, col // 4, col % 4]).astype(jnp.int32)
-    table = jnp.concatenate([block_pairs.reshape(2 * SLOTS), pair_count.reshape(1), place])
-    lead = series.T
-    packed = jnp.concatenate([start_basis[:32], start_basis[32:]], axis=1)
-    first = jnp.concatenate([packed[:16], lead[:HALF]], axis=0)
-    second = jnp.concatenate([lead[HALF:], packed[16:]], axis=0)
-    trail = jnp.concatenate([series, start_basis], axis=0)
-    first, second, trail = lax.optimization_barrier((first, second, trail))
+    table = (block_pairs.reshape(SLOTS, 2).T, pair_count, place)
+    first, second, trail = pack(series, start_basis)
     first, second = around(first, "z"), around(second, "y")
     trail = around(trail, "x")
     first, second = both_ways(first, "y"), both_ways(second, "z")

time: 201 us -> 200 us (level)
  local copies, waits for them, and re-layouts: 6.22 us -> 3.95 us
    unnamed x16 -> x20, local copies, waits for them, and re-layouts: 4.03 us -> 3.87 us
    pallas_call x1 -> x2, Pallas kernels: 4 us -> 4.13 us  [the longest x1 4.01 us: project(): call(project_body, shape(PACKED, 2 * RANK), [SMEM] * 3 + [HBM] + [VMEM] *...]
  transfers between devices with their start and end apart: 52 -> 52, of which waited for: 31 -> 32; matrix products, arithmetic and copies ran while one was open for 1% -> 0% of each run, Pallas kernels for 1% -> 1%
where the time goes in v3:
time: 200 us; the launch traced here: 199 us
  waiting for transfers between devices  78.6 us (39%)
  starting transfers between devices  77.7 us (39%)
  Pallas kernels  36.9 us (18%)
  local copies, waits for them, and re-layouts  3.95 us (2%)
    ppermute x48, waiting for transfers between devices, shift(): return lax.ppermute(x, 'row' if axis in ('x', 'core') else 'col', pairs)  65.1 us
    ppermute x48, starting transfers between devices, shift(): return lax.ppermute(x, 'row' if axis in ('x', 'core') else 'col', pairs)  62.6 us
    pallas_call x1, Pallas kernels, build(): call(build_body, [shape(TILE_ROOM, BLOCK, BLOCK, dtype=BF16), shape(N_COL...  17.2 us
    all_to_all x4, starting transfers between devices, swap(): return lax.all_to_all(x, axis, 0, 0, tiled=True)  15.1 us
    all_to_all x4, waiting for transfers between devices, swap(): return lax.all_to_all(x, axis, 0, 0, tiled=True)  13.5 us
    pallas_call x1, Pallas kernels, product(): call(product_body, [shape(N_COL, RANK, BLOCK), shape(N_ROW, RANK + 16, BL...  5.93 us
    pallas_call x1, Pallas kernels, project(): call(project_body, shape(PACKED, 2 * RANK), [SMEM] * 3 + [HBM] + [VMEM] *...  4.01 us
  transfers between devices with their start and end apart: 52, of which 32 were waited for; matrix products, arithmetic and copies ran while one was open for 0% of the time, Pallas kernels for 1%

profile of v3, /device:TPU:0, one launch (start us, length us, event | category | flops | bytes accessed | tf_op | source)
XLA Modules:
  0.0 199.3 jit_solution(16807422402992271948)
XLA Ops:
  7.1 10.9 %collective-permute-done.2 = bf16[576,256]{1,0:T(8,128)(2,1)S(1)} collective-permute-done((bf16[576,256]{1,0:T(8,128)(2,1)S(1)}, bf16[576,256]{1,0:T(8,128)(2,1)S(1)}, u32[]{:S(2)}, u32[]{:S(2)}) %collective-permute-start.2) | collective-permute-done | bytes 294944 | tf_op jit(solution)/shard_map/ppermute | solution.py:524
  18.0 3.7 %collective-permute-done = bf16[576,256]{1,0:T(8,128)(2,1)S(1)} collective-permute-done((bf16[576,256]{1,0:T(8,128)(2,1)S(1)}, bf16[576,256]{1,0:T(8,128)(2,1)S(1)}, u32[]{:S(2)}, u32[]{:S(2)}) %collective-permute-start) | collective-permute-done | bytes 294944 | tf_op jit(solution)/shard_map/ppermute | solution.py:524
  27.2 4.0 %collective-permute-start.6 = (bf16[144,512]{1,0:T(8,128)(2,1)S(1)}, bf16[144,512]{1,0:T(8,128)(2,1)S(1)}, u32[]{:S(2)}, u32[]{:S(2)}) collective-permute-start(bf16[144,512]{1,0:T(8,128)(2,1)S(1)} %get-tuple-element.21), channel_id=1, source_target_pairs={{0,3},{1,0},{2,1},{3,2},{4,7},{5,4},{6,5},{7,6},{8,11},{9,8},{10,9... | collective-permute-start | bytes 442376 | tf_op jit(solution)/shard_map/ppermute | solution.py:524
  37.1 4.2 %collective-permute-start.19 = (bf16[2,144,512]{2,1,0:T(8,128)(2,1)S(1)}, bf16[2,144,512]{2,1,0:T(8,128)(2,1)}, u32[]{:S(2)}, u32[]{:S(2)}) collective-permute-start(bf16[2,144,512]{2,1,0:T(8,128)(2,1)S(1)} %pad_maximum_fusion.4.rest_9_), channel_id=1, source_target_pairs={{0,3},{1,0},{2,1},{3,2},{4,7},{5,4},{6,5},{7,6},{8,11},{9,8},{10,9... | collective-permute-start | bytes 884744 | tf_op jit(solution)/shard_map/ppermute | solution.py:524
  41.3 6.5 %collective-permute-done.4 = bf16[144,512]{1,0:T(8,128)(2,1)S(1)} collective-permute-done((bf16[144,512]{1,0:T(8,128)(2,1)S(1)}, bf16[144,512]{1,0:T(8,128)(2,1)S(1)}, u32[]{:S(2)}, u32[]{:S(2)}) %collective-permute-start.4) | collective-permute-done | bytes 147488 | tf_op jit(solution)/shard_map/ppermute | solution.py:524
  51.0 3.2 %collective-permute-start.10 = (bf16[2,144,512]{2,1,0:T(8,128)(2,1)S(1)}, bf16[2,144,512]{2,1,0:T(8,128)(2,1)}, u32[]{:S(2)}, u32[]{:S(2)}) collective-permute-start(bf16[2,144,512]{2,1,0:T(8,128)(2,1)S(1)} %pad_maximum_fusion.2.rest_1_), channel_id=1, source_target_pairs={{0,12},{1,13},{2,14},{3,15},{4,0},{5,1},{6,2},{7,3},{8,4},{9,5},{1... | collective-permute-start | bytes 884744 | tf_op jit(solution)/shard_map/ppermute | solution.py:524
  63.6 3.1 %collective-permute-start.11 = (bf16[2,144,512]{2,1,0:T(8,128)(2,1)}, bf16[2,144,512]{2,1,0:T(8,128)(2,1)}, u32[]{:S(2)}, u32[]{:S(2)}) collective-permute-start(bf16[2,144,512]{2,1,0:T(8,128)(2,1)} %collective-permute-done.10.rest_7_), channel_id=1, source_target_pairs={{0,12},{1,13},{2,14},{3,15},{4,0},{5,1},{6,2},{7,3},{8,4},{9,5},{1... | collective-permute-start | bytes 884744 | tf_op jit(solution)/shard_map/ppermute | solution.py:524
  72.1 17.2 %shard_map.70 = (bf16[288,256,256]{2,1,0:T(8,128)(2,1)}, f32[16,64,256]{2,1,0:T(8,128)}, f32[8,64,256]{2,1,0:T(8,128)S(1)}) custom-call(s32[2,32]{1,0:T(2,128)S(1)} %bitcast.32, s32[1,1]{1,0:T(1,128)S(6)} %copy.7.count, s32[4]{0:T(128)S(1)} %pad_add_fusion.place, f32[4]{0:T(128)S(1)} %copy-done.9, bf16[8,4,512,256]{3,2,1,0:T(8,128)(2,1)S(1)} %get-tuple-element.19.sums_ref, ...), custom_call_target="tpu_custom_call" | custom-call | flops 8999999488 | bytes 20971520 | tf_op jit(solution)/shard_map/pallas_call | solution.py:204
  89.4 4.2 %all-to-all-start = ((f32[16,64,256]{2,1,0:T(8,128)}), f32[16,64,256]{2,1,0:T(8,128)S(1)}, u32[]{:S(2)}, u32[]{:S(2)}) async-start(f32[16,64,256]{2,1,0:T(8,128)} %get-tuple-element.24), calls=%async_computation | async-start | bytes 2097152 | tf_op jit(solution)/shard_map/all_to_all | solution.py:512
  95.7 3.1 %collective-permute-start.23 = (f32[1,64,256]{2,1,0:T(8,128)S(1)}, f32[1,64,256]{2,1,0:T(8,128)S(1)}, u32[]{:S(2)}, u32[]{:S(2)}) collective-permute-start(f32[1,64,256]{2,1,0:T(8,128)S(1)} %get-tuple-element.39), channel_id=1, source_target_pairs={{0,96},{16,112},{32,0},{48,16},{64,32},{80,48},{96,64},{112,80},{1... | collective-permute-start | bytes 196616 | tf_op jit(solution)/shard_map/ppermute | solution.py:524
  98.8 3.5 %collective-permute-done.25.c_ref = f32[1,64,256]{2,1,0:T(8,128)S(1)} collective-permute-done((f32[1,64,256]{2,1,0:T(8,128)S(1)}, f32[1,64,256]{2,1,0:T(8,128)S(1)}, u32[]{:S(2)}, u32[]{:S(2)}) %collective-permute-start.25) | collective-permute-done | bytes 65568 | tf_op jit(solution)/shard_map/ppermute | solution.py:524
  102.9 3.6 %all-to-all-done.rr_ref = f32[16,64,256]{2,1,0:T(8,128)S(1)} async-done(((f32[16,64,256]{2,1,0:T(8,128)}), f32[16,64,256]{2,1,0:T(8,128)S(1)}, u32[]{:S(2)}, u32[]{:S(2)}) %all-to-all-start) | async-done | bytes 1048608 | tf_op jit(solution)/shard_map/all_to_all | solution.py:512
  107.6 3.7 %all-to-all-start.1 = ((bf16[16,128,256]{2,1,0:T(8,128)(2,1)}), bf16[16,128,256]{2,1,0:T(8,128)(2,1)S(1)}, u32[]{:S(2)}, u32[]{:S(2)}) async-start(bf16[16,128,256]{2,1,0:T(8,128)(2,1)} %get-tuple-element.26), calls=%async_computation.1 | async-start | bytes 2097152 | tf_op jit(solution)/shard_map/all_to_all | solution.py:512
  116.2 3.3 %collective-permute-done.27 = bf16[128,256]{1,0:T(8,128)(2,1)S(1)} collective-permute-done((bf16[128,256]{1,0:T(8,128)(2,1)S(1)}, bf16[128,256]{1,0:T(8,128)(2,1)S(1)}, u32[]{:S(2)}, u32[]{:S(2)}) %collective-permute-start.27) | collective-permute-done | bytes 65568 | tf_op jit(solution)/shard_map/ppermute | solution.py:524
  121.8 6.0 %all-to-all-done.1.qr_ref = bf16[16,128,256]{2,1,0:T(8,128)(2,1)S(1)} async-done(((bf16[16,128,256]{2,1,0:T(8,128)(2,1)}), bf16[16,128,256]{2,1,0:T(8,128)(2,1)S(1)}, u32[]{:S(2)}, u32[]{:S(2)}) %all-to-all-start.1) | async-done | bytes 1048608 | tf_op jit(solution)/shard_map/all_to_all | solution.py:512
  127.8 5.9 %shard_map.72 = (f32[16,64,256]{2,1,0:T(8,128)}, f32[8,80,256]{2,1,0:T(8,128)S(1)}) custom-call(s32[2,32]{1,0:T(2,128)S(1)} %bitcast.33, s32[1,1]{1,0:T(1,128)S(6)} %copy.7.count, s32[4]{0:T(128)S(1)} %pad_add_fusion.place, bf16[288,256,256]{2,1,0:T(8,128)(2,1)} %get-tuple-element.23.tiles_ref, bf16[16,128,256]{2,1,0:T(8,128)(2,1)S(1)} %all-to-all-done.1.qr_ref, ...), custom_call_target="tpu_custom_call" | custom-call | flops 1000000000 | bytes 8388608 | tf_op jit(solution)/shard_map/pallas_call | solution.py:315
  133.7 3.7 %all-to-all-start.2 = ((f32[16,64,256]{2,1,0:T(8,128)}), f32[16,64,256]{2,1,0:T(8,128)S(1)}, u32[]{:S(2)}, u32[]{:S(2)}) async-start(f32[16,64,256]{2,1,0:T(8,128)} %get-tuple-element.28), calls=%async_computation.2 | async-start | bytes 2097152 | tf_op jit(solution)/shard_map/all_to_all | solution.py:512
  142.5 4.2 %collective-permute-done.33.c_ref = f32[1,80,256]{2,1,0:T(8,128)S(1)} collective-permute-done((f32[1,80,256]{2,1,0:T(8,128)S(1)}, f32[1,80,256]{2,1,0:T(8,128)S(1)}, u32[]{:S(2)}, u32[]{:S(2)}) %collective-permute-start.33) | collective-permute-done | bytes 81952 | tf_op jit(solution)/shard_map/ppermute | solution.py:524
  147.3 3.9 %all-to-all-done.2.rr_ref = f32[16,64,256]{2,1,0:T(8,128)S(1)} async-done(((f32[16,64,256]{2,1,0:T(8,128)}), f32[16,64,256]{2,1,0:T(8,128)S(1)}, u32[]{:S(2)}, u32[]{:S(2)}) %all-to-all-start.2) | async-done | bytes 1048608 | tf_op jit(solution)/shard_map/all_to_all | solution.py:512
  154.0 3.6 %all-to-all-start.3 = ((bf16[16,64,256]{2,1,0:T(8,128)(2,1)}), bf16[16,64,256]{2,1,0:T(8,128)(2,1)S(1)}, u32[]{:S(2)}, u32[]{:S(2)}) async-start(bf16[16,64,256]{2,1,0:T(8,128)(2,1)} %get-tuple-element.30), calls=%async_computation.3 | async-start | bytes 1048576 | tf_op jit(solution)/shard_map/all_to_all | solution.py:512
  157.6 3.5 %collective-permute-start.36 = (bf16[64,256]{1,0:T(8,128)(2,1)S(1)}, bf16[64,256]{1,0:T(8,128)(2,1)S(1)}, u32[]{:S(2)}, u32[]{:S(2)}) collective-permute-start(bf16[64,256]{1,0:T(8,128)(2,1)S(1)} %get-tuple-element.31), channel_id=1, source_target_pairs={{0,96},{16,112},{32,0},{48,16},{64,32},{80,48},{96,64},{112,80},{1... | collective-permute-start | bytes 98312 | tf_op jit(solution)/shard_map/ppermute | solution.py:524
  162.7 3.9 %collective-permute-done.35 = bf16[64,256]{1,0:T(8,128)(2,1)S(1)} collective-permute-done((bf16[64,256]{1,0:T(8,128)(2,1)S(1)}, bf16[64,256]{1,0:T(8,128)(2,1)S(1)}, u32[]{:S(2)}, u32[]{:S(2)}) %collective-permute-start.35) | collective-permute-done | bytes 32800 | tf_op jit(solution)/shard_map/ppermute | solution.py:524
  168.0 4.0 %shard_map.74 = f32[40,128]{1,0:T(8,128)S(1)} custom-call(s32[2,32]{1,0:T(2,128)S(1)} %bitcast.34, s32[1,1]{1,0:T(1,128)S(6)} %copy.7.count, s32[4]{0:T(128)S(1)} %pad_add_fusion.place, bf16[288,256,256]{2,1,0:T(8,128)(2,1)} %get-tuple-element.23.tiles_ref, bf16[16,64,256]{2,1,0:T(8,128)(2,1)S(1)} %all-to-all-done.3.qr_ref, ...), custom_call_target="tpu_custom_call" | custom-call | flops 500000000 | bytes 6291456 | tf_op jit(solution)/shard_map/pallas_call | solution.py:474
  192.6 3.3 %collective-permute-done.46.b_ref = f32[40,128]{1,0:T(8,128)S(1)} collective-permute-done((f32[40,128]{1,0:T(8,128)S(1)}, f32[40,128]{1,0:T(8,128)S(1)}, u32[]{:S(2)}, u32[]{:S(2)}) %collective-permute-start.46) | collective-permute-done | bytes 20512 | tf_op jit(solution)/shard_map/ppermute | solution.py:524
  (125 shorter events, 81.5 us)
Async XLA Ops:
  2.5 15.5 %collective-permute-start.2 = (bf16[576,256]{1,0:T(8,128)(2,1)S(1)}, bf16[576,256]{1,0:T(8,128)(2,1)S(1)}, u32[]{:S(2)}, u32[]{:S(2)}) collective-permute-start(bf16[576,256]{1,0:T(8,128)(2,1)S(1)} %get-tuple-element.18), channel_id=1, source_target_pairs={{0,96},{16,112},{32,0},{48,16},{64,32},{80,48},{96,64},{112,80},{1... | collective-permute-start | bytes 884744 | tf_op jit(solution)/shard_map/ppermute | solution.py:524
  5.4 12.6 %collective-permute-start.1 = (bf16[576,256]{1,0:T(8,128)(2,1)S(1)}, bf16[576,256]{1,0:T(8,128)(2,1)S(1)}, u32[]{:S(2)}, u32[]{:S(2)}) collective-permute-start(bf16[576,256]{1,0:T(8,128)(2,1)S(1)} %get-tuple-element.18), channel_id=1, source_target_pairs={{0,64},{16,80},{32,96},{48,112},{64,0},{80,16},{96,32},{112,48},{1... | collective-permute-start | bytes 884744 | tf_op jit(solution)/shard_map/ppermute | solution.py:524
  6.2 15.5 %collective-permute-start = (bf16[576,256]{1,0:T(8,128)(2,1)S(1)}, bf16[576,256]{1,0:T(8,128)(2,1)S(1)}, u32[]{:S(2)}, u32[]{:S(2)}) collective-permute-start(bf16[576,256]{1,0:T(8,128)(2,1)S(1)} %get-tuple-element.18), channel_id=1, source_target_pairs={{0,32},{16,48},{32,64},{48,80},{64,96},{80,112},{96,0},{112,16},{1... | collective-permute-start | bytes 884744 | tf_op jit(solution)/shard_map/ppermute | solution.py:524
  21.8 41.7 %collective-permute-start.3 = (bf16[4,576,256]{2,1,0:T(8,128)(2,1)S(1)}, bf16[4,576,256]{2,1,0:T(8,128)(2,1)S(1)}, u32[]{:S(2)}, u32[]{:S(2)}) collective-permute-start(bf16[4,576,256]{2,1,0:T(8,128)(2,1)S(1)} %pad_maximum_fusion.own_ref), channel_id=1, source_target_pairs={{0,16},{16,0},{32,48},{48,32},{64,80},{80,64},{96,112},{112,96},{1... | collective-permute-start | bytes 3538952 | tf_op jit(solution)/shard_map/ppermute | solution.py:524
  21.9 9.3 %collective-permute-start.13 = (bf16[144,512]{1,0:T(8,128)(2,1)S(1)}, bf16[144,512]{1,0:T(8,128)(2,1)S(1)}, u32[]{:S(2)}, u32[]{:S(2)}) collective-permute-start(bf16[144,512]{1,0:T(8,128)(2,1)S(1)} %get-tuple-element.22), channel_id=1, source_target_pairs={{0,4},{1,5},{2,6},{3,7},{4,8},{5,9},{6,10},{7,11},{8,12},{9,13},{1... | collective-permute-start | bytes 442376 | tf_op jit(solution)/shard_map/ppermute | solution.py:524
  23.6 9.8 %collective-permute-start.15 = (bf16[144,512]{1,0:T(8,128)(2,1)S(1)}, bf16[144,512]{1,0:T(8,128)(2,1)S(1)}, u32[]{:S(2)}, u32[]{:S(2)}) collective-permute-start(bf16[144,512]{1,0:T(8,128)(2,1)S(1)} %get-tuple-element.22), channel_id=1, source_target_pairs={{0,12},{1,13},{2,14},{3,15},{4,0},{5,1},{6,2},{7,3},{8,4},{9,5},{1... | collective-permute-start | bytes 442376 | tf_op jit(solution)/shard_map/ppermute | solution.py:524
  25.2 9.1 %collective-permute-start.14 = (bf16[144,512]{1,0:T(8,128)(2,1)S(1)}, bf16[144,512]{1,0:T(8,128)(2,1)S(1)}, u32[]{:S(2)}, u32[]{:S(2)}) collective-permute-start(bf16[144,512]{1,0:T(8,128)(2,1)S(1)} %get-tuple-element.22), channel_id=1, source_target_pairs={{0,8},{1,9},{2,10},{3,11},{4,12},{5,13},{6,14},{7,15},{8,0},{9,1},... | collective-permute-start | bytes 442376 | tf_op jit(solution)/shard_map/ppermute | solution.py:524
  27.2 9.8 %collective-permute-start.6 = (bf16[144,512]{1,0:T(8,128)(2,1)S(1)}, bf16[144,512]{1,0:T(8,128)(2,1)S(1)}, u32[]{:S(2)}, u32[]{:S(2)}) collective-permute-start(bf16[144,512]{1,0:T(8,128)(2,1)S(1)} %get-tuple-element.21), channel_id=1, source_target_pairs={{0,3},{1,0},{2,1},{3,2},{4,7},{5,4},{6,5},{7,6},{8,11},{9,8},{10,9... | collective-permute-start | bytes 442376 | tf_op jit(solution)/shard_map/ppermute | solution.py:524
  31.3 10.0 %collective-permute-start.5 = (bf16[144,512]{1,0:T(8,128)(2,1)S(1)}, bf16[144,512]{1,0:T(8,128)(2,1)S(1)}, u32[]{:S(2)}, u32[]{:S(2)}) collective-permute-start(bf16[144,512]{1,0:T(8,128)(2,1)S(1)} %get-tuple-element.21), channel_id=1, source_target_pairs={{0,2},{1,3},{2,0},{3,1},{4,6},{5,7},{6,4},{7,5},{8,10},{9,11},{10,... | collective-permute-start | bytes 442376 | tf_op jit(solution)/shard_map/ppermute | solution.py:524
  33.4 14.9 %collective-permute-start.21 = (bf16[2,144,512]{2,1,0:T(8,128)(2,1)S(1)}, bf16[2,144,512]{2,1,0:T(8,128)(2,1)S(1)}, u32[]{:S(2)}, u32[]{:S(2)}) collective-permute-start(bf16[2,144,512]{2,1,0:T(8,128)(2,1)S(1)} %pad_maximum_fusion.3.rest_8_), channel_id=1, source_target_pairs={{0,3},{1,0},{2,1},{3,2},{4,7},{5,4},{6,5},{7,6},{8,11},{9,8},{10,9... | collective-permute-start | bytes 884744 | tf_op jit(solution)/shard_map/ppermute | solution.py:524
  34.3 16.7 %collective-permute-start.16 = (bf16[2,144,512]{2,1,0:T(8,128)(2,1)S(1)}, bf16[2,144,512]{2,1,0:T(8,128)(2,1)}, u32[]{:S(2)}, u32[]{:S(2)}) collective-permute-start(bf16[2,144,512]{2,1,0:T(8,128)(2,1)S(1)} %pad_maximum_fusion.3.rest_8_), channel_id=1, source_target_pairs={{0,1},{1,2},{2,3},{3,0},{4,5},{5,6},{6,7},{7,4},{8,9},{9,10},{10,1... | collective-permute-start | bytes 884744 | tf_op jit(solution)/shard_map/ppermute | solution.py:524
  37.1 13.9 %collective-permute-start.19 = (bf16[2,144,512]{2,1,0:T(8,128)(2,1)S(1)}, bf16[2,144,512]{2,1,0:T(8,128)(2,1)}, u32[]{:S(2)}, u32[]{:S(2)}) collective-permute-start(bf16[2,144,512]{2,1,0:T(8,128)(2,1)S(1)} %pad_maximum_fusion.4.rest_9_), channel_id=1, source_target_pairs={{0,3},{1,0},{2,1},{3,2},{4,7},{5,4},{6,5},{7,6},{8,11},{9,8},{10,9... | collective-permute-start | bytes 884744 | tf_op jit(solution)/shard_map/ppermute | solution.py:524
  47.7 8.8 %collective-permute-start.17 = (bf16[2,144,512]{2,1,0:T(8,128)(2,1)S(1)}, bf16[2,144,512]{2,1,0:T(8,128)(2,1)S(1)}, u32[]{:S(2)}, u32[]{:S(2)}) collective-permute-start(bf16[2,144,512]{2,1,0:T(8,128)(2,1)S(1)} %pad_maximum_fusion.4.rest_9_), channel_id=1, source_target_pairs={{0,1},{1,2},{2,3},{3,0},{4,5},{5,6},{6,7},{7,4},{8,9},{9,10},{10,1... | collective-permute-start | bytes 884744 | tf_op jit(solution)/shard_map/ppermute | solution.py:524
  49.0 9.9 %collective-permute-start.12 = (bf16[2,144,512]{2,1,0:T(8,128)(2,1)S(1)}, bf16[2,144,512]{2,1,0:T(8,128)(2,1)S(1)}, u32[]{:S(2)}, u32[]{:S(2)}) collective-permute-start(bf16[2,144,512]{2,1,0:T(8,128)(2,1)S(1)} %pad_maximum_fusion.1.rest_0_), channel_id=1, source_target_pairs={{0,12},{1,13},{2,14},{3,15},{4,0},{5,1},{6,2},{7,3},{8,4},{9,5},{1... | collective-permute-start | bytes 884744 | tf_op jit(solution)/shard_map/ppermute | solution.py:524
  51.0 10.3 %collective-permute-start.7 = (bf16[2,144,512]{2,1,0:T(8,128)(2,1)S(1)}, bf16[2,144,512]{2,1,0:T(8,128)(2,1)}, u32[]{:S(2)}, u32[]{:S(2)}) collective-permute-start(bf16[2,144,512]{2,1,0:T(8,128)(2,1)S(1)} %pad_maximum_fusion.1.rest_0_), channel_id=1, source_target_pairs={{0,4},{1,5},{2,6},{3,7},{4,8},{5,9},{6,10},{7,11},{8,12},{9,13},{1... | collective-permute-start | bytes 884744 | tf_op jit(solution)/shard_map/ppermute | solution.py:524
  51.0 12.4 %collective-permute-start.10 = (bf16[2,144,512]{2,1,0:T(8,128)(2,1)S(1)}, bf16[2,144,512]{2,1,0:T(8,128)(2,1)}, u32[]{:S(2)}, u32[]{:S(2)}) collective-permute-start(bf16[2,144,512]{2,1,0:T(8,128)(2,1)S(1)} %pad_maximum_fusion.2.rest_1_), channel_id=1, source_target_pairs={{0,12},{1,13},{2,14},{3,15},{4,0},{5,1},{6,2},{7,3},{8,4},{9,5},{1... | collective-permute-start | bytes 884744 | tf_op jit(solution)/shard_map/ppermute | solution.py:524
  57.2 12.9 %collective-permute-start.8 = (bf16[2,144,512]{2,1,0:T(8,128)(2,1)S(1)}, bf16[2,144,512]{2,1,0:T(8,128)(2,1)}, u32[]{:S(2)}, u32[]{:S(2)}) collective-permute-start(bf16[2,144,512]{2,1,0:T(8,128)(2,1)S(1)} %pad_maximum_fusion.2.rest_1_), channel_id=1, source_target_pairs={{0,4},{1,5},{2,6},{3,7},{4,8},{5,9},{6,10},{7,11},{8,12},{9,13},{1... | collective-permute-start | bytes 884744 | tf_op jit(solution)/shard_map/ppermute | solution.py:524
  59.6 10.6 %collective-permute-start.18 = (bf16[2,144,512]{2,1,0:T(8,128)(2,1)}, bf16[2,144,512]{2,1,0:T(8,128)(2,1)}, u32[]{:S(2)}, u32[]{:S(2)}) collective-permute-start(bf16[2,144,512]{2,1,0:T(8,128)(2,1)} %collective-permute-done.16.rest_10_), channel_id=1, source_target_pairs={{0,1},{1,2},{2,3},{3,0},{4,5},{5,6},{6,7},{7,4},{8,9},{9,10},{10,1... | collective-permute-start | bytes 884744 | tf_op jit(solution)/shard_map/ppermute | solution.py:524
  61.3 8.9 %collective-permute-start.20 = (bf16[2,144,512]{2,1,0:T(8,128)(2,1)}, bf16[2,144,512]{2,1,0:T(8,128)(2,1)}, u32[]{:S(2)}, u32[]{:S(2)}) collective-permute-start(bf16[2,144,512]{2,1,0:T(8,128)(2,1)} %collective-permute-done.19.rest_15_), channel_id=1, source_target_pairs={{0,3},{1,0},{2,1},{3,2},{4,7},{5,4},{6,5},{7,6},{8,11},{9,8},{10,9... | collective-permute-start | bytes 884744 | tf_op jit(solution)/shard_map/ppermute | solution.py:524
  63.4 8.7 %collective-permute-start.9 = (bf16[2,144,512]{2,1,0:T(8,128)(2,1)}, bf16[2,144,512]{2,1,0:T(8,128)(2,1)}, u32[]{:S(2)}, u32[]{:S(2)}) collective-permute-start(bf16[2,144,512]{2,1,0:T(8,128)(2,1)} %collective-permute-done.7.rest_2_), channel_id=1, source_target_pairs={{0,4},{1,5},{2,6},{3,7},{4,8},{5,9},{6,10},{7,11},{8,12},{9,13},{1... | collective-permute-start | bytes 884744 | tf_op jit(solution)/shard_map/ppermute | solution.py:524
  89.4 17.2 %all-to-all-start = ((f32[16,64,256]{2,1,0:T(8,128)}), f32[16,64,256]{2,1,0:T(8,128)S(1)}, u32[]{:S(2)}, u32[]{:S(2)}) async-start(f32[16,64,256]{2,1,0:T(8,128)} %get-tuple-element.24), calls=%async_computation | async-start | bytes 2097152 | tf_op jit(solution)/shard_map/all_to_all | solution.py:512
  107.6 20.2 %all-to-all-start.1 = ((bf16[16,128,256]{2,1,0:T(8,128)(2,1)}), bf16[16,128,256]{2,1,0:T(8,128)(2,1)S(1)}, u32[]{:S(2)}, u32[]{:S(2)}) async-start(bf16[16,128,256]{2,1,0:T(8,128)(2,1)} %get-tuple-element.26), calls=%async_computation.1 | async-start | bytes 2097152 | tf_op jit(solution)/shard_map/all_to_all | solution.py:512
  133.7 17.5 %all-to-all-start.2 = ((f32[16,64,256]{2,1,0:T(8,128)}), f32[16,64,256]{2,1,0:T(8,128)S(1)}, u32[]{:S(2)}, u32[]{:S(2)}) async-start(f32[16,64,256]{2,1,0:T(8,128)} %get-tuple-element.28), calls=%async_computation.2 | async-start | bytes 2097152 | tf_op jit(solution)/shard_map/all_to_all | solution.py:512
  154.0 14.0 %all-to-all-start.3 = ((bf16[16,64,256]{2,1,0:T(8,128)(2,1)}), bf16[16,64,256]{2,1,0:T(8,128)(2,1)S(1)}, u32[]{:S(2)}, u32[]{:S(2)}) async-start(bf16[16,64,256]{2,1,0:T(8,128)(2,1)} %get-tuple-element.30), calls=%async_computation.3 | async-start | bytes 1048576 | tf_op jit(solution)/shard_map/all_to_all | solution.py:512
  (38 other events, 168.2 us)

commit v4 on v3

--- a/solution.py
+++ b/solution.py
@@ -66,8 +66,11 @@
     )(series, start)
 
 
+EDGE = 16
+
+
 def shift_body(own_ref, other_ref, out_ref, xc_ref):
-    day = lax.broadcasted_iota(jnp.int32, (DAYS, BLOCK), 0)
+    day = lax.broadcasted_iota(jnp.int32, (EDGE, BLOCK), 0)
     for core, ref in enumerate((own_ref, other_ref)):
 
         def one(step, carry, core=core, ref=ref):
@@ -75,9 +78,12 @@
             x = ref[step, :DAYS].astype(F32) * (BETA_CORR / DAYS)
             out_ref[block, 0] = (x + x).astype(BF16)
             for lag in range(1, LAGS):
-                later = jnp.where(day < DAYS - lag, pltpu.roll(x, DAYS - lag, 0), 0.0)
-                earlier = jnp.where(day >= lag, pltpu.roll(x, lag, 0), 0.0)
-                out_ref[block, lag] = (later + earlier).astype(BF16)
+                later, earlier = pltpu.roll(x, DAYS - lag, 0), pltpu.roll(x, lag, 0)
+                total = later + earlier
+                head = jnp.where(day < lag, later[:EDGE], total[:EDGE])
+                tail = jnp.where(day >= EDGE - lag, earlier[DAYS - EDGE :], total[DAYS - EDGE :])
+                total = jnp.concatenate([head, total[EDGE : DAYS - EDGE], tail], axis=0)
+                out_ref[block, lag] = total.astype(BF16)
             xc_ref[block] = ref[step, DAYS:]
             return carry
 
@@ -483,8 +489,22 @@
     )(*table, tiles, qr, near, far, gram)
 
 
-def finish_body(own_ref, a_ref, b_ref, c_ref, p_ref, basis_ref, form_ref):
+def respread_body(own_ref, a_ref, b_ref, c_ref, out_ref):
     total = sum_of_four(own_ref[...], a_ref[...], b_ref[...], c_ref[...])
+    for k in range(N_COL):
+        out_ref[k] = total
+
+
+def respread(parts):
+    return call(
+        respread_body, shape(N_COL, PACKED, 2 * RANK), [VMEM] * 4, 100_000, 1 << 19, 4
+    )(*parts)
+
+
+def finish_body(parts_ref, p_ref, basis_ref, form_ref):
+    total = parts_ref[0]
+    for k in range(1, N_COL):
+        total = total + parts_ref[k]
     top = total[: RANK // 2]
     packed = jnp.concatenate([top[:, :RANK], top[:, RANK:]], axis=0)
     lower = jnp.where(row_less_col(False), 0.0, packed)
@@ -504,8 +524,8 @@
 
 def finish(parts, p):
     return call(
-        finish_body, [shape(RANK, BLOCK), shape(RANK, RANK)], [VMEM] * 5, 10_000_000, 1 << 20, 6
-    )(*parts, p)
+        finish_body, [shape(RANK, BLOCK), shape(RANK, RANK)], [VMEM] * 2, 10_000_000, 1 << 20, 6
+    )(parts, p)
 
 
 def swap(x, axis):
@@ -566,9 +586,7 @@
     p2, q2, wide, gram = mid2(*scatter(rows, cols))
     part = project(table, tiles, *gather(q2, wide), gram)
     part = part + shift(part, "core", 1)
-    part = sum_of_four(*around(part, "x"))
-    part = sum_of_four(*around(part, "z"))
-    return finish(around(part, "y"), p2)
+    return finish(swap(respread(around(part, "x")), "col"), p2)
 
 
 def solution(mesh):

time: 200 us -> 199 us (level)
  the two profiles are of different devices: /device:TPU:0 before, /device:TPU:1 now
where the time goes in v4:
time: 199 us; the launch traced here: 196 us
  starting transfers between devices  86.5 us (43%)
  waiting for transfers between devices  60 us (30%)
  Pallas kernels  30.2 us (15%)
  blocking collectives  13.7 us (7%)
  local copies, waits for them, and re-layouts  3.91 us (2%)
    ppermute x42, starting transfers between devices, shift(): return lax.ppermute(x, 'row' if axis in ('x', 'core') else 'col', pairs)  63.8 us
    ppermute x42, waiting for transfers between devices, shift(): return lax.ppermute(x, 'row' if axis in ('x', 'core') else 'col', pairs)  56.6 us
    all_to_all x4, starting transfers between devices, swap(): return lax.all_to_all(x, axis, 0, 0, tiled=True)  22.7 us
    all_to_all x1, blocking collectives, swap(): return lax.all_to_all(x, axis, 0, 0, tiled=True)  13.7 us
    pallas_call x1, Pallas kernels, build(): call(build_body, [shape(TILE_ROOM, BLOCK, BLOCK, dtype=BF16), shape(N_COL...  12.4 us
    pallas_call x1, Pallas kernels, product(): call(product_body, [shape(N_COL, RANK, BLOCK), shape(N_ROW, RANK + 16, BL...  4.7 us
  transfers between devices with their start and end apart: 46, of which 24 were waited for; matrix products, arithmetic and copies ran while one was open for 0% of the time, Pallas kernels for 1%

profile of v4, /device:TPU:1, one launch (start us, length us, event | category | flops | bytes accessed | tf_op | source)
XLA Modules:
  0.0 196.4 jit_solution(11933524812869712631)
XLA Ops:
  2.5 3.4 %collective-permute-start.2 = (bf16[576,256]{1,0:T(8,128)(2,1)S(1)}, bf16[576,256]{1,0:T(8,128)(2,1)S(1)}, u32[]{:S(2)}, u32[]{:S(2)}) collective-permute-start(bf16[576,256]{1,0:T(8,128)(2,1)S(1)} %get-tuple-element.18), channel_id=1, source_target_pairs={{0,96},{16,112},{32,0},{48,16},{64,32},{80,48},{96,64},{112,80},{1... | collective-permute-start | bytes 884744 | tf_op jit(solution)/shard_map/ppermute | solution.py:544
  7.0 5.7 %collective-permute-done.2 = bf16[576,256]{1,0:T(8,128)(2,1)S(1)} collective-permute-done((bf16[576,256]{1,0:T(8,128)(2,1)S(1)}, bf16[576,256]{1,0:T(8,128)(2,1)S(1)}, u32[]{:S(2)}, u32[]{:S(2)}) %collective-permute-start.2) | collective-permute-done | bytes 294944 | tf_op jit(solution)/shard_map/ppermute | solution.py:544
  15.0 7.6 %collective-permute-done = bf16[576,256]{1,0:T(8,128)(2,1)S(1)} collective-permute-done((bf16[576,256]{1,0:T(8,128)(2,1)S(1)}, bf16[576,256]{1,0:T(8,128)(2,1)S(1)}, u32[]{:S(2)}, u32[]{:S(2)}) %collective-permute-start) | collective-permute-done | bytes 294944 | tf_op jit(solution)/shard_map/ppermute | solution.py:544
  27.7 3.8 %collective-permute-start.6 = (bf16[144,512]{1,0:T(8,128)(2,1)S(1)}, bf16[144,512]{1,0:T(8,128)(2,1)S(1)}, u32[]{:S(2)}, u32[]{:S(2)}) collective-permute-start(bf16[144,512]{1,0:T(8,128)(2,1)S(1)} %get-tuple-element.21), channel_id=1, source_target_pairs={{0,3},{1,0},{2,1},{3,2},{4,7},{5,4},{6,5},{7,6},{8,11},{9,8},{10,9... | collective-permute-start | bytes 442376 | tf_op jit(solution)/shard_map/ppermute | solution.py:544
  39.1 8.2 %collective-permute-done.4 = bf16[144,512]{1,0:T(8,128)(2,1)S(1)} collective-permute-done((bf16[144,512]{1,0:T(8,128)(2,1)S(1)}, bf16[144,512]{1,0:T(8,128)(2,1)S(1)}, u32[]{:S(2)}, u32[]{:S(2)}) %collective-permute-start.4) | collective-permute-done | bytes 147488 | tf_op jit(solution)/shard_map/ppermute | solution.py:544
  52.3 2.9 %collective-permute-done.17.rest_11_ = bf16[2,144,512]{2,1,0:T(8,128)(2,1)S(1)} collective-permute-done((bf16[2,144,512]{2,1,0:T(8,128)(2,1)S(1)}, bf16[2,144,512]{2,1,0:T(8,128)(2,1)S(1)}, u32[]{:S(2)}, u32[]{:S(2)}) %collective-permute-start.17) | collective-permute-done | bytes 294944 | tf_op jit(solution)/shard_map/ppermute | solution.py:544
  59.5 3.0 %collective-permute-done.10.rest_7_ = bf16[2,144,512]{2,1,0:T(8,128)(2,1)} collective-permute-done((bf16[2,144,512]{2,1,0:T(8,128)(2,1)S(1)}, bf16[2,144,512]{2,1,0:T(8,128)(2,1)}, u32[]{:S(2)}, u32[]{:S(2)}) %collective-permute-start.10) | collective-permute-done | bytes 294944 | tf_op jit(solution)/shard_map/ppermute | solution.py:544
  70.4 12.4 %shard_map.70 = (bf16[288,256,256]{2,1,0:T(8,128)(2,1)}, f32[16,64,256]{2,1,0:T(8,128)}, f32[8,64,256]{2,1,0:T(8,128)S(1)}) custom-call(s32[2,32]{1,0:T(2,128)S(1)} %bitcast.32, s32[1,1]{1,0:T(1,128)S(6)} %copy.7.count, s32[4]{0:T(128)S(1)} %pad_add_fusion.place, f32[4]{0:T(128)S(1)} %copy-done.9, bf16[8,4,512,256]{3,2,1,0:T(8,128)(2,1)S(1)} %get-tuple-element.19.sums_ref, ...), custom_call_target="tpu_custom_call" | custom-call | flops 8999999488 | bytes 20971520 | tf_op jit(solution)/shard_map/pallas_call | solution.py:210
  82.8 5.2 %all-to-all-start = ((f32[16,64,256]{2,1,0:T(8,128)}), f32[16,64,256]{2,1,0:T(8,128)S(1)}, u32[]{:S(2)}, u32[]{:S(2)}) async-start(f32[16,64,256]{2,1,0:T(8,128)} %get-tuple-element.24), calls=%async_computation | async-start | bytes 2097152 | tf_op jit(solution)/shard_map/all_to_all | solution.py:532
  88.0 7.2 %collective-permute-start.22 = (f32[4,64,256]{2,1,0:T(8,128)S(1)}, f32[4,64,256]{2,1,0:T(8,128)S(1)}, u32[]{:S(2)}, u32[]{:S(2)}) collective-permute-start(f32[4,64,256]{2,1,0:T(8,128)S(1)} %slice.31), channel_id=1, source_target_pairs={{0,16},{16,0},{32,48},{48,32},{64,80},{80,64},{96,112},{112,96},{1... | collective-permute-start | bytes 786440 | tf_op jit(solution)/shard_map/ppermute | solution.py:544
  99.2 3.6 %collective-permute-done.25.c_ref = f32[1,64,256]{2,1,0:T(8,128)S(1)} collective-permute-done((f32[1,64,256]{2,1,0:T(8,128)S(1)}, f32[1,64,256]{2,1,0:T(8,128)S(1)}, u32[]{:S(2)}, u32[]{:S(2)}) %collective-permute-start.25) | collective-permute-done | bytes 65568 | tf_op jit(solution)/shard_map/ppermute | solution.py:544
  103.9 6.9 %all-to-all-start.1 = ((bf16[16,128,256]{2,1,0:T(8,128)(2,1)}), bf16[16,128,256]{2,1,0:T(8,128)(2,1)S(1)}, u32[]{:S(2)}, u32[]{:S(2)}) async-start(bf16[16,128,256]{2,1,0:T(8,128)(2,1)} %get-tuple-element.26), calls=%async_computation.1 | async-start | bytes 2097152 | tf_op jit(solution)/shard_map/all_to_all | solution.py:532
  115.1 3.0 %collective-permute-done.27 = bf16[128,256]{1,0:T(8,128)(2,1)S(1)} collective-permute-done((bf16[128,256]{1,0:T(8,128)(2,1)S(1)}, bf16[128,256]{1,0:T(8,128)(2,1)S(1)}, u32[]{:S(2)}, u32[]{:S(2)}) %collective-permute-start.27) | collective-permute-done | bytes 65568 | tf_op jit(solution)/shard_map/ppermute | solution.py:544
  118.6 3.0 %collective-permute-start.29 = (bf16[4,128,256]{2,1,0:T(8,128)(2,1)S(1)}, bf16[4,128,256]{2,1,0:T(8,128)(2,1)S(1)}, u32[]{:S(2)}, u32[]{:S(2)}) collective-permute-start(bf16[4,128,256]{2,1,0:T(8,128)(2,1)S(1)} %pad_maximum_fusion.5.near_ref), channel_id=1, source_target_pairs={{0,16},{16,0},{32,48},{48,32},{64,80},{80,64},{96,112},{112,96},{1... | collective-permute-start | bytes 786440 | tf_op jit(solution)/shard_map/ppermute | solution.py:544
  122.7 3.4 %all-to-all-done.1.qr_ref = bf16[16,128,256]{2,1,0:T(8,128)(2,1)S(1)} async-done(((bf16[16,128,256]{2,1,0:T(8,128)(2,1)}), bf16[16,128,256]{2,1,0:T(8,128)(2,1)S(1)}, u32[]{:S(2)}, u32[]{:S(2)}) %all-to-all-start.1) | async-done | bytes 1048608 | tf_op jit(solution)/shard_map/all_to_all | solution.py:532
  126.1 4.7 %shard_map.72 = (f32[16,64,256]{2,1,0:T(8,128)}, f32[8,80,256]{2,1,0:T(8,128)S(1)}) custom-call(s32[2,32]{1,0:T(2,128)S(1)} %bitcast.33, s32[1,1]{1,0:T(1,128)S(6)} %copy.7.count, s32[4]{0:T(128)S(1)} %pad_add_fusion.place, bf16[288,256,256]{2,1,0:T(8,128)(2,1)} %get-tuple-element.23.tiles_ref, bf16[16,128,256]{2,1,0:T(8,128)(2,1)S(1)} %all-to-all-done.1.qr_ref, ...), custom_call_target="tpu_custom_call" | custom-call | flops 1000000000 | bytes 8388608 | tf_op jit(solution)/shard_map/pallas_call | solution.py:321
  130.8 3.7 %all-to-all-start.2 = ((f32[16,64,256]{2,1,0:T(8,128)}), f32[16,64,256]{2,1,0:T(8,128)S(1)}, u32[]{:S(2)}, u32[]{:S(2)}) async-start(f32[16,64,256]{2,1,0:T(8,128)} %get-tuple-element.28), calls=%async_computation.2 | async-start | bytes 2097152 | tf_op jit(solution)/shard_map/all_to_all | solution.py:532
  134.5 4.3 %collective-permute-start.30 = (f32[4,80,256]{2,1,0:T(8,128)S(1)}, f32[4,80,256]{2,1,0:T(8,128)S(1)}, u32[]{:S(2)}, u32[]{:S(2)}) collective-permute-start(f32[4,80,256]{2,1,0:T(8,128)S(1)} %slice.36), channel_id=1, source_target_pairs={{0,16},{16,0},{32,48},{48,32},{64,80},{80,64},{96,112},{112,96},{1... | collective-permute-start | bytes 983048 | tf_op jit(solution)/shard_map/ppermute | solution.py:544
  142.9 4.3 %collective-permute-done.33.c_ref = f32[1,80,256]{2,1,0:T(8,128)S(1)} collective-permute-done((f32[1,80,256]{2,1,0:T(8,128)S(1)}, f32[1,80,256]{2,1,0:T(8,128)S(1)}, u32[]{:S(2)}, u32[]{:S(2)}) %collective-permute-start.33) | collective-permute-done | bytes 81952 | tf_op jit(solution)/shard_map/ppermute | solution.py:544
  150.0 6.9 %all-to-all-start.3 = ((bf16[16,64,256]{2,1,0:T(8,128)(2,1)}), bf16[16,64,256]{2,1,0:T(8,128)(2,1)S(1)}, u32[]{:S(2)}, u32[]{:S(2)}) async-start(bf16[16,64,256]{2,1,0:T(8,128)(2,1)} %get-tuple-element.30), calls=%async_computation.3 | async-start | bytes 1048576 | tf_op jit(solution)/shard_map/all_to_all | solution.py:532
  160.8 3.3 %collective-permute-done.35 = bf16[64,256]{1,0:T(8,128)(2,1)S(1)} collective-permute-done((bf16[64,256]{1,0:T(8,128)(2,1)S(1)}, bf16[64,256]{1,0:T(8,128)(2,1)S(1)}, u32[]{:S(2)}, u32[]{:S(2)}) %collective-permute-start.35) | collective-permute-done | bytes 32800 | tf_op jit(solution)/shard_map/ppermute | solution.py:544
  164.1 3.9 %collective-permute-start.37 = (bf16[4,64,256]{2,1,0:T(8,128)(2,1)S(1)}, bf16[4,64,256]{2,1,0:T(8,128)(2,1)S(1)}, u32[]{:S(2)}, u32[]{:S(2)}) collective-permute-start(bf16[4,64,256]{2,1,0:T(8,128)(2,1)S(1)} %pad_maximum_fusion.6.near_ref), channel_id=1, source_target_pairs={{0,16},{16,0},{32,48},{48,32},{64,80},{80,64},{96,112},{112,96},{1... | collective-permute-start | bytes 393224 | tf_op jit(solution)/shard_map/ppermute | solution.py:544
  169.0 3.3 %shard_map.74 = f32[40,128]{1,0:T(8,128)S(1)} custom-call(s32[2,32]{1,0:T(2,128)S(1)} %bitcast.34, s32[1,1]{1,0:T(1,128)S(6)} %copy.7.count, s32[4]{0:T(128)S(1)} %pad_add_fusion.place, bf16[288,256,256]{2,1,0:T(8,128)(2,1)} %get-tuple-element.23.tiles_ref, bf16[16,64,256]{2,1,0:T(8,128)(2,1)S(1)} %all-to-all-done.3.qr_ref, ...), custom_call_target="tpu_custom_call" | custom-call | flops 500000000 | bytes 6291456 | tf_op jit(solution)/shard_map/pallas_call | solution.py:480
  179.7 13.7 %all_to_all.25.parts_ref = f32[16,40,128]{2,1,0:T(8,128)S(1)} all-to-all(f32[16,40,128]{2,1,0:T(8,128)S(1)} %shard_map.75), channel_id=1, replica_groups=mesh['row'=8,'col'=16] {'col'}, dimensions={0} | all-to-all | bytes 655360 | tf_op jit(solution)/shard_map/all_to_all | solution.py:532
  (113 shorter events, 67.4 us)
Async XLA Ops:
  2.5 10.2 %collective-permute-start.2 = (bf16[576,256]{1,0:T(8,128)(2,1)S(1)}, bf16[576,256]{1,0:T(8,128)(2,1)S(1)}, u32[]{:S(2)}, u32[]{:S(2)}) collective-permute-start(bf16[576,256]{1,0:T(8,128)(2,1)S(1)} %get-tuple-element.18), channel_id=1, source_target_pairs={{0,96},{16,112},{32,0},{48,16},{64,32},{80,48},{96,64},{112,80},{1... | collective-permute-start | bytes 884744 | tf_op jit(solution)/shard_map/ppermute | solution.py:544
  5.8 9.2 %collective-permute-start.1 = (bf16[576,256]{1,0:T(8,128)(2,1)S(1)}, bf16[576,256]{1,0:T(8,128)(2,1)S(1)}, u32[]{:S(2)}, u32[]{:S(2)}) collective-permute-start(bf16[576,256]{1,0:T(8,128)(2,1)S(1)} %get-tuple-element.18), channel_id=1, source_target_pairs={{0,64},{16,80},{32,96},{48,112},{64,0},{80,16},{96,32},{112,48},{1... | collective-permute-start | bytes 884744 | tf_op jit(solution)/shard_map/ppermute | solution.py:544
  6.3 16.2 %collective-permute-start = (bf16[576,256]{1,0:T(8,128)(2,1)S(1)}, bf16[576,256]{1,0:T(8,128)(2,1)S(1)}, u32[]{:S(2)}, u32[]{:S(2)}) collective-permute-start(bf16[576,256]{1,0:T(8,128)(2,1)S(1)} %get-tuple-element.18), channel_id=1, source_target_pairs={{0,32},{16,48},{32,64},{48,80},{64,96},{80,112},{96,0},{112,16},{1... | collective-permute-start | bytes 884744 | tf_op jit(solution)/shard_map/ppermute | solution.py:544
  22.7 39.8 %collective-permute-start.3 = (bf16[4,576,256]{2,1,0:T(8,128)(2,1)S(1)}, bf16[4,576,256]{2,1,0:T(8,128)(2,1)S(1)}, u32[]{:S(2)}, u32[]{:S(2)}) collective-permute-start(bf16[4,576,256]{2,1,0:T(8,128)(2,1)S(1)} %pad_maximum_fusion.own_ref), channel_id=1, source_target_pairs={{0,16},{16,0},{32,48},{48,32},{64,80},{80,64},{96,112},{112,96},{1... | collective-permute-start | bytes 3538952 | tf_op jit(solution)/shard_map/ppermute | solution.py:544
  23.3 8.1 %collective-permute-start.13 = (bf16[144,512]{1,0:T(8,128)(2,1)S(1)}, bf16[144,512]{1,0:T(8,128)(2,1)S(1)}, u32[]{:S(2)}, u32[]{:S(2)}) collective-permute-start(bf16[144,512]{1,0:T(8,128)(2,1)S(1)} %get-tuple-element.22), channel_id=1, source_target_pairs={{0,4},{1,5},{2,6},{3,7},{4,8},{5,9},{6,10},{7,11},{8,12},{9,13},{1... | collective-permute-start | bytes 442376 | tf_op jit(solution)/shard_map/ppermute | solution.py:544
  24.6 9.0 %collective-permute-start.15 = (bf16[144,512]{1,0:T(8,128)(2,1)S(1)}, bf16[144,512]{1,0:T(8,128)(2,1)S(1)}, u32[]{:S(2)}, u32[]{:S(2)}) collective-permute-start(bf16[144,512]{1,0:T(8,128)(2,1)S(1)} %get-tuple-element.22), channel_id=1, source_target_pairs={{0,12},{1,13},{2,14},{3,15},{4,0},{5,1},{6,2},{7,3},{8,4},{9,5},{1... | collective-permute-start | bytes 442376 | tf_op jit(solution)/shard_map/ppermute | solution.py:544
  26.0 8.2 %collective-permute-start.14 = (bf16[144,512]{1,0:T(8,128)(2,1)S(1)}, bf16[144,512]{1,0:T(8,128)(2,1)S(1)}, u32[]{:S(2)}, u32[]{:S(2)}) collective-permute-start(bf16[144,512]{1,0:T(8,128)(2,1)S(1)} %get-tuple-element.22), channel_id=1, source_target_pairs={{0,8},{1,9},{2,10},{3,11},{4,12},{5,13},{6,14},{7,15},{8,0},{9,1},... | collective-permute-start | bytes 442376 | tf_op jit(solution)/shard_map/ppermute | solution.py:544
  27.7 8.2 %collective-permute-start.6 = (bf16[144,512]{1,0:T(8,128)(2,1)S(1)}, bf16[144,512]{1,0:T(8,128)(2,1)S(1)}, u32[]{:S(2)}, u32[]{:S(2)}) collective-permute-start(bf16[144,512]{1,0:T(8,128)(2,1)S(1)} %get-tuple-element.21), channel_id=1, source_target_pairs={{0,3},{1,0},{2,1},{3,2},{4,7},{5,4},{6,5},{7,6},{8,11},{9,8},{10,9... | collective-permute-start | bytes 442376 | tf_op jit(solution)/shard_map/ppermute | solution.py:544
  33.6 14.6 %collective-permute-start.21 = (bf16[2,144,512]{2,1,0:T(8,128)(2,1)S(1)}, bf16[2,144,512]{2,1,0:T(8,128)(2,1)S(1)}, u32[]{:S(2)}, u32[]{:S(2)}) collective-permute-start(bf16[2,144,512]{2,1,0:T(8,128)(2,1)S(1)} %pad_maximum_fusion.3.rest_8_), channel_id=1, source_target_pairs={{0,3},{1,0},{2,1},{3,2},{4,7},{5,4},{6,5},{7,6},{8,11},{9,8},{10,9... | collective-permute-start | bytes 884744 | tf_op jit(solution)/shard_map/ppermute | solution.py:544
  34.2 15.4 %collective-permute-start.16 = (bf16[2,144,512]{2,1,0:T(8,128)(2,1)S(1)}, bf16[2,144,512]{2,1,0:T(8,128)(2,1)}, u32[]{:S(2)}, u32[]{:S(2)}) collective-permute-start(bf16[2,144,512]{2,1,0:T(8,128)(2,1)S(1)} %pad_maximum_fusion.3.rest_8_), channel_id=1, source_target_pairs={{0,1},{1,2},{2,3},{3,0},{4,5},{5,6},{6,7},{7,4},{8,9},{9,10},{10,1... | collective-permute-start | bytes 884744 | tf_op jit(solution)/shard_map/ppermute | solution.py:544
  35.9 14.5 %collective-permute-start.19 = (bf16[2,144,512]{2,1,0:T(8,128)(2,1)S(1)}, bf16[2,144,512]{2,1,0:T(8,128)(2,1)}, u32[]{:S(2)}, u32[]{:S(2)}) collective-permute-start(bf16[2,144,512]{2,1,0:T(8,128)(2,1)S(1)} %pad_maximum_fusion.4.rest_9_), channel_id=1, source_target_pairs={{0,3},{1,0},{2,1},{3,2},{4,7},{5,4},{6,5},{7,6},{8,11},{9,8},{10,9... | collective-permute-start | bytes 884744 | tf_op jit(solution)/shard_map/ppermute | solution.py:544
  38.1 9.2 %collective-permute-start.4 = (bf16[144,512]{1,0:T(8,128)(2,1)S(1)}, bf16[144,512]{1,0:T(8,128)(2,1)S(1)}, u32[]{:S(2)}, u32[]{:S(2)}) collective-permute-start(bf16[144,512]{1,0:T(8,128)(2,1)S(1)} %get-tuple-element.21), channel_id=1, source_target_pairs={{0,1},{1,2},{2,3},{3,0},{4,5},{5,6},{6,7},{7,4},{8,9},{9,10},{10,1... | collective-permute-start | bytes 442376 | tf_op jit(solution)/shard_map/ppermute | solution.py:544
  47.3 7.9 %collective-permute-start.17 = (bf16[2,144,512]{2,1,0:T(8,128)(2,1)S(1)}, bf16[2,144,512]{2,1,0:T(8,128)(2,1)S(1)}, u32[]{:S(2)}, u32[]{:S(2)}) collective-permute-start(bf16[2,144,512]{2,1,0:T(8,128)(2,1)S(1)} %pad_maximum_fusion.4.rest_9_), channel_id=1, source_target_pairs={{0,1},{1,2},{2,3},{3,0},{4,5},{5,6},{6,7},{7,4},{8,9},{9,10},{10,1... | collective-permute-start | bytes 884744 | tf_op jit(solution)/shard_map/ppermute | solution.py:544
  49.6 8.7 %collective-permute-start.7 = (bf16[2,144,512]{2,1,0:T(8,128)(2,1)S(1)}, bf16[2,144,512]{2,1,0:T(8,128)(2,1)}, u32[]{:S(2)}, u32[]{:S(2)}) collective-permute-start(bf16[2,144,512]{2,1,0:T(8,128)(2,1)S(1)} %pad_maximum_fusion.1.rest_0_), channel_id=1, source_target_pairs={{0,4},{1,5},{2,6},{3,7},{4,8},{5,9},{6,10},{7,11},{8,12},{9,13},{1... | collective-permute-start | bytes 884744 | tf_op jit(solution)/shard_map/ppermute | solution.py:544
  50.4 12.1 %collective-permute-start.10 = (bf16[2,144,512]{2,1,0:T(8,128)(2,1)S(1)}, bf16[2,144,512]{2,1,0:T(8,128)(2,1)}, u32[]{:S(2)}, u32[]{:S(2)}) collective-permute-start(bf16[2,144,512]{2,1,0:T(8,128)(2,1)S(1)} %pad_maximum_fusion.2.rest_1_), channel_id=1, source_target_pairs={{0,12},{1,13},{2,14},{3,15},{4,0},{5,1},{6,2},{7,3},{8,4},{9,5},{1... | collective-permute-start | bytes 884744 | tf_op jit(solution)/shard_map/ppermute | solution.py:544
  55.9 12.8 %collective-permute-start.8 = (bf16[2,144,512]{2,1,0:T(8,128)(2,1)S(1)}, bf16[2,144,512]{2,1,0:T(8,128)(2,1)}, u32[]{:S(2)}, u32[]{:S(2)}) collective-permute-start(bf16[2,144,512]{2,1,0:T(8,128)(2,1)S(1)} %pad_maximum_fusion.2.rest_1_), channel_id=1, source_target_pairs={{0,4},{1,5},{2,6},{3,7},{4,8},{5,9},{6,10},{7,11},{8,12},{9,13},{1... | collective-permute-start | bytes 884744 | tf_op jit(solution)/shard_map/ppermute | solution.py:544
  56.8 12.0 %collective-permute-start.18 = (bf16[2,144,512]{2,1,0:T(8,128)(2,1)}, bf16[2,144,512]{2,1,0:T(8,128)(2,1)}, u32[]{:S(2)}, u32[]{:S(2)}) collective-permute-start(bf16[2,144,512]{2,1,0:T(8,128)(2,1)} %collective-permute-done.16.rest_10_), channel_id=1, source_target_pairs={{0,1},{1,2},{2,3},{3,0},{4,5},{5,6},{6,7},{7,4},{8,9},{9,10},{10,1... | collective-permute-start | bytes 884744 | tf_op jit(solution)/shard_map/ppermute | solution.py:544
  58.3 10.4 %collective-permute-start.20 = (bf16[2,144,512]{2,1,0:T(8,128)(2,1)}, bf16[2,144,512]{2,1,0:T(8,128)(2,1)}, u32[]{:S(2)}, u32[]{:S(2)}) collective-permute-start(bf16[2,144,512]{2,1,0:T(8,128)(2,1)} %collective-permute-done.19.rest_15_), channel_id=1, source_target_pairs={{0,3},{1,0},{2,1},{3,2},{4,7},{5,4},{6,5},{7,6},{8,11},{9,8},{10,9... | collective-permute-start | bytes 884744 | tf_op jit(solution)/shard_map/ppermute | solution.py:544
  62.5 7.8 %collective-permute-start.9 = (bf16[2,144,512]{2,1,0:T(8,128)(2,1)}, bf16[2,144,512]{2,1,0:T(8,128)(2,1)}, u32[]{:S(2)}, u32[]{:S(2)}) collective-permute-start(bf16[2,144,512]{2,1,0:T(8,128)(2,1)} %collective-permute-done.7.rest_2_), channel_id=1, source_target_pairs={{0,4},{1,5},{2,6},{3,7},{4,8},{5,9},{6,10},{7,11},{8,12},{9,13},{1... | collective-permute-start | bytes 884744 | tf_op jit(solution)/shard_map/ppermute | solution.py:544
  82.8 20.0 %all-to-all-start = ((f32[16,64,256]{2,1,0:T(8,128)}), f32[16,64,256]{2,1,0:T(8,128)S(1)}, u32[]{:S(2)}, u32[]{:S(2)}) async-start(f32[16,64,256]{2,1,0:T(8,128)} %get-tuple-element.24), calls=%async_computation | async-start | bytes 2097152 | tf_op jit(solution)/shard_map/all_to_all | solution.py:532
  88.0 8.4 %collective-permute-start.22 = (f32[4,64,256]{2,1,0:T(8,128)S(1)}, f32[4,64,256]{2,1,0:T(8,128)S(1)}, u32[]{:S(2)}, u32[]{:S(2)}) collective-permute-start(f32[4,64,256]{2,1,0:T(8,128)S(1)} %slice.31), channel_id=1, source_target_pairs={{0,16},{16,0},{32,48},{48,32},{64,80},{80,64},{96,112},{112,96},{1... | collective-permute-start | bytes 786440 | tf_op jit(solution)/shard_map/ppermute | solution.py:544
  103.9 22.2 %all-to-all-start.1 = ((bf16[16,128,256]{2,1,0:T(8,128)(2,1)}), bf16[16,128,256]{2,1,0:T(8,128)(2,1)S(1)}, u32[]{:S(2)}, u32[]{:S(2)}) async-start(bf16[16,128,256]{2,1,0:T(8,128)(2,1)} %get-tuple-element.26), calls=%async_computation.1 | async-start | bytes 2097152 | tf_op jit(solution)/shard_map/all_to_all | solution.py:532
  130.8 16.4 %all-to-all-start.2 = ((f32[16,64,256]{2,1,0:T(8,128)}), f32[16,64,256]{2,1,0:T(8,128)S(1)}, u32[]{:S(2)}, u32[]{:S(2)}) async-start(f32[16,64,256]{2,1,0:T(8,128)} %get-tuple-element.28), calls=%async_computation.2 | async-start | bytes 2097152 | tf_op jit(solution)/shard_map/all_to_all | solution.py:532
  150.0 19.0 %all-to-all-start.3 = ((bf16[16,64,256]{2,1,0:T(8,128)(2,1)}), bf16[16,64,256]{2,1,0:T(8,128)(2,1)S(1)}, u32[]{:S(2)}, u32[]{:S(2)}) async-start(bf16[16,64,256]{2,1,0:T(8,128)(2,1)} %get-tuple-element.30), calls=%async_computation.3 | async-start | bytes 1048576 | tf_op jit(solution)/shard_map/all_to_all | solution.py:532
  (32 other events, 140.7 us)

commit v5 on v4

--- a/solution.py
+++ b/solution.py
@@ -43,7 +43,15 @@
     return jax.ShapeDtypeStruct(dims, dtype)
 
 
-def pack_body(series_ref, start_ref, first_ref, second_ref, trail_ref):
+def pack_body(series_hbm, start_hbm, first_ref, second_ref, trail_ref, series_ref, start_ref, sems):
+    copies = [
+        pltpu.make_async_copy(series_hbm, series_ref, sems.at[0]),
+        pltpu.make_async_copy(start_hbm, start_ref, sems.at[1]),
+    ]
+    for copy in copies:
+        copy.start()
+    for copy in copies:
+        copy.wait()
     trail_ref[:DAYS] = series_ref[...]
     trail_ref[DAYS:] = start_ref[...]
     first_ref[:16, :BLOCK] = start_ref[:16]
@@ -59,10 +67,15 @@
     return call(
         pack_body,
         [half, half, shape(DAYS + RANK, BLOCK, dtype=BF16)],
-        [VMEM, VMEM],
+        [HBM, HBM],
         100_000,
         1 << 20,
-        4,
+        59,
+        scratch=[
+            pltpu.VMEM((DAYS, BLOCK), BF16),
+            pltpu.VMEM((RANK, BLOCK), BF16),
+            pltpu.SemaphoreType.DMA((2,)),
+        ],
     )(series, start)
 
 
@@ -107,11 +120,11 @@
 
 
 def count_of(table):
-    return table[1][0, 0]
+    return table[1][4]
 
 
 def row_offset(table, j):
-    place = table[2]
+    place = table[1]
     return ((j ^ place[1]) & 1) * 4 + ((place[0] - j // 2) & 3)
 
 
@@ -119,8 +132,8 @@
     return (count_of(table) + GROUP - 1) // GROUP
 
 
-def build_body(pairs, count, place, weight, sums_ref, xc_ref, *rest):
-    table = (pairs, count, place)
+def build_body(pairs, place, weight, sums_ref, xc_ref, *rest):
+    table = (pairs, place)
     first, second = rest[:8], rest[8:16]
     tiles_ref, rows_ref, cols_ref, at_ref, buffer, sems, out_sems = rest[16:]
     copies = []
@@ -144,8 +157,8 @@
 
     def indices(slot):
         i = table[0][0, slot] % N_COL
-        from_y = (table[2][2] - i // 4) & 3
-        from_z = (table[2][3] - i) & 3
+        from_y = (table[1][2] - i // 4) & 3
+        from_z = (table[1][3] - i) & 3
         return i, from_y, from_z, row_offset(table, table[0][1, slot] // N_COL)
 
     def basis_of(from_y, from_z):
@@ -214,7 +227,7 @@
             shape(N_COL, RANK, BLOCK),
             shape(N_ROW, RANK, BLOCK),
         ],
-        [SMEM] * 4 + [VMEM] * 2 + [ANY] * 16,
+        [SMEM] * 3 + [VMEM] * 2 + [ANY] * 16,
         9_000_000_000,
         20 << 20,
         30,
@@ -279,9 +292,9 @@
 
 
 def product_body(
-    pairs, count, place, tiles_ref, qr_ref, near_ref, far_ref, rows_ref, cols_ref, qc_ref, tiles, sems
+    pairs, place, tiles_ref, qr_ref, near_ref, far_ref, rows_ref, cols_ref, qc_ref, tiles, sems
 ):
-    table = (pairs, count, place)
+    table = (pairs, place)
     load_all(table, tiles_ref, tiles, sems)
     rows_ref[...] = jnp.zeros_like(rows_ref)
     cols_ref[...] = jnp.zeros_like(cols_ref)
@@ -321,7 +334,7 @@
     return call(
         product_body,
         [shape(N_COL, RANK, BLOCK), shape(N_ROW, RANK + 16, BLOCK)],
-        [SMEM] * 3 + [HBM] + [VMEM] * 3,
+        [SMEM] * 2 + [HBM] + [VMEM] * 3,
         1_000_000_000,
         8 << 20,
         30,
@@ -425,7 +438,6 @@
 
 def project_body(
     pairs,
-    count,
     place,
     tiles_ref,
     qr_ref,
@@ -438,7 +450,7 @@
     tiles,
     sems,
 ):
-    table = (pairs, count, place)
+    table = (pairs, place)
     load_all(table, tiles_ref, tiles, sems)
     cols_ref[...] = jnp.zeros_like(cols_ref)
     join(near_ref, far_ref, qc_ref)
@@ -480,7 +492,7 @@
     return call(
         project_body,
         shape(PACKED, 2 * RANK),
-        [SMEM] * 3 + [HBM] + [VMEM] * 4,
+        [SMEM] * 2 + [HBM] + [VMEM] * 4,
         500_000_000,
         6 << 20,
         30,
@@ -571,8 +583,8 @@
 
 def local(series, lag_weight, start_basis, block_pairs, pair_count):
     row, col = lax.axis_index("row"), lax.axis_index("col")
-    place = jnp.stack([row // 2, row % 2, col // 4, col % 4]).astype(jnp.int32)
-    table = (block_pairs.reshape(SLOTS, 2).T, pair_count, place)
+    place = jnp.stack([row // 2, row % 2, col // 4, col % 4, pair_count[0, 0]]).astype(jnp.int32)
+    table = (block_pairs.reshape(SLOTS, 2).T, place)
     first, second, trail = pack(series, start_basis)
     first, second = around(first, "z"), around(second, "y")
     trail = around(trail, "x")

time: 199 us -> 200 us (level)
  no operation moved by 1% of the time
where the time goes in v5:
time: 200 us; the launch traced here: 198 us
  starting transfers between devices  86.6 us (43%)
  waiting for transfers between devices  60.1 us (30%)
  Pallas kernels  31.9 us (16%)
  blocking collectives  13.7 us (7%)
  local copies, waits for them, and re-layouts  2.3 us (1%)
    ppermute x42, starting transfers between devices, shift(): return lax.ppermute(x, 'row' if axis in ('x', 'core') else 'col', pairs)  63.8 us
    ppermute x42, waiting for transfers between devices, shift(): return lax.ppermute(x, 'row' if axis in ('x', 'core') else 'col', pairs)  56.8 us
    all_to_all x4, starting transfers between devices, swap(): return lax.all_to_all(x, axis, 0, 0, tiled=True)  22.7 us
    all_to_all x1, blocking collectives, swap(): return lax.all_to_all(x, axis, 0, 0, tiled=True)  13.7 us
    pallas_call x1, Pallas kernels, build(): call(build_body, [shape(TILE_ROOM, BLOCK, BLOCK, dtype=BF16), shape(N_COL...  12.4 us
    pallas_call x1, Pallas kernels, product(): call(product_body, [shape(N_COL, RANK, BLOCK), shape(N_ROW, RANK + 16, BL...  4.7 us
  transfers between devices with their start and end apart: 46, of which 24 were waited for; matrix products, arithmetic and copies ran while one was open for 0% of the time, Pallas kernels for 1%

profile of v5, /device:TPU:1, one launch (start us, length us, event | category | flops | bytes accessed | tf_op | source)
XLA Modules:
  0.0 197.6 jit_solution(7116736529686185068)
XLA Ops:
  2.5 3.4 %collective-permute-start.2 = (bf16[576,256]{1,0:T(8,128)(2,1)}, bf16[576,256]{1,0:T(8,128)(2,1)S(1)}, u32[]{:S(2)}, u32[]{:S(2)}) collective-permute-start(bf16[576,256]{1,0:T(8,128)(2,1)} %get-tuple-element.18), channel_id=1, source_target_pairs={{0,96},{16,112},{32,0},{48,16},{64,32},{80,48},{96,64},{112,80},{1... | collective-permute-start | bytes 884744 | tf_op jit(solution)/shard_map/ppermute | solution.py:556
  7.0 6.0 %collective-permute-done.2 = bf16[576,256]{1,0:T(8,128)(2,1)S(1)} collective-permute-done((bf16[576,256]{1,0:T(8,128)(2,1)}, bf16[576,256]{1,0:T(8,128)(2,1)S(1)}, u32[]{:S(2)}, u32[]{:S(2)}) %collective-permute-start.2) | collective-permute-done | bytes 294944 | tf_op jit(solution)/shard_map/ppermute | solution.py:556
  15.3 7.6 %collective-permute-done = bf16[576,256]{1,0:T(8,128)(2,1)S(1)} collective-permute-done((bf16[576,256]{1,0:T(8,128)(2,1)}, bf16[576,256]{1,0:T(8,128)(2,1)S(1)}, u32[]{:S(2)}, u32[]{:S(2)}) %collective-permute-start) | collective-permute-done | bytes 294944 | tf_op jit(solution)/shard_map/ppermute | solution.py:556
  29.0 3.8 %collective-permute-start.6 = (bf16[144,512]{1,0:T(8,128)(2,1)S(1)}, bf16[144,512]{1,0:T(8,128)(2,1)S(1)}, u32[]{:S(2)}, u32[]{:S(2)}) collective-permute-start(bf16[144,512]{1,0:T(8,128)(2,1)S(1)} %copy-done.8), channel_id=1, source_target_pairs={{0,3},{1,0},{2,1},{3,2},{4,7},{5,4},{6,5},{7,6},{8,11},{9,8},{10,9... | collective-permute-start | bytes 442376 | tf_op jit(solution)/shard_map/ppermute | solution.py:556
  40.3 8.2 %collective-permute-done.4 = bf16[144,512]{1,0:T(8,128)(2,1)S(1)} collective-permute-done((bf16[144,512]{1,0:T(8,128)(2,1)S(1)}, bf16[144,512]{1,0:T(8,128)(2,1)S(1)}, u32[]{:S(2)}, u32[]{:S(2)}) %collective-permute-start.4) | collective-permute-done | bytes 147488 | tf_op jit(solution)/shard_map/ppermute | solution.py:556
  60.7 3.0 %collective-permute-done.10.rest_7_ = bf16[2,144,512]{2,1,0:T(8,128)(2,1)} collective-permute-done((bf16[2,144,512]{2,1,0:T(8,128)(2,1)S(1)}, bf16[2,144,512]{2,1,0:T(8,128)(2,1)}, u32[]{:S(2)}, u32[]{:S(2)}) %collective-permute-start.10) | collective-permute-done | bytes 294944 | tf_op jit(solution)/shard_map/ppermute | solution.py:556
  71.6 12.4 %shard_map.70 = (bf16[288,256,256]{2,1,0:T(8,128)(2,1)}, f32[16,64,256]{2,1,0:T(8,128)}, f32[8,64,256]{2,1,0:T(8,128)S(1)}) custom-call(s32[2,32]{1,0:T(2,128)S(1)} %bitcast.31, s32[5]{0:T(128)S(1)} %stack.100.place, f32[4]{0:T(128)S(1)} %copy-done.7, bf16[8,4,512,256]{3,2,1,0:T(8,128)(2,1)S(1)} %get-tuple-element.19.sums_ref, ...), custom_call_target="tpu_custom_call" | custom-call | flops 8999999488 | bytes 20971520 | tf_op jit(solution)/shard_map/pallas_call | solution.py:223
  84.0 5.3 %all-to-all-start = ((f32[16,64,256]{2,1,0:T(8,128)}), f32[16,64,256]{2,1,0:T(8,128)S(1)}, u32[]{:S(2)}, u32[]{:S(2)}) async-start(f32[16,64,256]{2,1,0:T(8,128)} %get-tuple-element.24), calls=%async_computation | async-start | bytes 2097152 | tf_op jit(solution)/shard_map/all_to_all | solution.py:544
  89.3 7.2 %collective-permute-start.22 = (f32[4,64,256]{2,1,0:T(8,128)S(1)}, f32[4,64,256]{2,1,0:T(8,128)S(1)}, u32[]{:S(2)}, u32[]{:S(2)}) collective-permute-start(f32[4,64,256]{2,1,0:T(8,128)S(1)} %slice.31), channel_id=1, source_target_pairs={{0,16},{16,0},{32,48},{48,32},{64,80},{80,64},{96,112},{112,96},{1... | collective-permute-start | bytes 786440 | tf_op jit(solution)/shard_map/ppermute | solution.py:556
  100.5 3.6 %collective-permute-done.25.c_ref = f32[1,64,256]{2,1,0:T(8,128)S(1)} collective-permute-done((f32[1,64,256]{2,1,0:T(8,128)S(1)}, f32[1,64,256]{2,1,0:T(8,128)S(1)}, u32[]{:S(2)}, u32[]{:S(2)}) %collective-permute-start.25) | collective-permute-done | bytes 65568 | tf_op jit(solution)/shard_map/ppermute | solution.py:556
  105.1 6.9 %all-to-all-start.1 = ((bf16[16,128,256]{2,1,0:T(8,128)(2,1)}), bf16[16,128,256]{2,1,0:T(8,128)(2,1)S(1)}, u32[]{:S(2)}, u32[]{:S(2)}) async-start(bf16[16,128,256]{2,1,0:T(8,128)(2,1)} %get-tuple-element.26), calls=%async_computation.1 | async-start | bytes 2097152 | tf_op jit(solution)/shard_map/all_to_all | solution.py:544
  116.4 3.0 %collective-permute-done.27 = bf16[128,256]{1,0:T(8,128)(2,1)S(1)} collective-permute-done((bf16[128,256]{1,0:T(8,128)(2,1)S(1)}, bf16[128,256]{1,0:T(8,128)(2,1)S(1)}, u32[]{:S(2)}, u32[]{:S(2)}) %collective-permute-start.27) | collective-permute-done | bytes 65568 | tf_op jit(solution)/shard_map/ppermute | solution.py:556
  119.8 3.0 %collective-permute-start.29 = (bf16[4,128,256]{2,1,0:T(8,128)(2,1)S(1)}, bf16[4,128,256]{2,1,0:T(8,128)(2,1)S(1)}, u32[]{:S(2)}, u32[]{:S(2)}) collective-permute-start(bf16[4,128,256]{2,1,0:T(8,128)(2,1)S(1)} %pad_maximum_fusion.5.near_ref), channel_id=1, source_target_pairs={{0,16},{16,0},{32,48},{48,32},{64,80},{80,64},{96,112},{112,96},{1... | collective-permute-start | bytes 786440 | tf_op jit(solution)/shard_map/ppermute | solution.py:556
  124.0 3.4 %all-to-all-done.1.qr_ref = bf16[16,128,256]{2,1,0:T(8,128)(2,1)S(1)} async-done(((bf16[16,128,256]{2,1,0:T(8,128)(2,1)}), bf16[16,128,256]{2,1,0:T(8,128)(2,1)S(1)}, u32[]{:S(2)}, u32[]{:S(2)}) %all-to-all-start.1) | async-done | bytes 1048608 | tf_op jit(solution)/shard_map/all_to_all | solution.py:544
  127.4 4.7 %shard_map.72 = (f32[16,64,256]{2,1,0:T(8,128)}, f32[8,80,256]{2,1,0:T(8,128)S(1)}) custom-call(s32[2,32]{1,0:T(2,128)S(1)} %bitcast.32, s32[5]{0:T(128)S(1)} %stack.100.place, bf16[288,256,256]{2,1,0:T(8,128)(2,1)} %get-tuple-element.23.tiles_ref, bf16[16,128,256]{2,1,0:T(8,128)(2,1)S(1)} %all-to-all-done.1.qr_ref, ...), custom_call_target="tpu_custom_call" | custom-call | flops 1000000000 | bytes 8388608 | tf_op jit(solution)/shard_map/pallas_call | solution.py:334
  132.1 3.7 %all-to-all-start.2 = ((f32[16,64,256]{2,1,0:T(8,128)}), f32[16,64,256]{2,1,0:T(8,128)S(1)}, u32[]{:S(2)}, u32[]{:S(2)}) async-start(f32[16,64,256]{2,1,0:T(8,128)} %get-tuple-element.28), calls=%async_computation.2 | async-start | bytes 2097152 | tf_op jit(solution)/shard_map/all_to_all | solution.py:544
  135.8 4.3 %collective-permute-start.30 = (f32[4,80,256]{2,1,0:T(8,128)S(1)}, f32[4,80,256]{2,1,0:T(8,128)S(1)}, u32[]{:S(2)}, u32[]{:S(2)}) collective-permute-start(f32[4,80,256]{2,1,0:T(8,128)S(1)} %slice.36), channel_id=1, source_target_pairs={{0,16},{16,0},{32,48},{48,32},{64,80},{80,64},{96,112},{112,96},{1... | collective-permute-start | bytes 983048 | tf_op jit(solution)/shard_map/ppermute | solution.py:556
  144.2 4.3 %collective-permute-done.33.c_ref = f32[1,80,256]{2,1,0:T(8,128)S(1)} collective-permute-done((f32[1,80,256]{2,1,0:T(8,128)S(1)}, f32[1,80,256]{2,1,0:T(8,128)S(1)}, u32[]{:S(2)}, u32[]{:S(2)}) %collective-permute-start.33) | collective-permute-done | bytes 81952 | tf_op jit(solution)/shard_map/ppermute | solution.py:556
  151.3 6.9 %all-to-all-start.3 = ((bf16[16,64,256]{2,1,0:T(8,128)(2,1)}), bf16[16,64,256]{2,1,0:T(8,128)(2,1)S(1)}, u32[]{:S(2)}, u32[]{:S(2)}) async-start(bf16[16,64,256]{2,1,0:T(8,128)(2,1)} %get-tuple-element.30), calls=%async_computation.3 | async-start | bytes 1048576 | tf_op jit(solution)/shard_map/all_to_all | solution.py:544
  162.0 3.3 %collective-permute-done.35 = bf16[64,256]{1,0:T(8,128)(2,1)S(1)} collective-permute-done((bf16[64,256]{1,0:T(8,128)(2,1)S(1)}, bf16[64,256]{1,0:T(8,128)(2,1)S(1)}, u32[]{:S(2)}, u32[]{:S(2)}) %collective-permute-start.35) | collective-permute-done | bytes 32800 | tf_op jit(solution)/shard_map/ppermute | solution.py:556
  165.4 3.9 %collective-permute-start.37 = (bf16[4,64,256]{2,1,0:T(8,128)(2,1)S(1)}, bf16[4,64,256]{2,1,0:T(8,128)(2,1)S(1)}, u32[]{:S(2)}, u32[]{:S(2)}) collective-permute-start(bf16[4,64,256]{2,1,0:T(8,128)(2,1)S(1)} %pad_maximum_fusion.6.near_ref), channel_id=1, source_target_pairs={{0,16},{16,0},{32,48},{48,32},{64,80},{80,64},{96,112},{112,96},{1... | collective-permute-start | bytes 393224 | tf_op jit(solution)/shard_map/ppermute | solution.py:556
  170.3 3.3 %shard_map.74 = f32[40,128]{1,0:T(8,128)S(1)} custom-call(s32[2,32]{1,0:T(2,128)S(1)} %bitcast.33, s32[5]{0:T(128)S(1)} %stack.100.place, bf16[288,256,256]{2,1,0:T(8,128)(2,1)} %get-tuple-element.23.tiles_ref, bf16[16,64,256]{2,1,0:T(8,128)(2,1)S(1)} %all-to-all-done.3.qr_ref, bf16[4,64,256]{2,1,0:T(8,128)(2,1)S(1)} %pad_maximum_fusion.6.near_ref, ...), custom_call_target="tpu_custom_call" | custom-call | flops 500000000 | bytes 6291456 | tf_op jit(solution)/shard_map/pallas_call | solution.py:492
  181.0 13.7 %all_to_all.25.parts_ref = f32[16,40,128]{2,1,0:T(8,128)S(1)} all-to-all(f32[16,40,128]{2,1,0:T(8,128)S(1)} %shard_map.75), channel_id=1, replica_groups=mesh['row'=8,'col'=16] {'col'}, dimensions={0} | all-to-all | bytes 655360 | tf_op jit(solution)/shard_map/all_to_all | solution.py:544
  194.7 2.9 %shard_map.76 = (f32[64,256]{1,0:T(8,128)}, f32[64,64]{1,0:T(8,128)}) custom-call(f32[16,40,128]{2,1,0:T(8,128)S(1)} %all_to_all.25.parts_ref, f32[64,256]{1,0:T(8,128)S(1)} %get-tuple-element.33.p_ref), custom_call_target="tpu_custom_call" | custom-call | flops 10000000 | bytes 1048576 | tf_op jit(solution)/shard_map/pallas_call | solution.py:538
  (113 shorter events, 68.4 us)
Async XLA Ops:
  2.5 10.5 %collective-permute-start.2 = (bf16[576,256]{1,0:T(8,128)(2,1)}, bf16[576,256]{1,0:T(8,128)(2,1)S(1)}, u32[]{:S(2)}, u32[]{:S(2)}) collective-permute-start(bf16[576,256]{1,0:T(8,128)(2,1)} %get-tuple-element.18), channel_id=1, source_target_pairs={{0,96},{16,112},{32,0},{48,16},{64,32},{80,48},{96,64},{112,80},{1... | collective-permute-start | bytes 884744 | tf_op jit(solution)/shard_map/ppermute | solution.py:556
  5.9 9.4 %collective-permute-start.1 = (bf16[576,256]{1,0:T(8,128)(2,1)}, bf16[576,256]{1,0:T(8,128)(2,1)S(1)}, u32[]{:S(2)}, u32[]{:S(2)}) collective-permute-start(bf16[576,256]{1,0:T(8,128)(2,1)} %get-tuple-element.18), channel_id=1, source_target_pairs={{0,64},{16,80},{32,96},{48,112},{64,0},{80,16},{96,32},{112,48},{1... | collective-permute-start | bytes 884744 | tf_op jit(solution)/shard_map/ppermute | solution.py:556
  6.4 16.4 %collective-permute-start = (bf16[576,256]{1,0:T(8,128)(2,1)}, bf16[576,256]{1,0:T(8,128)(2,1)S(1)}, u32[]{:S(2)}, u32[]{:S(2)}) collective-permute-start(bf16[576,256]{1,0:T(8,128)(2,1)} %get-tuple-element.18), channel_id=1, source_target_pairs={{0,32},{16,48},{32,64},{48,80},{64,96},{80,112},{96,0},{112,16},{1... | collective-permute-start | bytes 884744 | tf_op jit(solution)/shard_map/ppermute | solution.py:556
  24.0 39.8 %collective-permute-start.3 = (bf16[4,576,256]{2,1,0:T(8,128)(2,1)S(1)}, bf16[4,576,256]{2,1,0:T(8,128)(2,1)S(1)}, u32[]{:S(2)}, u32[]{:S(2)}) collective-permute-start(bf16[4,576,256]{2,1,0:T(8,128)(2,1)S(1)} %pad_maximum_fusion.own_ref), channel_id=1, source_target_pairs={{0,16},{16,0},{32,48},{48,32},{64,80},{80,64},{96,112},{112,96},{1... | collective-permute-start | bytes 3538952 | tf_op jit(solution)/shard_map/ppermute | solution.py:556
  24.6 8.1 %collective-permute-start.13 = (bf16[144,512]{1,0:T(8,128)(2,1)S(1)}, bf16[144,512]{1,0:T(8,128)(2,1)S(1)}, u32[]{:S(2)}, u32[]{:S(2)}) collective-permute-start(bf16[144,512]{1,0:T(8,128)(2,1)S(1)} %copy-done.9), channel_id=1, source_target_pairs={{0,4},{1,5},{2,6},{3,7},{4,8},{5,9},{6,10},{7,11},{8,12},{9,13},{1... | collective-permute-start | bytes 442376 | tf_op jit(solution)/shard_map/ppermute | solution.py:556
  25.9 9.0 %collective-permute-start.15 = (bf16[144,512]{1,0:T(8,128)(2,1)S(1)}, bf16[144,512]{1,0:T(8,128)(2,1)S(1)}, u32[]{:S(2)}, u32[]{:S(2)}) collective-permute-start(bf16[144,512]{1,0:T(8,128)(2,1)S(1)} %copy-done.9), channel_id=1, source_target_pairs={{0,12},{1,13},{2,14},{3,15},{4,0},{5,1},{6,2},{7,3},{8,4},{9,5},{1... | collective-permute-start | bytes 442376 | tf_op jit(solution)/shard_map/ppermute | solution.py:556
  27.3 8.2 %collective-permute-start.14 = (bf16[144,512]{1,0:T(8,128)(2,1)S(1)}, bf16[144,512]{1,0:T(8,128)(2,1)S(1)}, u32[]{:S(2)}, u32[]{:S(2)}) collective-permute-start(bf16[144,512]{1,0:T(8,128)(2,1)S(1)} %copy-done.9), channel_id=1, source_target_pairs={{0,8},{1,9},{2,10},{3,11},{4,12},{5,13},{6,14},{7,15},{8,0},{9,1},... | collective-permute-start | bytes 442376 | tf_op jit(solution)/shard_map/ppermute | solution.py:556
  29.0 8.2 %collective-permute-start.6 = (bf16[144,512]{1,0:T(8,128)(2,1)S(1)}, bf16[144,512]{1,0:T(8,128)(2,1)S(1)}, u32[]{:S(2)}, u32[]{:S(2)}) collective-permute-start(bf16[144,512]{1,0:T(8,128)(2,1)S(1)} %copy-done.8), channel_id=1, source_target_pairs={{0,3},{1,0},{2,1},{3,2},{4,7},{5,4},{6,5},{7,6},{8,11},{9,8},{10,9... | collective-permute-start | bytes 442376 | tf_op jit(solution)/shard_map/ppermute | solution.py:556
  34.9 14.6 %collective-permute-start.21 = (bf16[2,144,512]{2,1,0:T(8,128)(2,1)S(1)}, bf16[2,144,512]{2,1,0:T(8,128)(2,1)S(1)}, u32[]{:S(2)}, u32[]{:S(2)}) collective-permute-start(bf16[2,144,512]{2,1,0:T(8,128)(2,1)S(1)} %pad_maximum_fusion.3.rest_8_), channel_id=1, source_target_pairs={{0,3},{1,0},{2,1},{3,2},{4,7},{5,4},{6,5},{7,6},{8,11},{9,8},{10,9... | collective-permute-start | bytes 884744 | tf_op jit(solution)/shard_map/ppermute | solution.py:556
  35.5 15.4 %collective-permute-start.16 = (bf16[2,144,512]{2,1,0:T(8,128)(2,1)S(1)}, bf16[2,144,512]{2,1,0:T(8,128)(2,1)}, u32[]{:S(2)}, u32[]{:S(2)}) collective-permute-start(bf16[2,144,512]{2,1,0:T(8,128)(2,1)S(1)} %pad_maximum_fusion.3.rest_8_), channel_id=1, source_target_pairs={{0,1},{1,2},{2,3},{3,0},{4,5},{5,6},{6,7},{7,4},{8,9},{9,10},{10,1... | collective-permute-start | bytes 884744 | tf_op jit(solution)/shard_map/ppermute | solution.py:556
  37.2 14.5 %collective-permute-start.19 = (bf16[2,144,512]{2,1,0:T(8,128)(2,1)S(1)}, bf16[2,144,512]{2,1,0:T(8,128)(2,1)}, u32[]{:S(2)}, u32[]{:S(2)}) collective-permute-start(bf16[2,144,512]{2,1,0:T(8,128)(2,1)S(1)} %pad_maximum_fusion.4.rest_9_), channel_id=1, source_target_pairs={{0,3},{1,0},{2,1},{3,2},{4,7},{5,4},{6,5},{7,6},{8,11},{9,8},{10,9... | collective-permute-start | bytes 884744 | tf_op jit(solution)/shard_map/ppermute | solution.py:556
  39.4 9.1 %collective-permute-start.4 = (bf16[144,512]{1,0:T(8,128)(2,1)S(1)}, bf16[144,512]{1,0:T(8,128)(2,1)S(1)}, u32[]{:S(2)}, u32[]{:S(2)}) collective-permute-start(bf16[144,512]{1,0:T(8,128)(2,1)S(1)} %copy-done.8), channel_id=1, source_target_pairs={{0,1},{1,2},{2,3},{3,0},{4,5},{5,6},{6,7},{7,4},{8,9},{9,10},{10,1... | collective-permute-start | bytes 442376 | tf_op jit(solution)/shard_map/ppermute | solution.py:556
  48.5 7.9 %collective-permute-start.17 = (bf16[2,144,512]{2,1,0:T(8,128)(2,1)S(1)}, bf16[2,144,512]{2,1,0:T(8,128)(2,1)S(1)}, u32[]{:S(2)}, u32[]{:S(2)}) collective-permute-start(bf16[2,144,512]{2,1,0:T(8,128)(2,1)S(1)} %pad_maximum_fusion.4.rest_9_), channel_id=1, source_target_pairs={{0,1},{1,2},{2,3},{3,0},{4,5},{5,6},{6,7},{7,4},{8,9},{9,10},{10,1... | collective-permute-start | bytes 884744 | tf_op jit(solution)/shard_map/ppermute | solution.py:556
  50.9 8.7 %collective-permute-start.7 = (bf16[2,144,512]{2,1,0:T(8,128)(2,1)S(1)}, bf16[2,144,512]{2,1,0:T(8,128)(2,1)}, u32[]{:S(2)}, u32[]{:S(2)}) collective-permute-start(bf16[2,144,512]{2,1,0:T(8,128)(2,1)S(1)} %pad_maximum_fusion.1.rest_0_), channel_id=1, source_target_pairs={{0,4},{1,5},{2,6},{3,7},{4,8},{5,9},{6,10},{7,11},{8,12},{9,13},{1... | collective-permute-start | bytes 884744 | tf_op jit(solution)/shard_map/ppermute | solution.py:556
  51.7 12.1 %collective-permute-start.10 = (bf16[2,144,512]{2,1,0:T(8,128)(2,1)S(1)}, bf16[2,144,512]{2,1,0:T(8,128)(2,1)}, u32[]{:S(2)}, u32[]{:S(2)}) collective-permute-start(bf16[2,144,512]{2,1,0:T(8,128)(2,1)S(1)} %pad_maximum_fusion.2.rest_1_), channel_id=1, source_target_pairs={{0,12},{1,13},{2,14},{3,15},{4,0},{5,1},{6,2},{7,3},{8,4},{9,5},{1... | collective-permute-start | bytes 884744 | tf_op jit(solution)/shard_map/ppermute | solution.py:556
  57.1 12.9 %collective-permute-start.8 = (bf16[2,144,512]{2,1,0:T(8,128)(2,1)S(1)}, bf16[2,144,512]{2,1,0:T(8,128)(2,1)}, u32[]{:S(2)}, u32[]{:S(2)}) collective-permute-start(bf16[2,144,512]{2,1,0:T(8,128)(2,1)S(1)} %pad_maximum_fusion.2.rest_1_), channel_id=1, source_target_pairs={{0,4},{1,5},{2,6},{3,7},{4,8},{5,9},{6,10},{7,11},{8,12},{9,13},{1... | collective-permute-start | bytes 884744 | tf_op jit(solution)/shard_map/ppermute | solution.py:556
  58.0 12.0 %collective-permute-start.18 = (bf16[2,144,512]{2,1,0:T(8,128)(2,1)}, bf16[2,144,512]{2,1,0:T(8,128)(2,1)}, u32[]{:S(2)}, u32[]{:S(2)}) collective-permute-start(bf16[2,144,512]{2,1,0:T(8,128)(2,1)} %collective-permute-done.16.rest_10_), channel_id=1, source_target_pairs={{0,1},{1,2},{2,3},{3,0},{4,5},{5,6},{6,7},{7,4},{8,9},{9,10},{10,1... | collective-permute-start | bytes 884744 | tf_op jit(solution)/shard_map/ppermute | solution.py:556
  59.6 10.5 %collective-permute-start.20 = (bf16[2,144,512]{2,1,0:T(8,128)(2,1)}, bf16[2,144,512]{2,1,0:T(8,128)(2,1)}, u32[]{:S(2)}, u32[]{:S(2)}) collective-permute-start(bf16[2,144,512]{2,1,0:T(8,128)(2,1)} %collective-permute-done.19.rest_15_), channel_id=1, source_target_pairs={{0,3},{1,0},{2,1},{3,2},{4,7},{5,4},{6,5},{7,6},{8,11},{9,8},{10,9... | collective-permute-start | bytes 884744 | tf_op jit(solution)/shard_map/ppermute | solution.py:556
  63.8 7.8 %collective-permute-start.9 = (bf16[2,144,512]{2,1,0:T(8,128)(2,1)}, bf16[2,144,512]{2,1,0:T(8,128)(2,1)}, u32[]{:S(2)}, u32[]{:S(2)}) collective-permute-start(bf16[2,144,512]{2,1,0:T(8,128)(2,1)} %collective-permute-done.7.rest_2_), channel_id=1, source_target_pairs={{0,4},{1,5},{2,6},{3,7},{4,8},{5,9},{6,10},{7,11},{8,12},{9,13},{1... | collective-permute-start | bytes 884744 | tf_op jit(solution)/shard_map/ppermute | solution.py:556
  84.0 20.0 %all-to-all-start = ((f32[16,64,256]{2,1,0:T(8,128)}), f32[16,64,256]{2,1,0:T(8,128)S(1)}, u32[]{:S(2)}, u32[]{:S(2)}) async-start(f32[16,64,256]{2,1,0:T(8,128)} %get-tuple-element.24), calls=%async_computation | async-start | bytes 2097152 | tf_op jit(solution)/shard_map/all_to_all | solution.py:544
  89.3 8.3 %collective-permute-start.22 = (f32[4,64,256]{2,1,0:T(8,128)S(1)}, f32[4,64,256]{2,1,0:T(8,128)S(1)}, u32[]{:S(2)}, u32[]{:S(2)}) collective-permute-start(f32[4,64,256]{2,1,0:T(8,128)S(1)} %slice.31), channel_id=1, source_target_pairs={{0,16},{16,0},{32,48},{48,32},{64,80},{80,64},{96,112},{112,96},{1... | collective-permute-start | bytes 786440 | tf_op jit(solution)/shard_map/ppermute | solution.py:556
  105.1 22.2 %all-to-all-start.1 = ((bf16[16,128,256]{2,1,0:T(8,128)(2,1)}), bf16[16,128,256]{2,1,0:T(8,128)(2,1)S(1)}, u32[]{:S(2)}, u32[]{:S(2)}) async-start(bf16[16,128,256]{2,1,0:T(8,128)(2,1)} %get-tuple-element.26), calls=%async_computation.1 | async-start | bytes 2097152 | tf_op jit(solution)/shard_map/all_to_all | solution.py:544
  132.1 16.4 %all-to-all-start.2 = ((f32[16,64,256]{2,1,0:T(8,128)}), f32[16,64,256]{2,1,0:T(8,128)S(1)}, u32[]{:S(2)}, u32[]{:S(2)}) async-start(f32[16,64,256]{2,1,0:T(8,128)} %get-tuple-element.28), calls=%async_computation.2 | async-start | bytes 2097152 | tf_op jit(solution)/shard_map/all_to_all | solution.py:544
  151.3 19.0 %all-to-all-start.3 = ((bf16[16,64,256]{2,1,0:T(8,128)(2,1)}), bf16[16,64,256]{2,1,0:T(8,128)(2,1)S(1)}, u32[]{:S(2)}, u32[]{:S(2)}) async-start(bf16[16,64,256]{2,1,0:T(8,128)(2,1)} %get-tuple-element.30), calls=%async_computation.3 | async-start | bytes 1048576 | tf_op jit(solution)/shard_map/all_to_all | solution.py:544
  (32 other events, 146.8 us)
